TPU v7x, 32 devices: a whole 2x2x4 slice. The times are simulated.
32 devices in a mesh: win: 2 (over x), sta: 16 (over z, y, core).
Axes of the slice: x: 2, y: 2, z: 4, core: 2. Of those that a mesh axis runs over, the one named last changes fastest.
Arguments:
- records: bfloat16 [1024, 16384], P('win', 'sta'), parts along dimension 0, may hold values from -600 to 600
- filter_taps: bfloat16 [129], replicated, may hold values from -0.5 to 0.5
- ref_owner: int32 [4], P('win'), parts along dimension 0, may hold values from 0 to 15
- reference_station_order: int32 [4, 32], P('win'), parts along dimension 0, may hold values from 0 to 31, each once within a row
- pair_valid: int32 [4, 32, 512], P('win', None, 'sta'), parts along dimension 0, may hold values 0 or 1
Outputs:
- correlations: float32 [4, 32, 512, 256], P('win', None, 'sta'), parts along dimension 0
There are 2 independent parts, one for each index of `win`. A program takes and returns all parts, laid end to end along the dimension named above; an argument that names none is the same for every part. Nothing has to cross between parts.
Inputs may be any that keep to these rules, and one draw needn't show every extreme that they name: Each row of reference_station_order is a permutation of 0 .. 31.
All inputs are finite; a program needn't handle non-finite values. No bound on the sum of `pair_valid` on one device may be relied on, other than what follows from the above.
Results may differ from a plain program's by a relative error of at most 0.0073.
Values may be sent and summed in bfloat16 or wider, within the bound.
No kernel may reach another device: no remote copies, remote signals or barrier semaphores. Data moves between devices by JAX's collectives and lax.ppermute only.
A program may use at most 128 MiB of HBM per device.

v0:
```python
import functools
import math

import jax
import jax.numpy as jnp
import numpy as np
from jax import lax
from jax.experimental import pallas as pl
from jax.experimental.pallas import tpu as pltpu
from jax.sharding import PartitionSpec as P


NFFT = 1024
LAGS = 256
LANES = 128
SUB = 8


def forward_matrix(length):
    time_index = np.arange(length)[:, None]
    bin_index = np.arange(length // 2)[None, :]
    angles = (time_index * bin_index % length).astype(np.float32) * np.float32(2.0 * math.pi / length)
    return np.concatenate([np.cos(angles), -np.sin(angles)], axis=1).astype(jnp.bfloat16)


def inverse_transform_matrix(length, lag_count, segments):
    bin_index = np.arange(length // 2)[:, None]
    shifts = np.arange(lag_count)[None, :] - lag_count // 2
    angles = (bin_index * shifts % length).astype(np.float32) * np.float32(2.0 * math.pi / length)
    factor = np.float32(1.0 / math.sqrt(segments * (length // 2)))
    return np.concatenate([factor * np.cos(angles), -factor * np.sin(angles)], axis=0).astype(jnp.bfloat16)


def pick_body(owner_ref, records_ref, wanted_ref, *rest):
    halves, sems = rest[:-1], rest[-1]
    copies = [
        pltpu.make_async_copy(records_ref.at[owner_ref[k]], wanted_ref.at[k], sems.at[k])
        for k in range(wanted_ref.shape[0])
    ]
    for p, half in enumerate(halves):
        copies.append(pltpu.make_async_copy(records_ref.at[:, p], half, sems.at[len(copies)]))
    for copy in copies:
        copy.start()
    for copy in copies:
        copy.wait()


def pick(owner, records):
    devices, parts, some, width = records.shape
    steps = owner.shape[0]
    vmem = pl.BlockSpec(memory_space=pltpu.VMEM)
    return pl.pallas_call(
        pick_body,
        out_shape=[jax.ShapeDtypeStruct((steps, parts, some, width), records.dtype)]
        + [jax.ShapeDtypeStruct((devices, some, width), records.dtype)] * parts,
        in_specs=[pl.BlockSpec(memory_space=pltpu.SMEM), pl.BlockSpec(memory_space=pltpu.HBM)],
        out_specs=[vmem] * (1 + parts),
        scratch_shapes=[pltpu.SemaphoreType.DMA((steps + parts,))],
        compiler_params=pltpu.CompilerParams(vmem_limit_bytes=8 * 2**20),
    )(owner, records)


def band_body(row_ref, out_ref):
    width, height = 2 * LANES, 4 * LANES
    rows = jnp.broadcast_to(row_ref[...], (width, height))
    out_ref[...] = pltpu.roll(rows, 0, 1, stride=1, stride_axis=0).T.astype(out_ref.dtype)


def band_matrix(filter_taps):
    count = filter_taps.shape[0]
    before = LANES - (count - 1) // 2
    row = jnp.pad(filter_taps.astype(jnp.float32), (before, 4 * LANES - before - count))[None]
    return pl.pallas_call(
        band_body,
        out_shape=jax.ShapeDtypeStruct((4 * LANES, 2 * LANES), filter_taps.dtype),
        in_specs=[pl.BlockSpec(memory_space=pltpu.VMEM)],
        out_specs=pl.BlockSpec(memory_space=pltpu.VMEM),
        compiler_params=pltpu.CompilerParams(vmem_limit_bytes=4 * 2**20),
    )(row)


def whiten_body(index_ref, *rest, pieces, rows):
    band_ref, forward_ref, out_ref, padded, filtered = rest[-5:]
    raw_refs = rest[:-5] if len(rest) > 6 else [rest[0].at[piece] for piece in range(pieces)]
    stations = padded.shape[1]
    width = raw_refs[0].shape[-1]
    tiles = NFFT // LANES
    parts = width // LANES
    segments = out_ref.shape[0]
    bins = NFFT // 2
    edge = jnp.zeros((stations, LANES), padded.dtype)
    padded[0] = edge
    padded[segments * tiles + 1] = edge
    for piece in range(pieces):
        place = 1 + (index_ref[0] ^ piece) * parts
        held = raw_refs[piece]
        lead = len(held.shape) > 2
        for part in range(parts):
            lanes = slice(part * LANES, (part + 1) * LANES)
            if lead:
                padded[place + part] = held[..., lanes].reshape(stations, LANES)
            else:
                padded[place + part] = held[:, lanes]
    for first in range(0, segments, rows // stations):
        some = range(first, first + rows // stations)
        for tile in range(0, tiles, 2):
            window = jnp.concatenate(
                [jnp.concatenate([padded[g * tiles + tile + i] for g in some], axis=0) for i in range(4)], axis=1
            )
            filtered[:, tile * LANES : (tile + 2) * LANES] = jnp.dot(
                window, band_ref[...], preferred_element_type=jnp.float32
            ).astype(jnp.bfloat16)
        spectra = jnp.dot(filtered[...], forward_ref[...], preferred_element_type=jnp.float32)
        real_part, imag_part = spectra[:, :bins], spectra[:, bins:]
        energy = real_part * real_part + imag_part * imag_part
        water_level = jnp.sum(energy, axis=-1, keepdims=True) * (1.0 / bins)
        factor = lax.rsqrt(energy + water_level + 1e-06)
        some = slice(first, first + rows // stations)
        out_ref[some, :, :bins] = (real_part * factor).astype(jnp.bfloat16).reshape(-1, stations, bins)
        out_ref[some, :, bins:] = (imag_part * factor).astype(jnp.bfloat16).reshape(-1, stations, bins)


def whiten(raw, index, band, forward, rows=128):
    pieces = len(raw)
    width = raw[0].shape[-1]
    stations = math.prod(raw[0].shape[:-1])
    segments = pieces * width // NFFT
    operands = raw if isinstance(raw, list) else [raw]
    return pl.pallas_call(
        functools.partial(whiten_body, pieces=pieces, rows=rows),
        out_shape=jax.ShapeDtypeStruct((segments, stations, NFFT), jnp.bfloat16),
        in_specs=[pl.BlockSpec(memory_space=pltpu.SMEM)] + [pl.BlockSpec(memory_space=pltpu.VMEM)] * (len(operands) + 2),
        out_specs=pl.BlockSpec(memory_space=pltpu.VMEM),
        scratch_shapes=[
            pltpu.VMEM((segments * NFFT // LANES + 2, stations, LANES), jnp.bfloat16),
            pltpu.VMEM((rows, NFFT), jnp.bfloat16),
        ],
        compiler_params=pltpu.CompilerParams(vmem_limit_bytes=10 * 2**20),
        cost_estimate=pl.CostEstimate(
            flops=2 * segments * stations * NFFT * (NFFT + 512),
            bytes_accessed=2 * segments * stations * NFFT * 2,
            transcendentals=0,
        ),
    )(index, *operands, band, forward)


def correlate_body(order_ref, valid_ref, own_ref, chosen_ref, inverse_ref, *rest, part, group, pair):
    out_ref, own_parts, chosen_parts, cross, ready, sems = rest[-6:]
    segments, stations, width = own_ref.shape
    steps, block = order_ref.shape
    count = steps * block
    bins = width // 2
    tiles = bins // LANES

    def prepare(g, _):
        where = pl.ds(pl.multiple_of(g * count, count), count)
        for tile in range(tiles):
            real = slice(tile * LANES, (tile + 1) * LANES)
            imag = slice(bins + tile * LANES, bins + (tile + 1) * LANES)
            c, d = own_ref[g, :, real].astype(jnp.float32), own_ref[g, :, imag].astype(jnp.float32)
            own_parts[0, tile, g], own_parts[1, tile, g], own_parts[2, tile, g] = c, c + d, c - d
            a, b = chosen_ref[g, :, real].astype(jnp.float32), chosen_ref[g, :, imag].astype(jnp.float32)
            chosen_parts[0, tile, where], chosen_parts[1, tile, where], chosen_parts[2, tile, where] = a + b, a, b
        return 0

    lax.fori_loop(0, segments, prepare, 0, unroll=2)
    square = (stations, stations)
    diagonal = lax.broadcasted_iota(jnp.int32, square, 0) == lax.broadcasted_iota(jnp.int32, square, 1)

    def place(q):
        step = lax.div(q, block // group)
        start = pl.multiple_of(lax.rem(q, block // group) * group, group)
        return step, start

    def send(q):
        step, start = place(q)
        slot = lax.rem(q, 2)
        where = out_ref.at[step, pl.ds(start, group), pl.ds(part * stations, stations), :]
        return pltpu.make_async_copy(ready.at[slot], where, sems.at[slot])

    def some_rows(q, _):
        step, start = place(q)

        def products(turn, _):
            tile = lax.rem(turn, tiles)
            first = lax.div(turn, tiles) * pair
            picks = [step * block + order_ref[step, start + first + j] for j in range(pair)]
            sums = None
            for g in range(segments):
                own = [own_parts[n, tile, g].reshape(stations // SUB, SUB, LANES) for n in range(3)]
                terms = [
                    chosen_parts[n, tile, pl.ds(g * count + pick, SUB, stride=0), :][None] * own[n]
                    for pick in picks
                    for n in range(3)
                ]
                sums = terms if sums is None else [x + y for x, y in zip(sums, terms)]
            for j in range(pair):
                whole, real, imag = [s.reshape(stations, LANES) for s in sums[3 * j : 3 * j + 3]]
                where = pl.ds(pl.multiple_of((first + j) * stations, stations), stations)
                lanes = pl.multiple_of(tile * LANES, LANES)
                cross[where, pl.ds(lanes, LANES)] = (whole - imag).astype(jnp.bfloat16)
                cross[where, pl.ds(bins + lanes, LANES)] = (whole - real).astype(jnp.bfloat16)
            return 0

        lax.fori_loop(0, group // pair * tiles, products, 0)
        lagged = jnp.dot(cross[...], inverse_ref[...], preferred_element_type=jnp.float32)
        valid = valid_ref[step, pl.ds(start, group), :].astype(jnp.float32)

        @pl.when(q >= 2)
        def _():
            send(q - 2).wait()

        slot = lax.rem(q, 2)
        for j in range(group):
            row = valid[j : j + 1, part * stations : (part + 1) * stations]
            kept = jnp.sum(jnp.where(diagonal, jnp.broadcast_to(row, square), 0.0), axis=1, keepdims=True)
            ready[slot, j] = lagged[j * stations : (j + 1) * stations] * kept
        send(q).start()
        return 0

    turns = count // group
    lax.fori_loop(0, turns, some_rows, 0)
    for q in range(max(turns - 2, 0), turns):
        send(q).wait()


def correlate(part, parts, order, valid, own, chosen, inverse, earlier=None):
    segments, stations, width = own.shape
    steps, block = order.shape
    count = steps * block
    lags = inverse.shape[1]
    group = min(block, 2 * SUB)
    vmem, anywhere = pl.BlockSpec(memory_space=pltpu.VMEM), pl.BlockSpec(memory_space=pl.ANY)
    extra, aliases = ([], {}) if earlier is None else ([earlier], {5: 0})
    return pl.pallas_call(
        functools.partial(correlate_body, part=part, group=group, pair=64 // stations),
        out_shape=jax.ShapeDtypeStruct((steps, block, parts * stations, lags), jnp.float32),
        in_specs=[pl.BlockSpec(memory_space=pltpu.SMEM)] + [vmem] * 4 + [anywhere] * len(extra),
        out_specs=anywhere,
        scratch_shapes=[
            pltpu.VMEM((3, width // 2 // LANES, segments, stations, LANES), jnp.float32),
            pltpu.VMEM((3, width // 2 // LANES, segments * count, LANES), jnp.float32),
            pltpu.VMEM((group * stations, width), jnp.bfloat16),
            pltpu.VMEM((2, group, stations, lags), jnp.float32),
            pltpu.SemaphoreType.DMA((2,)),
        ],
        input_output_aliases=aliases,
        compiler_params=pltpu.CompilerParams(vmem_limit_bytes=16 * 2**20),
        cost_estimate=pl.CostEstimate(
            flops=10**10,
            bytes_accessed=own.size * 2 + chosen.size * 2 + count * stations * lags * 4,
            transcendentals=0,
        ),
    )(order, valid, own, chosen, inverse, *extra)


def swap(block, axis, distance):
    count = lax.axis_size(axis)
    return lax.ppermute(block, axis, [(i, i ^ distance) for i in range(count)])


def local(records, filter_taps, ref_owner, reference_station_order, pair_valid):
    axis = "sta"
    devices = lax.axis_size(axis)
    index = lax.axis_index(axis).astype(jnp.int32)
    stations = records.shape[0] // devices
    width = records.shape[1]

    parts = 2
    wanted, *halves = pick(ref_owner, records.reshape(devices, parts, stations // parts, width))
    pieces = {0: wanted}
    distance = devices
    while distance > 1:
        radix = 4 if distance >= 16 else 2
        distance //= radix
        held = list(pieces.items())
        for j in range(1, radix):
            pieces |= {o | j * distance: swap(p, axis, j * distance) for o, p in held}
    pieces = [pieces[o] for o in range(devices)]

    resident = []
    for p in range(parts):
        resident.append(lax.all_to_all(halves[p], axis, split_axis=0, concat_axis=0))

    band = band_matrix(filter_taps)
    forward = jnp.asarray(forward_matrix(NFFT))
    inverse = jnp.asarray(inverse_transform_matrix(NFFT, LAGS, devices * width // NFFT))
    chosen = whiten(pieces, index[None], band, forward)
    zero = jnp.zeros((1,), jnp.int32)
    result = None
    for p in range(parts):
        own = whiten(resident[p], zero, band, forward)
        result = correlate(p, parts, reference_station_order, pair_valid, own, chosen, inverse, result)
    return result


def solution(mesh):
    placed = (P("win", "sta"), P(), P("win"), P("win", None), P("win", None, "sta"))
    return jax.shard_map(local, mesh=mesh, in_specs=placed, out_specs=P("win", None, "sta", None), check_vma=False)
```

profile of v0, /device:TPU:0, one launch (start us, length us, event | category | flops | bytes accessed | tf_op | source)
XLA Modules:
  0.0 104.7 jit_solution(17639925899455926728)
XLA Ops:
  0.0 1.4 %copy-done.1 = bf16[512,1024]{1,0:T(8,128)(2,1)S(1)} copy-done((bf16[512,1024]{1,0:T(8,128)(2,1)S(1)}, bf16[512,1024]{1,0:T(8,128)(2,1)}, u32[]{:S(2)}) %copy-start.1) | copy-done | bytes 1048600
  1.4 0.7 copy-done.3
  2.0 1.6 %shard_map.73 = (bf16[2,2,16,1024]{3,2,1,0:T(8,128)(2,1)S(1)}, bf16[16,16,1024]{2,1,0:T(8,128)(2,1)}, bf16[16,16,1024]{2,1,0:T(8,128)(2,1)S(1)}) custom-call(s32[2]{0:T(128)S(1)} %copy-done.3, bf16[16,2,16,1024]{3,2,1,0:T(8,128)(2,1)S(1)} %bitcast.3), custom_call_target="tpu_custom_call" | custom-call | tf_op jit(solution)/shard_map/pallas_call | solution.py:52
  3.7 0.8 copy-done.2
  4.5 7.4 %all-to-all-start.1 = ((bf16[16,16,1024]{2,1,0:T(8,128)(2,1)}), bf16[16,16,1024]{2,1,0:T(8,128)(2,1)S(1)}, u32[]{:S(2)}, u32[]{:S(2)}) async-start(bf16[16,16,1024]{2,1,0:T(8,128)(2,1)} %get-tuple-element.10), calls=%async_computation.1 | async-start | bytes 1048576 | tf_op jit(solution)/shard_map/all_to_all | solution.py:283
  11.9 3.7 %collective-permute-start.11 = (bf16[2,2,16,1024]{3,2,1,0:T(8,128)(2,1)S(1)}, bf16[2,2,16,1024]{3,2,1,0:T(8,128)(2,1)S(1)}, u32[]{:S(2)}, u32[]{:S(2)}) collective-permute-start(bf16[2,2,16,1024]{3,2,1,0:T(8,128)(2,1)S(1)} %get-tuple-element.9.rest_0_), channel_id=1, source_target_pairs={{0,12},{1,13},{2,14},{3,15},{4,8},{5,9},{6,10},{7,11},{8,4},{9,5},... | collective-permute-start | bytes 393224 | tf_op jit(solution)/shard_map/ppermute | solution.py:259
  15.6 0.7 collective-permute-start.3
  16.3 1.9 %collective-permute-start.1 = (bf16[2,2,16,1024]{3,2,1,0:T(8,128)(2,1)S(1)}, bf16[2,2,16,1024]{3,2,1,0:T(8,128)(2,1)S(1)}, u32[]{:S(2)}, u32[]{:S(2)}) collective-permute-start(bf16[2,2,16,1024]{3,2,1,0:T(8,128)(2,1)S(1)} %get-tuple-element.9.rest_0_), channel_id=1, source_target_pairs={{0,2},{1,3},{2,0},{3,1},{4,6},{5,7},{6,4},{7,5},{8,10},{9,11},{10,... | collective-permute-start | bytes 393224 | tf_op jit(solution)/shard_map/ppermute | solution.py:259
  18.2 10.4 %collective-permute-done.11.rest_12_ = bf16[2,2,16,1024]{3,2,1,0:T(8,128)(2,1)S(1)} collective-permute-done((bf16[2,2,16,1024]{3,2,1,0:T(8,128)(2,1)S(1)}, bf16[2,2,16,1024]{3,2,1,0:T(8,128)(2,1)S(1)}, u32[]{:S(2)}, u32[]{:S(2)}) %collective-permute-start.11) | collective-permute-done | bytes 131104 | tf_op jit(solution)/shard_map/ppermute | solution.py:259
  28.6 1.5 %collective-permute-start.13 = (bf16[2,2,16,1024]{3,2,1,0:T(8,128)(2,1)S(1)}, bf16[2,2,16,1024]{3,2,1,0:T(8,128)(2,1)}, u32[]{:S(2)}, u32[]{:S(2)}) collective-permute-start(bf16[2,2,16,1024]{3,2,1,0:T(8,128)(2,1)S(1)} %collective-permute-done.11.rest_12_), channel_id=1, source_target_pairs={{0,2},{1,3},{2,0},{3,1},{4,6},{5,7},{6,4},{7,5},{8,10},{9,11},{10,... | collective-permute-start | bytes 393224 | tf_op jit(solution)/shard_map/ppermute | solution.py:259
  30.1 8.3 %collective-permute-done.7.rest_8_ = bf16[2,2,16,1024]{3,2,1,0:T(8,128)(2,1)S(1)} collective-permute-done((bf16[2,2,16,1024]{3,2,1,0:T(8,128)(2,1)S(1)}, bf16[2,2,16,1024]{3,2,1,0:T(8,128)(2,1)S(1)}, u32[]{:S(2)}, u32[]{:S(2)}) %collective-permute-start.7) | collective-permute-done | bytes 131104 | tf_op jit(solution)/shard_map/ppermute | solution.py:259
  38.4 1.5 %collective-permute-start.9 = (bf16[2,2,16,1024]{3,2,1,0:T(8,128)(2,1)S(1)}, bf16[2,2,16,1024]{3,2,1,0:T(8,128)(2,1)}, u32[]{:S(2)}, u32[]{:S(2)}) collective-permute-start(bf16[2,2,16,1024]{3,2,1,0:T(8,128)(2,1)S(1)} %collective-permute-done.7.rest_8_), channel_id=1, source_target_pairs={{0,2},{1,3},{2,0},{3,1},{4,6},{5,7},{6,4},{7,5},{8,10},{9,11},{10,... | collective-permute-start | bytes 393224 | tf_op jit(solution)/shard_map/ppermute | solution.py:259
  40.1 0.6 copy-done.4
  40.7 0.6 collective-permute-start.5
  41.3 0.6 copy-done.6
  41.9 0.5 collective-permute-start.2
  42.4 2.4 %collective-permute-done.9.rest_10_ = bf16[2,2,16,1024]{3,2,1,0:T(8,128)(2,1)} collective-permute-done((bf16[2,2,16,1024]{3,2,1,0:T(8,128)(2,1)S(1)}, bf16[2,2,16,1024]{3,2,1,0:T(8,128)(2,1)}, u32[]{:S(2)}, u32[]{:S(2)}) %collective-permute-start.9) | collective-permute-done | bytes 131104 | tf_op jit(solution)/shard_map/ppermute | solution.py:259
  44.8 0.7 copy-done.8
  45.5 0.5 collective-permute-start.10
  46.0 1.2 %collective-permute-done.5.rest_6_ = bf16[2,2,16,1024]{3,2,1,0:T(8,128)(2,1)} collective-permute-done((bf16[2,2,16,1024]{3,2,1,0:T(8,128)(2,1)S(1)}, bf16[2,2,16,1024]{3,2,1,0:T(8,128)(2,1)}, u32[]{:S(2)}, u32[]{:S(2)}) %collective-permute-start.5) | collective-permute-done | bytes 131104 | tf_op jit(solution)/shard_map/ppermute | solution.py:259
  47.5 1.4 %collective-permute-done.6.rest_7_ = bf16[2,2,16,1024]{3,2,1,0:T(8,128)(2,1)} collective-permute-done((bf16[2,2,16,1024]{3,2,1,0:T(8,128)(2,1)}, bf16[2,2,16,1024]{3,2,1,0:T(8,128)(2,1)}, u32[]{:S(2)}, u32[]{:S(2)}) %collective-permute-start.6) | collective-permute-done | bytes 131104 | tf_op jit(solution)/shard_map/ppermute | solution.py:259
  48.9 0.9 copy-done.5
  49.8 0.9 copy-done.7
  50.7 0.9 copy-done.9
  51.6 5.5 %shard_map.76.chosen_ref = bf16[16,64,1024]{2,1,0:T(8,128)(2,1)S(1)} custom-call(s32[1]{0:T(128)} %bitcast.2.index_ref, bf16[2,2,16,1024]{3,2,1,0:T(8,128)(2,1)S(1)} %get-tuple-element.9.rest_0_, bf16[2,2,16,1024]{3,2,1,0:T(8,128)(2,1)S(1)} %copy-done.5, bf16[2,2,16,1024]{3,2,1,0:T(8,128)(2,1)S(1)} %collective-permute-done.1.rest_2_, ...), custom_call_target="tpu_custom_call" | custom-call | flops 3221225472 | bytes 4194304 | tf_op jit(solution)/shard_map/pallas_call | solution.py:129
  57.1 1.3 %copy-done.14 = bf16[16,64,1024]{2,1,0:T(8,128)(2,1)} copy-done((bf16[16,64,1024]{2,1,0:T(8,128)(2,1)}, bf16[16,64,1024]{2,1,0:T(8,128)(2,1)S(1)}, u32[]{:S(2)}) %copy-start.14) | copy-done | bytes 2097176
  58.5 3.9 %all-to-all-start = ((bf16[16,16,1024]{2,1,0:T(8,128)(2,1)}), bf16[16,16,1024]{2,1,0:T(8,128)(2,1)S(1)}, u32[]{:S(2)}, u32[]{:S(2)}) async-start(bf16[16,16,1024]{2,1,0:T(8,128)(2,1)} %copy-done.2), calls=%async_computation | async-start | bytes 1048576 | tf_op jit(solution)/shard_map/all_to_all | solution.py:283
  62.4 1.2 %shard_map.77.own_ref = bf16[16,16,1024]{2,1,0:T(8,128)(2,1)S(1)} custom-call(s32[1]{0:T(128)} %constant.5.clone.1.index_ref, bf16[16,16,1024]{2,1,0:T(8,128)(2,1)S(1)} %all-to-all-done.1.rest_0_, bf16[512,256]{1,0:T(8,128)(2,1)S(1)} %shard_map.74.rest_1_.rest_16_, bf16[1024,1024]{1,0:T(8,128)(2,1)S(1)} %copy-done), custom_call_target="tpu_custom_call" | custom-call | flops 805306368 | bytes 1048576 | tf_op jit(solution)/shard_map/pallas_call | solution.py:129
  64.2 18.1 %shard_map.78.rest_0_ = f32[2,32,32,256]{3,2,1,0:T(8,128)} custom-call(s32[2,32]{1,0:T(2,128)S(1)} %copy-done.11, s32[2,32,32]{2,1,0:T(8,128)S(1)} %copy-done.10, bf16[16,16,1024]{2,1,0:T(8,128)(2,1)S(1)} %shard_map.77.own_ref, bf16[16,64,1024]{2,1,0:T(8,128)(2,1)S(1)} %copy-done.15, bf16[1024,256]{1,0:T(8,128)(2,1)S(1)} %copy-done.12), custom_call_target="tpu_custom_call" | custom-call | flops 10000000000 | bytes 3670016 | tf_op jit(solution)/shard_map/pallas_call | solution.py:235
  82.3 1.2 %shard_map.75.own_ref = bf16[16,16,1024]{2,1,0:T(8,128)(2,1)S(1)} custom-call(s32[1]{0:T(128)} %constant.5.clone.1.index_ref, bf16[16,16,1024]{2,1,0:T(8,128)(2,1)S(1)} %all-to-all-done.rest_0_, bf16[512,256]{1,0:T(8,128)(2,1)S(1)} %shard_map.74.rest_1_.rest_16_, bf16[1024,1024]{1,0:T(8,128)(2,1)S(1)} %copy-done), custom_call_target="tpu_custom_call" | custom-call | flops 805306368 | bytes 1048576 | tf_op jit(solution)/shard_map/pallas_call | solution.py:129
  83.6 0.5 copy-done.16
  84.1 20.6 %shard_map.79 = f32[2,32,32,256]{3,2,1,0:T(8,128)} custom-call(s32[2,32]{1,0:T(2,128)S(1)} %copy-done.11, s32[2,32,32]{2,1,0:T(8,128)S(1)} %copy-done.10, bf16[16,16,1024]{2,1,0:T(8,128)(2,1)S(1)} %shard_map.75.own_ref, bf16[16,64,1024]{2,1,0:T(8,128)(2,1)S(1)} %copy-done.16, bf16[1024,256]{1,0:T(8,128)(2,1)S(1)} %copy-done.13, ...), custom_call_target="tpu_custom_call", output_to_operand_aliasing={{}: (5, {})} | custom-call | flops 10000000000 | bytes 3670016 | tf_op jit(solution)/shard_map/pallas_call | solution.py:235
  (46 shorter events, 1.0 us)
Async XLA Ops:
  0.0 48.9 %copy-start = (bf16[1024,1024]{1,0:T(8,128)(2,1)S(1)}, bf16[1024,1024]{1,0:T(8,128)(2,1)}, u32[]{:S(2)}) copy-start(bf16[1024,1024]{1,0:T(8,128)(2,1)} %constant.14.clone.rest_2_.rest_17_) | copy-start | bytes 6291460
  0.0 1.4 %copy-start.1 = (bf16[512,1024]{1,0:T(8,128)(2,1)S(1)}, bf16[512,1024]{1,0:T(8,128)(2,1)}, u32[]{:S(2)}) copy-start(bf16[512,1024]{1,0:T(8,128)(2,1)} %param.7) | copy-start | bytes 3145732
  1.4 0.7 copy-start.3
  2.0 45.2 %copy-start.17 = (bf16[129]{0:T(256)(128)(2,1)S(1)}, bf16[129]{0:T(256)(128)(2,1)}, u32[]{:S(2)}) copy-start(bf16[129]{0:T(256)(128)(2,1)} %param.8) | copy-start | bytes 778
  3.7 0.8 copy-start.2
  4.5 54.0 %all-to-all-start.1 = ((bf16[16,16,1024]{2,1,0:T(8,128)(2,1)}), bf16[16,16,1024]{2,1,0:T(8,128)(2,1)S(1)}, u32[]{:S(2)}, u32[]{:S(2)}) async-start(bf16[16,16,1024]{2,1,0:T(8,128)(2,1)} %get-tuple-element.10), calls=%async_computation.1 | async-start | bytes 1048576 | tf_op jit(solution)/shard_map/all_to_all | solution.py:283
  11.9 16.8 %collective-permute-start.11 = (bf16[2,2,16,1024]{3,2,1,0:T(8,128)(2,1)S(1)}, bf16[2,2,16,1024]{3,2,1,0:T(8,128)(2,1)S(1)}, u32[]{:S(2)}, u32[]{:S(2)}) collective-permute-start(bf16[2,2,16,1024]{3,2,1,0:T(8,128)(2,1)S(1)} %get-tuple-element.9.rest_0_), channel_id=1, source_target_pairs={{0,12},{1,13},{2,14},{3,15},{4,8},{5,9},{6,10},{7,11},{8,4},{9,5},... | collective-permute-start | bytes 393224 | tf_op jit(solution)/shard_map/ppermute | solution.py:259
  15.6 22.7 %collective-permute-start.7 = (bf16[2,2,16,1024]{3,2,1,0:T(8,128)(2,1)S(1)}, bf16[2,2,16,1024]{3,2,1,0:T(8,128)(2,1)S(1)}, u32[]{:S(2)}, u32[]{:S(2)}) collective-permute-start(bf16[2,2,16,1024]{3,2,1,0:T(8,128)(2,1)S(1)} %get-tuple-element.9.rest_0_), channel_id=1, source_target_pairs={{0,8},{1,9},{2,10},{3,11},{4,12},{5,13},{6,14},{7,15},{8,0},{9,1},... | collective-permute-start | bytes 393224 | tf_op jit(solution)/shard_map/ppermute | solution.py:259
  15.6 22.7 %collective-permute-start.3 = (bf16[2,2,16,1024]{3,2,1,0:T(8,128)(2,1)S(1)}, bf16[2,2,16,1024]{3,2,1,0:T(8,128)(2,1)S(1)}, u32[]{:S(2)}, u32[]{:S(2)}) collective-permute-start(bf16[2,2,16,1024]{3,2,1,0:T(8,128)(2,1)S(1)} %get-tuple-element.9.rest_0_), channel_id=1, source_target_pairs={{0,4},{1,5},{2,6},{3,7},{4,0},{5,1},{6,2},{7,3},{8,12},{9,13},{10,... | collective-permute-start | bytes 393224 | tf_op jit(solution)/shard_map/ppermute | solution.py:259
  16.3 23.5 %collective-permute-start.1 = (bf16[2,2,16,1024]{3,2,1,0:T(8,128)(2,1)S(1)}, bf16[2,2,16,1024]{3,2,1,0:T(8,128)(2,1)S(1)}, u32[]{:S(2)}, u32[]{:S(2)}) collective-permute-start(bf16[2,2,16,1024]{3,2,1,0:T(8,128)(2,1)S(1)} %get-tuple-element.9.rest_0_), channel_id=1, source_target_pairs={{0,2},{1,3},{2,0},{3,1},{4,6},{5,7},{6,4},{7,5},{8,10},{9,11},{10,... | collective-permute-start | bytes 393224 | tf_op jit(solution)/shard_map/ppermute | solution.py:259
  18.2 21.9 %collective-permute-start = (bf16[2,2,16,1024]{3,2,1,0:T(8,128)(2,1)S(1)}, bf16[2,2,16,1024]{3,2,1,0:T(8,128)(2,1)S(1)}, u32[]{:S(2)}, u32[]{:S(2)}) collective-permute-start(bf16[2,2,16,1024]{3,2,1,0:T(8,128)(2,1)S(1)} %get-tuple-element.9.rest_0_), channel_id=1, source_target_pairs={{0,1},{1,0},{2,3},{3,2},{4,5},{5,4},{6,7},{7,6},{8,9},{9,8},{10,11... | collective-permute-start | bytes 393224 | tf_op jit(solution)/shard_map/ppermute | solution.py:259
  28.6 12.6 %collective-permute-start.13 = (bf16[2,2,16,1024]{3,2,1,0:T(8,128)(2,1)S(1)}, bf16[2,2,16,1024]{3,2,1,0:T(8,128)(2,1)}, u32[]{:S(2)}, u32[]{:S(2)}) collective-permute-start(bf16[2,2,16,1024]{3,2,1,0:T(8,128)(2,1)S(1)} %collective-permute-done.11.rest_12_), channel_id=1, source_target_pairs={{0,2},{1,3},{2,0},{3,1},{4,6},{5,7},{6,4},{7,5},{8,10},{9,11},{10,... | collective-permute-start | bytes 393224 | tf_op jit(solution)/shard_map/ppermute | solution.py:259
  38.4 2.9 %collective-permute-start.12 = (bf16[2,2,16,1024]{3,2,1,0:T(8,128)(2,1)S(1)}, bf16[2,2,16,1024]{3,2,1,0:T(8,128)(2,1)S(1)}, u32[]{:S(2)}, u32[]{:S(2)}) collective-permute-start(bf16[2,2,16,1024]{3,2,1,0:T(8,128)(2,1)S(1)} %collective-permute-done.11.rest_12_), channel_id=1, source_target_pairs={{0,1},{1,0},{2,3},{3,2},{4,5},{5,4},{6,7},{7,6},{8,9},{9,8},{10,11... | collective-permute-start | bytes 393224 | tf_op jit(solution)/shard_map/ppermute | solution.py:259
  38.4 6.5 %collective-permute-start.9 = (bf16[2,2,16,1024]{3,2,1,0:T(8,128)(2,1)S(1)}, bf16[2,2,16,1024]{3,2,1,0:T(8,128)(2,1)}, u32[]{:S(2)}, u32[]{:S(2)}) collective-permute-start(bf16[2,2,16,1024]{3,2,1,0:T(8,128)(2,1)S(1)} %collective-permute-done.7.rest_8_), channel_id=1, source_target_pairs={{0,2},{1,3},{2,0},{3,1},{4,6},{5,7},{6,4},{7,5},{8,10},{9,11},{10,... | collective-permute-start | bytes 393224 | tf_op jit(solution)/shard_map/ppermute | solution.py:259
  39.8 5.0 %collective-permute-start.8 = (bf16[2,2,16,1024]{3,2,1,0:T(8,128)(2,1)S(1)}, bf16[2,2,16,1024]{3,2,1,0:T(8,128)(2,1)S(1)}, u32[]{:S(2)}, u32[]{:S(2)}) collective-permute-start(bf16[2,2,16,1024]{3,2,1,0:T(8,128)(2,1)S(1)} %collective-permute-done.7.rest_8_), channel_id=1, source_target_pairs={{0,1},{1,0},{2,3},{3,2},{4,5},{5,4},{6,7},{7,6},{8,9},{9,8},{10,11... | collective-permute-start | bytes 393224 | tf_op jit(solution)/shard_map/ppermute | solution.py:259
  40.7 6.5 %collective-permute-start.5 = (bf16[2,2,16,1024]{3,2,1,0:T(8,128)(2,1)S(1)}, bf16[2,2,16,1024]{3,2,1,0:T(8,128)(2,1)}, u32[]{:S(2)}, u32[]{:S(2)}) collective-permute-start(bf16[2,2,16,1024]{3,2,1,0:T(8,128)(2,1)S(1)} %collective-permute-done.3.rest_4_), channel_id=1, source_target_pairs={{0,2},{1,3},{2,0},{3,1},{4,6},{5,7},{6,4},{7,5},{8,10},{9,11},{10,... | collective-permute-start | bytes 393224 | tf_op jit(solution)/shard_map/ppermute | solution.py:259
  41.3 6.2 %collective-permute-start.4 = (bf16[2,2,16,1024]{3,2,1,0:T(8,128)(2,1)S(1)}, bf16[2,2,16,1024]{3,2,1,0:T(8,128)(2,1)}, u32[]{:S(2)}, u32[]{:S(2)}) collective-permute-start(bf16[2,2,16,1024]{3,2,1,0:T(8,128)(2,1)S(1)} %collective-permute-done.3.rest_4_), channel_id=1, source_target_pairs={{0,1},{1,0},{2,3},{3,2},{4,5},{5,4},{6,7},{7,6},{8,9},{9,8},{10,11... | collective-permute-start | bytes 393224 | tf_op jit(solution)/shard_map/ppermute | solution.py:259
  41.9 5.5 %collective-permute-start.2 = (bf16[2,2,16,1024]{3,2,1,0:T(8,128)(2,1)S(1)}, bf16[2,2,16,1024]{3,2,1,0:T(8,128)(2,1)}, u32[]{:S(2)}, u32[]{:S(2)}) collective-permute-start(bf16[2,2,16,1024]{3,2,1,0:T(8,128)(2,1)S(1)} %collective-permute-done.1.rest_2_), channel_id=1, source_target_pairs={{0,1},{1,0},{2,3},{3,2},{4,5},{5,4},{6,7},{7,6},{8,9},{9,8},{10,11... | collective-permute-start | bytes 393224 | tf_op jit(solution)/shard_map/ppermute | solution.py:259
  44.8 2.6 %collective-permute-start.14 = (bf16[2,2,16,1024]{3,2,1,0:T(8,128)(2,1)}, bf16[2,2,16,1024]{3,2,1,0:T(8,128)(2,1)}, u32[]{:S(2)}, u32[]{:S(2)}) collective-permute-start(bf16[2,2,16,1024]{3,2,1,0:T(8,128)(2,1)} %collective-permute-done.13.rest_14_), channel_id=1, source_target_pairs={{0,1},{1,0},{2,3},{3,2},{4,5},{5,4},{6,7},{7,6},{8,9},{9,8},{10,11... | collective-permute-start | bytes 393224 | tf_op jit(solution)/shard_map/ppermute | solution.py:259
  45.5 2.0 %collective-permute-start.10 = (bf16[2,2,16,1024]{3,2,1,0:T(8,128)(2,1)}, bf16[2,2,16,1024]{3,2,1,0:T(8,128)(2,1)}, u32[]{:S(2)}, u32[]{:S(2)}) collective-permute-start(bf16[2,2,16,1024]{3,2,1,0:T(8,128)(2,1)} %collective-permute-done.9.rest_10_), channel_id=1, source_target_pairs={{0,1},{1,0},{2,3},{3,2},{4,5},{5,4},{6,7},{7,6},{8,9},{9,8},{10,11... | collective-permute-start | bytes 393224 | tf_op jit(solution)/shard_map/ppermute | solution.py:259
  47.2 1.7 %collective-permute-start.6 = (bf16[2,2,16,1024]{3,2,1,0:T(8,128)(2,1)}, bf16[2,2,16,1024]{3,2,1,0:T(8,128)(2,1)}, u32[]{:S(2)}, u32[]{:S(2)}) collective-permute-start(bf16[2,2,16,1024]{3,2,1,0:T(8,128)(2,1)} %collective-permute-done.5.rest_6_), channel_id=1, source_target_pairs={{0,1},{1,0},{2,3},{3,2},{4,5},{5,4},{6,7},{7,6},{8,9},{9,8},{10,11... | collective-permute-start | bytes 393224 | tf_op jit(solution)/shard_map/ppermute | solution.py:259
  48.9 0.9 copy-start.5
  49.8 0.9 copy-start.7
  50.7 0.9 copy-start.9
  57.1 1.4 %copy-start.14 = (bf16[16,64,1024]{2,1,0:T(8,128)(2,1)}, bf16[16,64,1024]{2,1,0:T(8,128)(2,1)S(1)}, u32[]{:S(2)}) copy-start(bf16[16,64,1024]{2,1,0:T(8,128)(2,1)S(1)} %shard_map.76.chosen_ref) | copy-start | bytes 6291460
  58.5 5.2 %copy-start.10 = (s32[2,32,32]{2,1,0:T(8,128)S(1)}, s32[2,32,32]{2,1,0:T(8,128)}, u32[]{:S(2)}) copy-start(s32[2,32,32]{2,1,0:T(8,128)} %valid_ref.3) | copy-start | bytes 24580
  58.5 5.2 %copy-start.11 = (s32[2,32]{1,0:T(2,128)S(1)}, s32[2,32]{1,0:T(2,128)}, u32[]{:S(2)}) copy-start(s32[2,32]{1,0:T(2,128)} %order_ref.3) | copy-start | bytes 772
  58.5 23.8 %all-to-all-start = ((bf16[16,16,1024]{2,1,0:T(8,128)(2,1)}), bf16[16,16,1024]{2,1,0:T(8,128)(2,1)S(1)}, u32[]{:S(2)}, u32[]{:S(2)}) async-start(bf16[16,16,1024]{2,1,0:T(8,128)(2,1)} %copy-done.2), calls=%async_computation | async-start | bytes 1048576 | tf_op jit(solution)/shard_map/all_to_all | solution.py:283
  62.4 1.3 %copy-start.12 = (bf16[1024,256]{1,0:T(8,128)(2,1)S(1)}, bf16[1024,256]{1,0:T(8,128)(2,1)}, u32[]{:S(2)}) copy-start(bf16[1024,256]{1,0:T(8,128)(2,1)} %constant.15.clone.inverse_ref) | copy-start | bytes 1572868
  62.4 1.8 %copy-start.15 = (bf16[16,64,1024]{2,1,0:T(8,128)(2,1)S(1)}, bf16[16,64,1024]{2,1,0:T(8,128)(2,1)}, u32[]{:S(2)}) copy-start(bf16[16,64,1024]{2,1,0:T(8,128)(2,1)} %copy-done.14) | copy-start | bytes 6291460
  82.3 1.3 %copy-start.13 = (bf16[1024,256]{1,0:T(8,128)(2,1)S(1)}, bf16[1024,256]{1,0:T(8,128)(2,1)}, u32[]{:S(2)}) copy-start(bf16[1024,256]{1,0:T(8,128)(2,1)} %constant.15.clone.inverse_ref) | copy-start | bytes 1572868
  82.3 1.8 %copy-start.16 = (bf16[16,64,1024]{2,1,0:T(8,128)(2,1)S(1)}, bf16[16,64,1024]{2,1,0:T(8,128)(2,1)}, u32[]{:S(2)}) copy-start(bf16[16,64,1024]{2,1,0:T(8,128)(2,1)} %copy-done.14) | copy-start | bytes 6291460
  (3 other events, 1.9 us)
where the time goes:
time: 105 us
  Pallas kernels  48.5 us (46%)
  waiting for transfers between devices  23.7 us (23%)
  starting transfers between devices  22.3 us (21%)
  local copies, waits for them, and re-layouts  9.81 us (9%)
    pallas_call x2, Pallas kernels, correlate(): pl.pallas_call(functools.partial(correlate_body, part=part, group=group,...  38.7 us
    ppermute x15, waiting for transfers between devices, swap(): return lax.ppermute(block, axis, [(i, i ^ distance) for i in range(count)])  23.7 us
    all_to_all x2, starting transfers between devices, local(): lax.all_to_all(halves[p], axis, split_axis=0, concat_axis=0)  11.3 us
    ppermute x15, starting transfers between devices, swap(): return lax.ppermute(block, axis, [(i, i ^ distance) for i in range(count)])  11.1 us
    unnamed x36, local copies, waits for them, and re-layouts  9.81 us
    pallas_call x3, Pallas kernels, whiten(): pl.pallas_call(functools.partial(whiten_body, pieces=pieces, rows=rows),...  8.02 us
  transfers between devices with their start and end apart: 17, of which 5 were waited for; matrix products, arithmetic and copies ran while one was open for 0% of the time, Pallas kernels for 24%

commit v1 on v0

--- a/solution.py
+++ b/solution.py
@@ -31,32 +31,27 @@
     return np.concatenate([factor * np.cos(angles), -factor * np.sin(angles)], axis=0).astype(jnp.bfloat16)
 
 
-def pick_body(owner_ref, records_ref, wanted_ref, *rest):
-    halves, sems = rest[:-1], rest[-1]
-    copies = [
-        pltpu.make_async_copy(records_ref.at[owner_ref[k]], wanted_ref.at[k], sems.at[k])
-        for k in range(wanted_ref.shape[0])
-    ]
-    for p, half in enumerate(halves):
-        copies.append(pltpu.make_async_copy(records_ref.at[:, p], half, sems.at[len(copies)]))
+def pick_body(owner_ref, records_ref, wanted_ref, sems):
+    steps, stations, _ = wanted_ref.shape
+    copies = []
+    for k in range(steps):
+        start = pl.multiple_of(owner_ref[k] * stations, stations)
+        copies.append(pltpu.make_async_copy(records_ref.at[pl.ds(start, stations)], wanted_ref.at[k], sems.at[k]))
     for copy in copies:
         copy.start()
     for copy in copies:
         copy.wait()
 
 
-def pick(owner, records):
-    devices, parts, some, width = records.shape
+def pick(owner, records, stations):
     steps = owner.shape[0]
-    vmem = pl.BlockSpec(memory_space=pltpu.VMEM)
     return pl.pallas_call(
         pick_body,
-        out_shape=[jax.ShapeDtypeStruct((steps, parts, some, width), records.dtype)]
-        + [jax.ShapeDtypeStruct((devices, some, width), records.dtype)] * parts,
+        out_shape=jax.ShapeDtypeStruct((steps, stations, records.shape[1]), records.dtype),
         in_specs=[pl.BlockSpec(memory_space=pltpu.SMEM), pl.BlockSpec(memory_space=pltpu.HBM)],
-        out_specs=[vmem] * (1 + parts),
-        scratch_shapes=[pltpu.SemaphoreType.DMA((steps + parts,))],
-        compiler_params=pltpu.CompilerParams(vmem_limit_bytes=8 * 2**20),
+        out_specs=pl.BlockSpec(memory_space=pltpu.VMEM),
+        scratch_shapes=[pltpu.SemaphoreType.DMA((steps,))],
+        compiler_params=pltpu.CompilerParams(vmem_limit_bytes=4 * 2**20),
     )(owner, records)
 
 
@@ -79,11 +74,12 @@
     )(row)
 
 
-def whiten_body(index_ref, *rest, pieces, rows):
+def whiten_body(index_ref, *rest, offsets, rows):
     band_ref, forward_ref, out_ref, padded, filtered = rest[-5:]
-    raw_refs = rest[:-5] if len(rest) > 6 else [rest[0].at[piece] for piece in range(pieces)]
+    stacks = rest[:-5]
+    held = [(o, stacks[k].at[i]) for k, some in enumerate(offsets) for i, o in enumerate(some)]
     stations = padded.shape[1]
-    width = raw_refs[0].shape[-1]
+    width = stacks[0].shape[-1]
     tiles = NFFT // LANES
     parts = width // LANES
     segments = out_ref.shape[0]
@@ -91,16 +87,10 @@
     edge = jnp.zeros((stations, LANES), padded.dtype)
     padded[0] = edge
     padded[segments * tiles + 1] = edge
-    for piece in range(pieces):
-        place = 1 + (index_ref[0] ^ piece) * parts
-        held = raw_refs[piece]
-        lead = len(held.shape) > 2
+    for offset, piece in held:
+        place = 1 + (index_ref[0] ^ offset) * parts
         for part in range(parts):
-            lanes = slice(part * LANES, (part + 1) * LANES)
-            if lead:
-                padded[place + part] = held[..., lanes].reshape(stations, LANES)
-            else:
-                padded[place + part] = held[:, lanes]
+            padded[place + part] = piece[:, part * LANES : (part + 1) * LANES]
     for first in range(0, segments, rows // stations):
         some = range(first, first + rows // stations)
         for tile in range(0, tiles, 2):
@@ -120,16 +110,14 @@
         out_ref[some, :, bins:] = (imag_part * factor).astype(jnp.bfloat16).reshape(-1, stations, bins)
 
 
-def whiten(raw, index, band, forward, rows=128):
-    pieces = len(raw)
-    width = raw[0].shape[-1]
-    stations = math.prod(raw[0].shape[:-1])
+def whiten(raw, offsets, index, band, forward, rows=128):
+    _, stations, width = raw[0].shape
+    pieces = sum(stack.shape[0] for stack in raw)
     segments = pieces * width // NFFT
-    operands = raw if isinstance(raw, list) else [raw]
-    return pl.pallas_call(
-        functools.partial(whiten_body, pieces=pieces, rows=rows),
+    return pl.pallas_call(
+        functools.partial(whiten_body, offsets=offsets, rows=rows),
         out_shape=jax.ShapeDtypeStruct((segments, stations, NFFT), jnp.bfloat16),
-        in_specs=[pl.BlockSpec(memory_space=pltpu.SMEM)] + [pl.BlockSpec(memory_space=pltpu.VMEM)] * (len(operands) + 2),
+        in_specs=[pl.BlockSpec(memory_space=pltpu.SMEM)] + [pl.BlockSpec(memory_space=pltpu.VMEM)] * (len(raw) + 2),
         out_specs=pl.BlockSpec(memory_space=pltpu.VMEM),
         scratch_shapes=[
             pltpu.VMEM((segments * NFFT // LANES + 2, stations, LANES), jnp.bfloat16),
@@ -141,14 +129,14 @@
             bytes_accessed=2 * segments * stations * NFFT * 2,
             transcendentals=0,
         ),
-    )(index, *operands, band, forward)
-
-
-def correlate_body(order_ref, valid_ref, own_ref, chosen_ref, inverse_ref, *rest, part, group, pair):
+    )(index, *raw, band, forward)
+
+
+def correlate_body(step_ref, order_ref, valid_ref, own_ref, chosen_ref, inverse_ref, *rest, group, pair):
     out_ref, own_parts, chosen_parts, cross, ready, sems = rest[-6:]
     segments, stations, width = own_ref.shape
-    steps, block = order_ref.shape
-    count = steps * block
+    count = chosen_ref.shape[1]
+    step = step_ref[0]
     bins = width // 2
     tiles = bins // LANES
 
@@ -167,24 +155,18 @@
     square = (stations, stations)
     diagonal = lax.broadcasted_iota(jnp.int32, square, 0) == lax.broadcasted_iota(jnp.int32, square, 1)
 
-    def place(q):
-        step = lax.div(q, block // group)
-        start = pl.multiple_of(lax.rem(q, block // group) * group, group)
-        return step, start
-
     def send(q):
-        step, start = place(q)
         slot = lax.rem(q, 2)
-        where = out_ref.at[step, pl.ds(start, group), pl.ds(part * stations, stations), :]
+        where = out_ref.at[step, pl.ds(pl.multiple_of(q * group, group), group)]
         return pltpu.make_async_copy(ready.at[slot], where, sems.at[slot])
 
     def some_rows(q, _):
-        step, start = place(q)
+        start = pl.multiple_of(q * group, group)
 
         def products(turn, _):
             tile = lax.rem(turn, tiles)
             first = lax.div(turn, tiles) * pair
-            picks = [step * block + order_ref[step, start + first + j] for j in range(pair)]
+            picks = [order_ref[step, start + first + j] for j in range(pair)]
             sums = None
             for g in range(segments):
                 own = [own_parts[n, tile, g].reshape(stations // SUB, SUB, LANES) for n in range(3)]
@@ -212,7 +194,7 @@
 
         slot = lax.rem(q, 2)
         for j in range(group):
-            row = valid[j : j + 1, part * stations : (part + 1) * stations]
+            row = valid[j : j + 1]
             kept = jnp.sum(jnp.where(diagonal, jnp.broadcast_to(row, square), 0.0), axis=1, keepdims=True)
             ready[slot, j] = lagged[j * stations : (j + 1) * stations] * kept
         send(q).start()
@@ -224,18 +206,18 @@
         send(q).wait()
 
 
-def correlate(part, parts, order, valid, own, chosen, inverse, earlier=None):
+def correlate(step, order, valid, own, chosen, inverse, earlier=None):
     segments, stations, width = own.shape
-    steps, block = order.shape
-    count = steps * block
+    steps, count = order.shape
     lags = inverse.shape[1]
-    group = min(block, 2 * SUB)
+    group = min(count, SUB)
     vmem, anywhere = pl.BlockSpec(memory_space=pltpu.VMEM), pl.BlockSpec(memory_space=pl.ANY)
-    extra, aliases = ([], {}) if earlier is None else ([earlier], {5: 0})
-    return pl.pallas_call(
-        functools.partial(correlate_body, part=part, group=group, pair=64 // stations),
-        out_shape=jax.ShapeDtypeStruct((steps, block, parts * stations, lags), jnp.float32),
-        in_specs=[pl.BlockSpec(memory_space=pltpu.SMEM)] + [vmem] * 4 + [anywhere] * len(extra),
+    smem = pl.BlockSpec(memory_space=pltpu.SMEM)
+    extra, aliases = ([], {}) if earlier is None else ([earlier], {6: 0})
+    return pl.pallas_call(
+        functools.partial(correlate_body, group=group, pair=2),
+        out_shape=jax.ShapeDtypeStruct((steps, count, stations, lags), jnp.float32),
+        in_specs=[smem] * 2 + [vmem] * 4 + [anywhere] * len(extra),
         out_specs=anywhere,
         scratch_shapes=[
             pltpu.VMEM((3, width // 2 // LANES, segments, stations, LANES), jnp.float32),
@@ -251,7 +233,7 @@
             bytes_accessed=own.size * 2 + chosen.size * 2 + count * stations * lags * 4,
             transcendentals=0,
         ),
-    )(order, valid, own, chosen, inverse, *extra)
+    )(step, order, valid, own, chosen, inverse, *extra)
 
 
 def swap(block, axis, distance):
@@ -266,32 +248,31 @@
     stations = records.shape[0] // devices
     width = records.shape[1]
 
-    parts = 2
-    wanted, *halves = pick(ref_owner, records.reshape(devices, parts, stations // parts, width))
-    pieces = {0: wanted}
+    wanted = pick(ref_owner, records, stations)
+    held, offsets = [wanted[None]], [0]
     distance = devices
-    while distance > 1:
+    while distance > 2:
         radix = 4 if distance >= 16 else 2
         distance //= radix
-        held = list(pieces.items())
-        for j in range(1, radix):
-            pieces |= {o | j * distance: swap(p, axis, j * distance) for o, p in held}
-    pieces = [pieces[o] for o in range(devices)]
-
-    resident = []
-    for p in range(parts):
-        resident.append(lax.all_to_all(halves[p], axis, split_axis=0, concat_axis=0))
+        block = jnp.concatenate(held, axis=0)
+        held = [block] + [swap(block, axis, j * distance) for j in range(1, radix)]
+        offsets = [j * distance | o for j in range(radix) for o in offsets]
+    mine = lax.rem(index, 2)
+    of_step = lambda k: jnp.concatenate([lax.dynamic_index_in_dim(part, k, 1, keepdims=False) for part in held], axis=0)
+    kept = of_step(mine)
+    taken = swap(of_step(1 - mine), axis, 1)
+
+    rows = lax.all_to_all(records.reshape(devices, stations, width), axis, split_axis=0, concat_axis=0)
 
     band = band_matrix(filter_taps)
     forward = jnp.asarray(forward_matrix(NFFT))
     inverse = jnp.asarray(inverse_transform_matrix(NFFT, LAGS, devices * width // NFFT))
-    chosen = whiten(pieces, index[None], band, forward)
-    zero = jnp.zeros((1,), jnp.int32)
-    result = None
-    for p in range(parts):
-        own = whiten(resident[p], zero, band, forward)
-        result = correlate(p, parts, reference_station_order, pair_valid, own, chosen, inverse, result)
-    return result
+    first = whiten([kept, taken], [offsets, [o | 1 for o in offsets]], index[None], band, forward)
+    second = swap(first, axis, 1)
+    own = whiten([rows], [list(range(devices))], jnp.zeros((1,), jnp.int32), band, forward)
+    order = reference_station_order
+    done = correlate(mine[None], order, pair_valid, own, first, inverse)
+    return correlate(1 - mine[None], order, pair_valid, own, second, inverse, done)
 
 
 def solution(mesh):

time: 105 us -> 104 us (level)
  waiting for transfers between devices: 23.7 us -> 46 us
  starting transfers between devices: 22.3 us -> 13.8 us
  local copies, waits for them, and re-layouts: 9.81 us -> 1.7 us
  Pallas kernels: 48.5 us -> 42 us
    ppermute x15 -> x6, waiting for transfers between devices: 23.7 us -> 46 us  [swap(): return lax.ppermute(block, axis, [(i, i ^ distance) for i in range(count)])]
    unnamed x36 -> x16, local copies, waits for them, and re-layouts: 9.81 us -> 1.63 us
    pallas_call x6 -> x5, Pallas kernels: 48.3 us -> 41.8 us  [the longest x2 36.5 us: correlate(): pl.pallas_call(functools.partial(correlate_body, group=group, pair=2), ou...]
    ppermute x15 -> x6, starting transfers between devices: 11.1 us -> 6.26 us  [swap(): return lax.ppermute(block, axis, [(i, i ^ distance) for i in range(count)])]
    all_to_all x2 -> x1, starting transfers between devices: 11.3 us -> 7.55 us  [local(): lax.all_to_all(records.reshape(devices, stations, width), axis, split_axi...]
  transfers between devices with their start and end apart: 17 -> 7, of which waited for: 5 -> 4; matrix products, arithmetic and copies ran while one was open for 0% -> 0% of each run, Pallas kernels for 24% -> 23%
where the time goes in v1:
time: 104 us
  waiting for transfers between devices  46 us (44%)
  Pallas kernels  42 us (40%)
  starting transfers between devices  13.8 us (13%)
  local copies, waits for them, and re-layouts  1.7 us (2%)
    ppermute x6, waiting for transfers between devices, swap(): return lax.ppermute(block, axis, [(i, i ^ distance) for i in range(count)])  46 us
    pallas_call x2, Pallas kernels, correlate(): pl.pallas_call(functools.partial(correlate_body, group=group, pair=2), ou...  36.5 us
    all_to_all x1, starting transfers between devices, local(): lax.all_to_all(records.reshape(devices, stations, width), axis, split_axi...  7.55 us
    ppermute x6, starting transfers between devices, swap(): return lax.ppermute(block, axis, [(i, i ^ distance) for i in range(count)])  6.26 us
    pallas_call x2, Pallas kernels, whiten(): pl.pallas_call(functools.partial(whiten_body, offsets=offsets, rows=rows)...  4.52 us
  transfers between devices with their start and end apart: 7, of which 4 were waited for; matrix products, arithmetic and copies ran while one was open for 0% of the time, Pallas kernels for 23%

profile of v1, /device:TPU:0, one launch (start us, length us, event | category | flops | bytes accessed | tf_op | source)
XLA Modules:
  0.0 103.8 jit_solution(17057983667396778938)
XLA Ops:
  0.0 7.5 %all-to-all-start = ((bf16[16,32,1024]{2,1,0:T(8,128)(2,1)}), bf16[16,32,1024]{2,1,0:T(8,128)(2,1)S(1)}, u32[]{:S(2)}, u32[]{:S(2)}) async-start(bf16[16,32,1024]{2,1,0:T(8,128)(2,1)} %bitcast.13), calls=%async_computation | async-start | bytes 2097152 | tf_op jit(solution)/shard_map/all_to_all | solution.py:265
  7.6 0.0 copy-done
  7.6 0.0 copy-done.1
  7.6 0.7 shard_map.75
  8.3 0.0 copy-start.7
  8.3 3.8 %collective-permute-start.2 = (bf16[1,2,32,1024]{3,2,1,0:T(8,128)(2,1)S(1)}, bf16[1,2,32,1024]{3,2,1,0:T(8,128)(2,1)S(1)}, u32[]{:S(2)}, u32[]{:S(2)}) collective-permute-start(bf16[1,2,32,1024]{3,2,1,0:T(8,128)(2,1)S(1)} %bitcast.14), channel_id=1, source_target_pairs={{0,12},{1,13},{2,14},{3,15},{4,8},{5,9},{6,10},{7,11},{8,4},{9,5},... | collective-permute-start | bytes 393224 | tf_op jit(solution)/shard_map/ppermute | solution.py:241
  12.1 0.0 collective-permute-start.1
  12.1 0.7 collective-permute-start
  12.8 20.1 %collective-permute-done.2 = bf16[1,2,32,1024]{3,2,1,0:T(8,128)(2,1)S(1)} collective-permute-done((bf16[1,2,32,1024]{3,2,1,0:T(8,128)(2,1)S(1)}, bf16[1,2,32,1024]{3,2,1,0:T(8,128)(2,1)S(1)}, u32[]{:S(2)}, u32[]{:S(2)}) %collective-permute-start.2) | collective-permute-done | bytes 131104 | tf_op jit(solution)/shard_map/ppermute | solution.py:241
  32.9 12.4 %collective-permute-done.1 = bf16[1,2,32,1024]{3,2,1,0:T(8,128)(2,1)S(1)} collective-permute-done((bf16[1,2,32,1024]{3,2,1,0:T(8,128)(2,1)S(1)}, bf16[1,2,32,1024]{3,2,1,0:T(8,128)(2,1)S(1)}, u32[]{:S(2)}, u32[]{:S(2)}) %collective-permute-start.1) | collective-permute-done | bytes 131104 | tf_op jit(solution)/shard_map/ppermute | solution.py:241
  45.3 0.0 collective-permute-done
  45.3 0.1 pad_maximum_fusion
  45.4 1.5 %collective-permute-start.3 = (bf16[4,2,32,1024]{3,2,1,0:T(8,128)(2,1)S(1)}, bf16[4,2,32,1024]{3,2,1,0:T(8,128)(2,1)S(1)}, u32[]{:S(2)}, u32[]{:S(2)}) collective-permute-start(bf16[4,2,32,1024]{3,2,1,0:T(8,128)(2,1)S(1)} %pad_maximum_fusion), channel_id=1, source_target_pairs={{0,2},{1,3},{2,0},{3,1},{4,6},{5,7},{6,4},{7,5},{8,10},{9,11},{10,... | collective-permute-start | bytes 1572872 | tf_op jit(solution)/shard_map/ppermute | solution.py:241
  47.0 11.9 %collective-permute-done.3 = bf16[4,2,32,1024]{3,2,1,0:T(8,128)(2,1)S(1)} collective-permute-done((bf16[4,2,32,1024]{3,2,1,0:T(8,128)(2,1)S(1)}, bf16[4,2,32,1024]{3,2,1,0:T(8,128)(2,1)S(1)}, u32[]{:S(2)}, u32[]{:S(2)}) %collective-permute-start.3) | collective-permute-done | bytes 524320 | tf_op jit(solution)/shard_map/ppermute | solution.py:241
  58.9 0.1 collective-permute-start.4
  59.0 0.1 pad_convert_fusion
  59.1 0.2 shard_map.73.rest_1_.rest_2_
  59.3 1.6 %collective-permute-done.4.rest_1_ = bf16[8,32,1024]{2,1,0:T(8,128)(2,1)S(1)} collective-permute-done((bf16[8,32,1024]{2,1,0:T(8,128)(2,1)S(1)}, bf16[8,32,1024]{2,1,0:T(8,128)(2,1)S(1)}, u32[]{:S(2)}, u32[]{:S(2)}) %collective-permute-start.4) | collective-permute-done | bytes 524320 | tf_op jit(solution)/shard_map/ppermute | solution.py:241
  60.9 0.0 copy-done.4
  60.9 2.3 %shard_map.76.chosen_ref = bf16[16,32,1024]{2,1,0:T(8,128)(2,1)S(1)} custom-call(s32[1]{0:T(128)} %bitcast.3.index_ref, bf16[8,32,1024]{2,1,0:T(8,128)(2,1)S(1)} %pad_maximum_fusion.1.rest_0_, bf16[8,32,1024]{2,1,0:T(8,128)(2,1)S(1)} %collective-permute-done.4.rest_1_, bf16[512,256]{1,0:T(8,128)(2,1)S(1)} %shard_map.73.rest_1_.rest_2_, ...), custom_call_target="tpu_custom_call" | custom-call | flops 1610612736 | bytes 2097152 | tf_op jit(solution)/shard_map/pallas_call | solution.py:117
  63.2 0.0 copy-start.2
  63.2 0.0 copy-start.3
  63.2 0.2 collective-permute-start.5
  63.4 0.0 all-to-all-done.rest_0_
  63.4 1.6 %copy-done.5 = bf16[1024,1024]{1,0:T(8,128)(2,1)S(1)} copy-done((bf16[1024,1024]{1,0:T(8,128)(2,1)S(1)}, bf16[1024,1024]{1,0:T(8,128)(2,1)}, u32[]{:S(2)}) %copy-start.5) | copy-done | bytes 2097176
  65.0 2.2 %shard_map.74.own_ref = bf16[16,32,1024]{2,1,0:T(8,128)(2,1)S(1)} custom-call(s32[1]{0:T(128)} %constant.31.clone.1.index_ref, bf16[16,32,1024]{2,1,0:T(8,128)(2,1)S(1)} %all-to-all-done.rest_0_, bf16[512,256]{1,0:T(8,128)(2,1)S(1)} %shard_map.73.rest_1_.rest_2_, bf16[1024,1024]{1,0:T(8,128)(2,1)S(1)} %copy-done.5), custom_call_target="tpu_custom_call" | custom-call | flops 1610612736 | bytes 2097152 | tf_op jit(solution)/shard_map/pallas_call | solution.py:117
  67.3 0.0 copy-done.2
  67.3 0.0 copy-done.3
  67.3 0.0 copy-done.6
  67.3 18.0 %shard_map.77.rest_0_ = f32[2,32,32,256]{3,2,1,0:T(8,128)} custom-call(s32[1]{0:T(128)} %bitcast.step_ref, s32[2,32]{1,0:T(2,128)S(1)} %copy-done.3, s32[2,32,32]{2,1,0:T(8,128)S(1)} %copy-done.2, bf16[16,32,1024]{2,1,0:T(8,128)(2,1)S(1)} %shard_map.74.own_ref, bf16[16,32,1024]{2,1,0:T(8,128)(2,1)S(1)} %shard_map.76.chosen_ref, bf16[1024,256]{1,0:T(8,128)(2,1)S(1)} %copy-done.6), custom_call_target="tpu_custom_call" | custom-call | flops 10000000000 | bytes 3145728 | tf_op jit(solution)/shard_map/pallas_call | solution.py:217
  85.3 0.0 collective-permute-done.5.chosen_ref
  85.3 18.6 %shard_map.78 = f32[2,32,32,256]{3,2,1,0:T(8,128)} custom-call(s32[1]{0:T(128)S(6)} %sub.6.step_ref, s32[2,32]{1,0:T(2,128)S(1)} %copy-done.3, s32[2,32,32]{2,1,0:T(8,128)S(1)} %copy-done.2, bf16[16,32,1024]{2,1,0:T(8,128)(2,1)S(1)} %shard_map.74.own_ref, bf16[16,32,1024]{2,1,0:T(8,128)(2,1)} %collective-permute-done.5.chosen_ref, ...), custom_call_target="tpu_custom_call", output_to_operand_aliasing={{}: (6, {})} | custom-call | flops 10000000000 | bytes 3145728 | tf_op jit(solution)/shard_map/pallas_call | solution.py:217
  (10 shorter events, 0.2 us)
Async XLA Ops:
  0.0 7.6 %copy-start = (bf16[512,1024]{1,0:T(8,128)(2,1)S(1)}, bf16[512,1024]{1,0:T(8,128)(2,1)}, u32[]{:S(2)}) copy-start(bf16[512,1024]{1,0:T(8,128)(2,1)} %records_ref.1) | copy-start | bytes 3145732
  0.0 7.6 %copy-start.1 = (s32[2]{0:T(128)S(1)}, s32[2]{0:T(128)}, u32[]{:S(2)}) copy-start(s32[2]{0:T(128)} %owner_ref.1) | copy-start | bytes 28
  0.0 63.4 %all-to-all-start = ((bf16[16,32,1024]{2,1,0:T(8,128)(2,1)}), bf16[16,32,1024]{2,1,0:T(8,128)(2,1)S(1)}, u32[]{:S(2)}, u32[]{:S(2)}) async-start(bf16[16,32,1024]{2,1,0:T(8,128)(2,1)} %bitcast.13), calls=%async_computation | async-start | bytes 2097152 | tf_op jit(solution)/shard_map/all_to_all | solution.py:265
  8.3 50.7 %copy-start.7 = (bf16[129]{0:T(256)(128)(2,1)S(1)}, bf16[129]{0:T(256)(128)(2,1)}, u32[]{:S(2)}) copy-start(bf16[129]{0:T(256)(128)(2,1)} %param.8) | copy-start | bytes 778
  8.3 24.6 %collective-permute-start.2 = (bf16[1,2,32,1024]{3,2,1,0:T(8,128)(2,1)S(1)}, bf16[1,2,32,1024]{3,2,1,0:T(8,128)(2,1)S(1)}, u32[]{:S(2)}, u32[]{:S(2)}) collective-permute-start(bf16[1,2,32,1024]{3,2,1,0:T(8,128)(2,1)S(1)} %bitcast.14), channel_id=1, source_target_pairs={{0,12},{1,13},{2,14},{3,15},{4,8},{5,9},{6,10},{7,11},{8,4},{9,5},... | collective-permute-start | bytes 393224 | tf_op jit(solution)/shard_map/ppermute | solution.py:241
  12.1 33.2 %collective-permute-start.1 = (bf16[1,2,32,1024]{3,2,1,0:T(8,128)(2,1)S(1)}, bf16[1,2,32,1024]{3,2,1,0:T(8,128)(2,1)S(1)}, u32[]{:S(2)}, u32[]{:S(2)}) collective-permute-start(bf16[1,2,32,1024]{3,2,1,0:T(8,128)(2,1)S(1)} %bitcast.15), channel_id=1, source_target_pairs={{0,8},{1,9},{2,10},{3,11},{4,12},{5,13},{6,14},{7,15},{8,0},{9,1},... | collective-permute-start | bytes 393224 | tf_op jit(solution)/shard_map/ppermute | solution.py:241
  12.1 33.2 %collective-permute-start = (bf16[1,2,32,1024]{3,2,1,0:T(8,128)(2,1)S(1)}, bf16[1,2,32,1024]{3,2,1,0:T(8,128)(2,1)S(1)}, u32[]{:S(2)}, u32[]{:S(2)}) collective-permute-start(bf16[1,2,32,1024]{3,2,1,0:T(8,128)(2,1)S(1)} %bitcast.16), channel_id=1, source_target_pairs={{0,4},{1,5},{2,6},{3,7},{4,0},{5,1},{6,2},{7,3},{8,12},{9,13},{10,... | collective-permute-start | bytes 393224 | tf_op jit(solution)/shard_map/ppermute | solution.py:241
  45.4 13.4 %collective-permute-start.3 = (bf16[4,2,32,1024]{3,2,1,0:T(8,128)(2,1)S(1)}, bf16[4,2,32,1024]{3,2,1,0:T(8,128)(2,1)S(1)}, u32[]{:S(2)}, u32[]{:S(2)}) collective-permute-start(bf16[4,2,32,1024]{3,2,1,0:T(8,128)(2,1)S(1)} %pad_maximum_fusion), channel_id=1, source_target_pairs={{0,2},{1,3},{2,0},{3,1},{4,6},{5,7},{6,4},{7,5},{8,10},{9,11},{10,... | collective-permute-start | bytes 1572872 | tf_op jit(solution)/shard_map/ppermute | solution.py:241
  46.9 14.0 %copy-start.4 = (bf16[1024,1024]{1,0:T(8,128)(2,1)S(1)}, bf16[1024,1024]{1,0:T(8,128)(2,1)}, u32[]{:S(2)}) copy-start(bf16[1024,1024]{1,0:T(8,128)(2,1)} %constant.35.clone.rest_2_.rest_3_) | copy-start | bytes 6291460
  58.9 2.0 %collective-permute-start.4 = (bf16[8,32,1024]{2,1,0:T(8,128)(2,1)S(1)}, bf16[8,32,1024]{2,1,0:T(8,128)(2,1)S(1)}, u32[]{:S(2)}, u32[]{:S(2)}) collective-permute-start(bf16[8,32,1024]{2,1,0:T(8,128)(2,1)S(1)} %pad_maximum_fusion.2), channel_id=1, source_target_pairs={{0,1},{1,0},{2,3},{3,2},{4,5},{5,4},{6,7},{7,6},{8,9},{9,8},{10,11... | collective-permute-start | bytes 1572872 | tf_op jit(solution)/shard_map/ppermute | solution.py:241
  63.2 4.1 %copy-start.2 = (s32[2,32,32]{2,1,0:T(8,128)S(1)}, s32[2,32,32]{2,1,0:T(8,128)}, u32[]{:S(2)}) copy-start(s32[2,32,32]{2,1,0:T(8,128)} %valid_ref.3) | copy-start | bytes 24580
  63.2 4.1 %copy-start.3 = (s32[2,32]{1,0:T(2,128)S(1)}, s32[2,32]{1,0:T(2,128)}, u32[]{:S(2)}) copy-start(s32[2,32]{1,0:T(2,128)} %order_ref.3) | copy-start | bytes 772
  63.2 22.1 %collective-permute-start.5 = (bf16[16,32,1024]{2,1,0:T(8,128)(2,1)S(1)}, bf16[16,32,1024]{2,1,0:T(8,128)(2,1)}, u32[]{:S(2)}, u32[]{:S(2)}) collective-permute-start(bf16[16,32,1024]{2,1,0:T(8,128)(2,1)S(1)} %shard_map.76.chosen_ref), channel_id=1, source_target_pairs={{0,1},{1,0},{2,3},{3,2},{4,5},{5,4},{6,7},{7,6},{8,9},{9,8},{10,11... | collective-permute-start | bytes 3145736 | tf_op jit(solution)/shard_map/ppermute | solution.py:241
  63.4 1.6 %copy-start.5 = (bf16[1024,1024]{1,0:T(8,128)(2,1)S(1)}, bf16[1024,1024]{1,0:T(8,128)(2,1)}, u32[]{:S(2)}) copy-start(bf16[1024,1024]{1,0:T(8,128)(2,1)} %constant.35.clone.rest_2_.rest_3_) | copy-start | bytes 6291460
  65.0 2.3 %copy-start.6 = (bf16[1024,256]{1,0:T(8,128)(2,1)S(1)}, bf16[1024,256]{1,0:T(8,128)(2,1)}, u32[]{:S(2)}) copy-start(bf16[1024,256]{1,0:T(8,128)(2,1)} %constant.36.clone.inverse_ref) | copy-start | bytes 1572868

commit v2 on v1

--- a/solution.py
+++ b/solution.py
@@ -51,7 +51,7 @@
         in_specs=[pl.BlockSpec(memory_space=pltpu.SMEM), pl.BlockSpec(memory_space=pltpu.HBM)],
         out_specs=pl.BlockSpec(memory_space=pltpu.VMEM),
         scratch_shapes=[pltpu.SemaphoreType.DMA((steps,))],
-        compiler_params=pltpu.CompilerParams(vmem_limit_bytes=4 * 2**20),
+        compiler_params=pltpu.CompilerParams(vmem_limit_bytes=60 * 2**20),
     )(owner, records)
 
 
@@ -75,8 +75,10 @@
 
 
 def whiten_body(index_ref, *rest, offsets, rows):
-    band_ref, forward_ref, out_ref, padded, filtered = rest[-5:]
-    stacks = rest[:-5]
+    band_ref, forward_source, out_ref, padded, filtered, forward_ref, sem = rest[-7:]
+    brought = pltpu.make_async_copy(forward_source, forward_ref, sem)
+    brought.start()
+    stacks = rest[:-7]
     held = [(o, stacks[k].at[i]) for k, some in enumerate(offsets) for i, o in enumerate(some)]
     stations = padded.shape[1]
     width = stacks[0].shape[-1]
@@ -97,10 +99,14 @@
             window = jnp.concatenate(
                 [jnp.concatenate([padded[g * tiles + tile + i] for g in some], axis=0) for i in range(4)], axis=1
             )
-            filtered[:, tile * LANES : (tile + 2) * LANES] = jnp.dot(
+            filtered[first * stations : first * stations + rows, tile * LANES : (tile + 2) * LANES] = jnp.dot(
                 window, band_ref[...], preferred_element_type=jnp.float32
             ).astype(jnp.bfloat16)
-        spectra = jnp.dot(filtered[...], forward_ref[...], preferred_element_type=jnp.float32)
+    brought.wait()
+    for first in range(0, segments, rows // stations):
+        spectra = jnp.dot(
+            filtered[first * stations : first * stations + rows], forward_ref[...], preferred_element_type=jnp.float32
+        )
         real_part, imag_part = spectra[:, :bins], spectra[:, bins:]
         energy = real_part * real_part + imag_part * imag_part
         water_level = jnp.sum(energy, axis=-1, keepdims=True) * (1.0 / bins)
@@ -117,13 +123,16 @@
     return pl.pallas_call(
         functools.partial(whiten_body, offsets=offsets, rows=rows),
         out_shape=jax.ShapeDtypeStruct((segments, stations, NFFT), jnp.bfloat16),
-        in_specs=[pl.BlockSpec(memory_space=pltpu.SMEM)] + [pl.BlockSpec(memory_space=pltpu.VMEM)] * (len(raw) + 2),
+        in_specs=[pl.BlockSpec(memory_space=pltpu.SMEM)] + [pl.BlockSpec(memory_space=pltpu.VMEM)] * (len(raw) + 1)
+        + [pl.BlockSpec(memory_space=pl.ANY)],
         out_specs=pl.BlockSpec(memory_space=pltpu.VMEM),
         scratch_shapes=[
             pltpu.VMEM((segments * NFFT // LANES + 2, stations, LANES), jnp.bfloat16),
-            pltpu.VMEM((rows, NFFT), jnp.bfloat16),
+            pltpu.VMEM((segments * stations, NFFT), jnp.bfloat16),
+            pltpu.VMEM(forward.shape, forward.dtype),
+            pltpu.SemaphoreType.DMA,
         ],
-        compiler_params=pltpu.CompilerParams(vmem_limit_bytes=10 * 2**20),
+        compiler_params=pltpu.CompilerParams(vmem_limit_bytes=50 * 2**20),
         cost_estimate=pl.CostEstimate(
             flops=2 * segments * stations * NFFT * (NFFT + 512),
             bytes_accessed=2 * segments * stations * NFFT * 2,
@@ -132,108 +141,134 @@
     )(index, *raw, band, forward)
 
 
-def correlate_body(step_ref, order_ref, valid_ref, own_ref, chosen_ref, inverse_ref, *rest, group, pair):
-    out_ref, own_parts, chosen_parts, cross, ready, sems = rest[-6:]
+def correlate_body(
+    mine_ref, order_ref, valid_ref, own_ref, first_ref, second_ref, inverse_ref, out_ref, *rest, group, unroll, pitch
+):
+    paired, products, cross, ready, sems = rest
     segments, stations, width = own_ref.shape
-    count = chosen_ref.shape[1]
-    step = step_ref[0]
+    steps, block = order_ref.shape
+    count = steps * block
     bins = width // 2
     tiles = bins // LANES
-
-    def prepare(g, _):
-        where = pl.ds(pl.multiple_of(g * count, count), count)
+    depth = 2 * segments
+    half = 2 * stations
+    (near, far), (near_out, far_out) = pitch
+    mine = mine_ref[0]
+
+    def arrange(g, _):
         for tile in range(tiles):
             real = slice(tile * LANES, (tile + 1) * LANES)
             imag = slice(bins + tile * LANES, bins + (tile + 1) * LANES)
-            c, d = own_ref[g, :, real].astype(jnp.float32), own_ref[g, :, imag].astype(jnp.float32)
-            own_parts[0, tile, g], own_parts[1, tile, g], own_parts[2, tile, g] = c, c + d, c - d
-            a, b = chosen_ref[g, :, real].astype(jnp.float32), chosen_ref[g, :, imag].astype(jnp.float32)
-            chosen_parts[0, tile, where], chosen_parts[1, tile, where], chosen_parts[2, tile, where] = a + b, a, b
+            re, im = own_ref[g, :, real], own_ref[g, :, imag]
+            for part in range(2):
+                lanes = imag if part else real
+                chosen = [first_ref[g, :, lanes], second_ref[g, :, lanes]]
+                resident = [im, re] if part else [re, -im]
+                stack = jnp.concatenate(resident + chosen if tile % 2 == 0 else chosen + resident, axis=0)
+                where = pl.ds((part * segments + g) * near + tile, LANES, stride=far)
+                paired[where, :] = stack.T.astype(jnp.float32)
         return 0
 
-    lax.fori_loop(0, segments, prepare, 0, unroll=2)
+    lax.fori_loop(0, segments, arrange, 0)
+    low = lax.broadcasted_iota(jnp.int32, (depth, LANES), 1) < half
+    column = lax.broadcasted_iota(jnp.int32, (count, tiles * depth), 1)
+    even = lax.rem(lax.div(column, depth), 2) == 0
+    none = jnp.zeros((), jnp.bfloat16)
+    zeros = jnp.zeros((depth, LANES), jnp.bfloat16)
+
+    def multiply(q, _):
+        parts = [
+            paired[pl.ds(q * far + tile, depth, stride=near), :].astype(jnp.bfloat16) for tile in range(tiles)
+        ]
+        turned = jnp.concatenate(parts, axis=0).T
+        left = jnp.where(even, turned[half:], turned[:half])
+        right = []
+        for tile in range(tiles):
+            kept = jnp.where(low if tile % 2 == 0 else ~low, parts[tile], none)
+            blocks = [zeros] * (tiles // 2)
+            blocks[tile // 2] = kept
+            right.append(jnp.concatenate(blocks, axis=1))
+        result = jnp.dot(left, jnp.concatenate(right, axis=0), preferred_element_type=jnp.float32)
+        for h in range(tiles // 2):
+            products[pl.ds(q * far_out + h, count, stride=near_out), :] = result[:, h * LANES : (h + 1) * LANES]
+        return 0
+
+    lax.fori_loop(0, LANES, multiply, 0, unroll=unroll)
     square = (stations, stations)
     diagonal = lax.broadcasted_iota(jnp.int32, square, 0) == lax.broadcasted_iota(jnp.int32, square, 1)
-
-    def send(q):
-        slot = lax.rem(q, 2)
-        where = out_ref.at[step, pl.ds(pl.multiple_of(q * group, group), group)]
-        return pltpu.make_async_copy(ready.at[slot], where, sems.at[slot])
-
-    def some_rows(q, _):
-        start = pl.multiple_of(q * group, group)
-
-        def products(turn, _):
-            tile = lax.rem(turn, tiles)
-            first = lax.div(turn, tiles) * pair
-            picks = [order_ref[step, start + first + j] for j in range(pair)]
-            sums = None
-            for g in range(segments):
-                own = [own_parts[n, tile, g].reshape(stations // SUB, SUB, LANES) for n in range(3)]
-                terms = [
-                    chosen_parts[n, tile, pl.ds(g * count + pick, SUB, stride=0), :][None] * own[n]
-                    for pick in picks
-                    for n in range(3)
-                ]
-                sums = terms if sums is None else [x + y for x, y in zip(sums, terms)]
-            for j in range(pair):
-                whole, real, imag = [s.reshape(stations, LANES) for s in sums[3 * j : 3 * j + 3]]
-                where = pl.ds(pl.multiple_of((first + j) * stations, stations), stations)
-                lanes = pl.multiple_of(tile * LANES, LANES)
-                cross[where, pl.ds(lanes, LANES)] = (whole - imag).astype(jnp.bfloat16)
-                cross[where, pl.ds(bins + lanes, LANES)] = (whole - real).astype(jnp.bfloat16)
-            return 0
-
-        lax.fori_loop(0, group // pair * tiles, products, 0)
+    turns = count // group
+
+    def place(n):
+        return lax.div(n, block // group), pl.multiple_of(lax.rem(n, block // group) * group, group)
+
+    def send(n):
+        step, start = place(n)
+        slot = lax.rem(n, 2)
+        return pltpu.make_async_copy(ready.at[slot], out_ref.at[step, pl.ds(start, group)], sems.at[slot])
+
+    def finish(n, _):
+        step, start = place(n)
+        for j in range(group):
+            row = (step ^ mine) * block + order_ref[step, start + j]
+            for h in range(tiles // 2):
+                turned = products[pl.ds(row * near_out + h, LANES, stride=far_out), :].astype(jnp.bfloat16).T
+                for tile in range(2):
+                    for part in range(2):
+                        at = (2 * tile + part) * stations
+                        lane = part * bins + (2 * h + tile) * LANES
+                        cross[j * stations : (j + 1) * stations, lane : lane + LANES] = turned[at : at + stations]
         lagged = jnp.dot(cross[...], inverse_ref[...], preferred_element_type=jnp.float32)
         valid = valid_ref[step, pl.ds(start, group), :].astype(jnp.float32)
 
-        @pl.when(q >= 2)
+        @pl.when(n >= 2)
         def _():
-            send(q - 2).wait()
-
-        slot = lax.rem(q, 2)
+            send(n - 2).wait()
+
+        slot = lax.rem(n, 2)
         for j in range(group):
-            row = valid[j : j + 1]
-            kept = jnp.sum(jnp.where(diagonal, jnp.broadcast_to(row, square), 0.0), axis=1, keepdims=True)
+            kept = jnp.sum(
+                jnp.where(diagonal, jnp.broadcast_to(valid[j : j + 1], square), 0.0), axis=1, keepdims=True
+            )
             ready[slot, j] = lagged[j * stations : (j + 1) * stations] * kept
-        send(q).start()
+        send(n).start()
         return 0
 
-    turns = count // group
-    lax.fori_loop(0, turns, some_rows, 0)
-    for q in range(max(turns - 2, 0), turns):
-        send(q).wait()
-
-
-def correlate(step, order, valid, own, chosen, inverse, earlier=None):
+    lax.fori_loop(0, turns, finish, 0)
+    for n in range(max(turns - 2, 0), turns):
+        send(n).wait()
+
+
+def correlate(mine, order, valid, own, first, second, inverse):
     segments, stations, width = own.shape
-    steps, count = order.shape
+    steps, block = order.shape
+    count = steps * block
     lags = inverse.shape[1]
-    group = min(count, SUB)
-    vmem, anywhere = pl.BlockSpec(memory_space=pltpu.VMEM), pl.BlockSpec(memory_space=pl.ANY)
-    smem = pl.BlockSpec(memory_space=pltpu.SMEM)
-    extra, aliases = ([], {}) if earlier is None else ([earlier], {6: 0})
+    tiles = width // 2 // LANES
+    depth = 2 * segments
+    assert steps == 2 and tiles * depth == LANES and 2 * stations == count and 4 * stations == LANES
+    group = min(block, 2 * SUB)
+    near, near_out = tiles + 1, tiles // 2 + 1
+    pitch = (near, near * depth + 1), (near_out, near_out * count + 1)
+    vmem, smem = pl.BlockSpec(memory_space=pltpu.VMEM), pl.BlockSpec(memory_space=pltpu.SMEM)
     return pl.pallas_call(
-        functools.partial(correlate_body, group=group, pair=2),
-        out_shape=jax.ShapeDtypeStruct((steps, count, stations, lags), jnp.float32),
-        in_specs=[smem] * 2 + [vmem] * 4 + [anywhere] * len(extra),
-        out_specs=anywhere,
+        functools.partial(correlate_body, group=group, unroll=16, pitch=pitch),
+        out_shape=jax.ShapeDtypeStruct((steps, block, stations, lags), jnp.float32),
+        in_specs=[smem] * 2 + [vmem] * 5,
+        out_specs=pl.BlockSpec(memory_space=pl.ANY),
         scratch_shapes=[
-            pltpu.VMEM((3, width // 2 // LANES, segments, stations, LANES), jnp.float32),
-            pltpu.VMEM((3, width // 2 // LANES, segments * count, LANES), jnp.float32),
+            pltpu.VMEM((LANES * pitch[0][1], LANES), jnp.float32),
+            pltpu.VMEM((LANES * pitch[1][1], LANES), jnp.float32),
             pltpu.VMEM((group * stations, width), jnp.bfloat16),
             pltpu.VMEM((2, group, stations, lags), jnp.float32),
             pltpu.SemaphoreType.DMA((2,)),
         ],
-        input_output_aliases=aliases,
-        compiler_params=pltpu.CompilerParams(vmem_limit_bytes=16 * 2**20),
+        compiler_params=pltpu.CompilerParams(vmem_limit_bytes=30 * 2**20),
         cost_estimate=pl.CostEstimate(
             flops=10**10,
-            bytes_accessed=own.size * 2 + chosen.size * 2 + count * stations * lags * 4,
+            bytes_accessed=(own.size + first.size + second.size) * 2 + count * stations * lags * 4,
             transcendentals=0,
         ),
-    )(step, order, valid, own, chosen, inverse, *extra)
+    )(mine, order, valid, own, first, second, inverse)
 
 
 def swap(block, axis, distance):
@@ -270,9 +305,7 @@
     first = whiten([kept, taken], [offsets, [o | 1 for o in offsets]], index[None], band, forward)
     second = swap(first, axis, 1)
     own = whiten([rows], [list(range(devices))], jnp.zeros((1,), jnp.int32), band, forward)
-    order = reference_station_order
-    done = correlate(mine[None], order, pair_valid, own, first, inverse)
-    return correlate(1 - mine[None], order, pair_valid, own, second, inverse, done)
+    return correlate(mine[None], reference_station_order, pair_valid, own, first, second, inverse)
 
 
 def solution(mesh):

time: 104 us -> 62.4 us (0.60)
  the two profiles are of different devices: /device:TPU:0 before, /device:TPU:9 now
where the time goes in v2:
time: 62.4 us; the launch traced here: 62 us
  waiting for transfers between devices  23.9 us (38%)
  Pallas kernels  19 us (30%)
  starting transfers between devices  17.7 us (28%)
  other arithmetic  1.14 us (2%)
    ppermute x6, waiting for transfers between devices, swap(): return lax.ppermute(block, axis, [(i, i ^ distance) for i in range(count)])  13.6 us
    ppermute x6, starting transfers between devices, swap(): return lax.ppermute(block, axis, [(i, i ^ distance) for i in range(count)])  10.4 us
    all_to_all x1, waiting for transfers between devices, local(): lax.all_to_all(records.reshape(devices, stations, width), axis, split_axi...  10.3 us
    pallas_call x1, Pallas kernels, correlate(): pl.pallas_call(functools.partial(correlate_body, group=group, unroll=16,...  9.05 us
    pallas_call x2, Pallas kernels, whiten(): pl.pallas_call(functools.partial(whiten_body, offsets=offsets, rows=rows)...  7.58 us
    all_to_all x1, starting transfers between devices, local(): lax.all_to_all(records.reshape(devices, stations, width), axis, split_axi...  7.34 us
    pallas_call x1, Pallas kernels, pick(): pl.pallas_call(pick_body, out_shape=jax.ShapeDtypeStruct((steps, stations...  2.21 us
  transfers between devices with their start and end apart: 7, of which 6 were waited for; matrix products, arithmetic and copies ran while one was open for 0% of the time, Pallas kernels for 13%

profile of v2, /device:TPU:9, one launch (start us, length us, event | category | flops | bytes accessed | tf_op | source)
XLA Modules:
  0.0 62.0 jit_solution(2778803085581388049)
XLA Ops:
  0.0 2.2 %shard_map.75 = bf16[2,32,1024]{2,1,0:T(8,128)(2,1)} custom-call(s32[2]{0:T(128)} %owner_ref.1, bf16[512,1024]{1,0:T(8,128)(2,1)} %records_ref.1), custom_call_target="tpu_custom_call" | custom-call | tf_op jit(solution)/shard_map/pallas_call | solution.py:48
  2.2 1.4 %collective-permute-start.2 = (bf16[1,2,32,1024]{3,2,1,0:T(8,128)(2,1)}, bf16[1,2,32,1024]{3,2,1,0:T(8,128)(2,1)S(1)}, u32[]{:S(2)}, u32[]{:S(2)}) collective-permute-start(bf16[1,2,32,1024]{3,2,1,0:T(8,128)(2,1)} %bitcast.14), channel_id=1, source_target_pairs={{0,12},{1,13},{2,14},{3,15},{4,8},{5,9},{6,10},{7,11},{8,4},{9,5},... | collective-permute-start | bytes 393224 | tf_op jit(solution)/shard_map/ppermute | solution.py:276
  3.6 1.1 %collective-permute-start.1 = (bf16[1,2,32,1024]{3,2,1,0:T(8,128)(2,1)}, bf16[1,2,32,1024]{3,2,1,0:T(8,128)(2,1)S(1)}, u32[]{:S(2)}, u32[]{:S(2)}) collective-permute-start(bf16[1,2,32,1024]{3,2,1,0:T(8,128)(2,1)} %bitcast.15), channel_id=1, source_target_pairs={{0,8},{1,9},{2,10},{3,11},{4,12},{5,13},{6,14},{7,15},{8,0},{9,1},... | collective-permute-start | bytes 393224 | tf_op jit(solution)/shard_map/ppermute | solution.py:276
  4.7 1.1 %collective-permute-start = (bf16[1,2,32,1024]{3,2,1,0:T(8,128)(2,1)}, bf16[1,2,32,1024]{3,2,1,0:T(8,128)(2,1)S(1)}, u32[]{:S(2)}, u32[]{:S(2)}) collective-permute-start(bf16[1,2,32,1024]{3,2,1,0:T(8,128)(2,1)} %bitcast.16), channel_id=1, source_target_pairs={{0,4},{1,5},{2,6},{3,7},{4,0},{5,1},{6,2},{7,3},{8,12},{9,13},{10,... | collective-permute-start | bytes 393224 | tf_op jit(solution)/shard_map/ppermute | solution.py:276
  5.8 6.9 %collective-permute-done.2 = bf16[1,2,32,1024]{3,2,1,0:T(8,128)(2,1)S(1)} collective-permute-done((bf16[1,2,32,1024]{3,2,1,0:T(8,128)(2,1)}, bf16[1,2,32,1024]{3,2,1,0:T(8,128)(2,1)S(1)}, u32[]{:S(2)}, u32[]{:S(2)}) %collective-permute-start.2) | collective-permute-done | bytes 131104 | tf_op jit(solution)/shard_map/ppermute | solution.py:276
  12.7 1.8 %collective-permute-done.1 = bf16[1,2,32,1024]{3,2,1,0:T(8,128)(2,1)S(1)} collective-permute-done((bf16[1,2,32,1024]{3,2,1,0:T(8,128)(2,1)}, bf16[1,2,32,1024]{3,2,1,0:T(8,128)(2,1)S(1)}, u32[]{:S(2)}, u32[]{:S(2)}) %collective-permute-start.1) | collective-permute-done | bytes 131104 | tf_op jit(solution)/shard_map/ppermute | solution.py:276
  14.5 0.1 collective-permute-done
  14.6 1.0 %pad_maximum_fusion = bf16[4,2,32,1024]{3,2,1,0:T(8,128)(2,1)S(1)} fusion(bf16[1,2,32,1024]{3,2,1,0:T(8,128)(2,1)S(1)} %collective-permute-done.2, bf16[1,2,32,1024]{3,2,1,0:T(8,128)(2,1)S(1)} %collective-permute-done.1, bf16[1,2,32,1024]{3,2,1,0:T(8,128)(2,1)S(1)} %collective-permute-done, bf16[1,2,32,1024]{3,2,1,0:T(8,128)(2,1)} %bitcast.17), kind=kLoop, calls=%fused_computation | loop fusion | flops 786432 | bytes 1048576 | tf_op jit(solution)/shard_map/concatenate | solution.py:292
  15.6 1.3 %collective-permute-start.3 = (bf16[4,2,32,1024]{3,2,1,0:T(8,128)(2,1)S(1)}, bf16[4,2,32,1024]{3,2,1,0:T(8,128)(2,1)S(1)}, u32[]{:S(2)}, u32[]{:S(2)}) collective-permute-start(bf16[4,2,32,1024]{3,2,1,0:T(8,128)(2,1)S(1)} %pad_maximum_fusion), channel_id=1, source_target_pairs={{0,2},{1,3},{2,0},{3,1},{4,6},{5,7},{6,4},{7,5},{8,10},{9,11},{10,... | collective-permute-start | bytes 1572872 | tf_op jit(solution)/shard_map/ppermute | solution.py:276
  16.9 7.3 %all-to-all-start = ((bf16[16,32,1024]{2,1,0:T(8,128)(2,1)}), bf16[16,32,1024]{2,1,0:T(8,128)(2,1)S(1)}, u32[]{:S(2)}, u32[]{:S(2)}) async-start(bf16[16,32,1024]{2,1,0:T(8,128)(2,1)} %bitcast.1), calls=%async_computation | async-start | bytes 2097152 | tf_op jit(solution)/shard_map/all_to_all | solution.py:300
  24.2 0.0 copy-start.3
  24.2 0.1 dynamic-slice_bitcast_fusion.1
  24.3 3.6 %collective-permute-done.3 = bf16[4,2,32,1024]{3,2,1,0:T(8,128)(2,1)S(1)} collective-permute-done((bf16[4,2,32,1024]{3,2,1,0:T(8,128)(2,1)S(1)}, bf16[4,2,32,1024]{3,2,1,0:T(8,128)(2,1)S(1)}, u32[]{:S(2)}, u32[]{:S(2)}) %collective-permute-start.3) | collective-permute-done | bytes 524320 | tf_op jit(solution)/shard_map/ppermute | solution.py:276
  28.0 5.1 %collective-permute-start.4 = (bf16[8,32,1024]{2,1,0:T(8,128)(2,1)S(1)}, bf16[8,32,1024]{2,1,0:T(8,128)(2,1)S(1)}, u32[]{:S(2)}, u32[]{:S(2)}) collective-permute-start(bf16[8,32,1024]{2,1,0:T(8,128)(2,1)S(1)} %pad_maximum_fusion.2), channel_id=1, source_target_pairs={{0,1},{1,0},{2,3},{3,2},{4,5},{5,4},{6,7},{7,6},{8,9},{9,8},{10,11... | collective-permute-start | bytes 1572872 | tf_op jit(solution)/shard_map/ppermute | solution.py:276
  33.1 0.0 copy-done.3
  33.1 0.1 pad_convert_fusion
  33.2 0.2 shard_map.73.rest_1_.rest_2_
  33.4 1.2 %collective-permute-done.4.rest_1_ = bf16[8,32,1024]{2,1,0:T(8,128)(2,1)S(1)} collective-permute-done((bf16[8,32,1024]{2,1,0:T(8,128)(2,1)S(1)}, bf16[8,32,1024]{2,1,0:T(8,128)(2,1)S(1)}, u32[]{:S(2)}, u32[]{:S(2)}) %collective-permute-start.4) | collective-permute-done | bytes 524320 | tf_op jit(solution)/shard_map/ppermute | solution.py:276
  34.6 3.8 %shard_map.76.first_ref = bf16[16,32,1024]{2,1,0:T(8,128)(2,1)S(1)} custom-call(s32[1]{0:T(128)} %bitcast.3.index_ref, bf16[8,32,1024]{2,1,0:T(8,128)(2,1)S(1)} %pad_maximum_fusion.1.rest_0_, bf16[8,32,1024]{2,1,0:T(8,128)(2,1)S(1)} %collective-permute-done.4.rest_1_, bf16[512,256]{1,0:T(8,128)(2,1)S(1)} %shard_map.73.rest_1_.rest_2_, ...), custom_call_target="tpu_custom_call" | custom-call | flops 1610612736 | bytes 2097152 | tf_op jit(solution)/shard_map/pallas_call | solution.py:123
  38.4 0.0 copy-start
  38.4 0.0 copy-start.1
  38.4 0.4 collective-permute-start.5
  38.9 10.3 %all-to-all-done.rest_0_ = bf16[16,32,1024]{2,1,0:T(8,128)(2,1)S(1)} async-done(((bf16[16,32,1024]{2,1,0:T(8,128)(2,1)}), bf16[16,32,1024]{2,1,0:T(8,128)(2,1)S(1)}, u32[]{:S(2)}, u32[]{:S(2)}) %all-to-all-start) | async-done | bytes 1048608 | tf_op jit(solution)/shard_map/all_to_all | solution.py:300
  49.1 0.0 copy-start.2
  49.2 3.8 %shard_map.74.own_ref = bf16[16,32,1024]{2,1,0:T(8,128)(2,1)S(1)} custom-call(s32[1]{0:T(128)} %constant.29.clone.1.index_ref, bf16[16,32,1024]{2,1,0:T(8,128)(2,1)S(1)} %all-to-all-done.rest_0_, bf16[512,256]{1,0:T(8,128)(2,1)S(1)} %shard_map.73.rest_1_.rest_2_, bf16[1024,1024]{1,0:T(8,128)(2,1)} %constant.33.clone.rest_2_.rest_3_), custom_call_target="tpu_custom_call" | custom-call | flops 1610612736 | bytes 2097152 | tf_op jit(solution)/shard_map/pallas_call | solution.py:123
  52.9 0.0 collective-permute-done.5.second_ref
  53.0 0.0 copy-done
  53.0 0.0 copy-done.1
  53.0 0.0 copy-done.2
  53.0 9.1 %shard_map.77 = f32[2,32,32,256]{3,2,1,0:T(8,128)} custom-call(s32[1]{0:T(128)} %bitcast.mine_ref, s32[2,32]{1,0:T(2,128)S(1)} %copy-done.1, s32[2,32,32]{2,1,0:T(8,128)S(1)} %copy-done, bf16[16,32,1024]{2,1,0:T(8,128)(2,1)S(1)} %shard_map.74.own_ref, bf16[16,32,1024]{2,1,0:T(8,128)(2,1)S(1)} %shard_map.76.first_ref, ...), custom_call_target="tpu_custom_call" | custom-call | flops 10000000000 | bytes 5242880 | tf_op jit(solution)/shard_map/pallas_call | solution.py:253
  (3 shorter events, 0.1 us)
Async XLA Ops:
  2.2 10.5 %collective-permute-start.2 = (bf16[1,2,32,1024]{3,2,1,0:T(8,128)(2,1)}, bf16[1,2,32,1024]{3,2,1,0:T(8,128)(2,1)S(1)}, u32[]{:S(2)}, u32[]{:S(2)}) collective-permute-start(bf16[1,2,32,1024]{3,2,1,0:T(8,128)(2,1)} %bitcast.14), channel_id=1, source_target_pairs={{0,12},{1,13},{2,14},{3,15},{4,8},{5,9},{6,10},{7,11},{8,4},{9,5},... | collective-permute-start | bytes 393224 | tf_op jit(solution)/shard_map/ppermute | solution.py:276
  3.6 10.9 %collective-permute-start.1 = (bf16[1,2,32,1024]{3,2,1,0:T(8,128)(2,1)}, bf16[1,2,32,1024]{3,2,1,0:T(8,128)(2,1)S(1)}, u32[]{:S(2)}, u32[]{:S(2)}) collective-permute-start(bf16[1,2,32,1024]{3,2,1,0:T(8,128)(2,1)} %bitcast.15), channel_id=1, source_target_pairs={{0,8},{1,9},{2,10},{3,11},{4,12},{5,13},{6,14},{7,15},{8,0},{9,1},... | collective-permute-start | bytes 393224 | tf_op jit(solution)/shard_map/ppermute | solution.py:276
  4.7 9.9 %collective-permute-start = (bf16[1,2,32,1024]{3,2,1,0:T(8,128)(2,1)}, bf16[1,2,32,1024]{3,2,1,0:T(8,128)(2,1)S(1)}, u32[]{:S(2)}, u32[]{:S(2)}) collective-permute-start(bf16[1,2,32,1024]{3,2,1,0:T(8,128)(2,1)} %bitcast.16), channel_id=1, source_target_pairs={{0,4},{1,5},{2,6},{3,7},{4,0},{5,1},{6,2},{7,3},{8,12},{9,13},{10,... | collective-permute-start | bytes 393224 | tf_op jit(solution)/shard_map/ppermute | solution.py:276
  15.6 12.3 %collective-permute-start.3 = (bf16[4,2,32,1024]{3,2,1,0:T(8,128)(2,1)S(1)}, bf16[4,2,32,1024]{3,2,1,0:T(8,128)(2,1)S(1)}, u32[]{:S(2)}, u32[]{:S(2)}) collective-permute-start(bf16[4,2,32,1024]{3,2,1,0:T(8,128)(2,1)S(1)} %pad_maximum_fusion), channel_id=1, source_target_pairs={{0,2},{1,3},{2,0},{3,1},{4,6},{5,7},{6,4},{7,5},{8,10},{9,11},{10,... | collective-permute-start | bytes 1572872 | tf_op jit(solution)/shard_map/ppermute | solution.py:276
  16.9 32.3 %all-to-all-start = ((bf16[16,32,1024]{2,1,0:T(8,128)(2,1)}), bf16[16,32,1024]{2,1,0:T(8,128)(2,1)S(1)}, u32[]{:S(2)}, u32[]{:S(2)}) async-start(bf16[16,32,1024]{2,1,0:T(8,128)(2,1)} %bitcast.1), calls=%async_computation | async-start | bytes 2097152 | tf_op jit(solution)/shard_map/all_to_all | solution.py:300
  24.2 8.8 %copy-start.3 = (bf16[129]{0:T(256)(128)(2,1)S(1)}, bf16[129]{0:T(256)(128)(2,1)}, u32[]{:S(2)}) copy-start(bf16[129]{0:T(256)(128)(2,1)} %param.8) | copy-start | bytes 778
  28.0 6.6 %collective-permute-start.4 = (bf16[8,32,1024]{2,1,0:T(8,128)(2,1)S(1)}, bf16[8,32,1024]{2,1,0:T(8,128)(2,1)S(1)}, u32[]{:S(2)}, u32[]{:S(2)}) collective-permute-start(bf16[8,32,1024]{2,1,0:T(8,128)(2,1)S(1)} %pad_maximum_fusion.2), channel_id=1, source_target_pairs={{0,1},{1,0},{2,3},{3,2},{4,5},{5,4},{6,7},{7,6},{8,9},{9,8},{10,11... | collective-permute-start | bytes 1572872 | tf_op jit(solution)/shard_map/ppermute | solution.py:276
  38.4 14.5 %copy-start = (s32[2,32,32]{2,1,0:T(8,128)S(1)}, s32[2,32,32]{2,1,0:T(8,128)}, u32[]{:S(2)}) copy-start(s32[2,32,32]{2,1,0:T(8,128)} %valid_ref.1) | copy-start | bytes 24580
  38.4 14.5 %copy-start.1 = (s32[2,32]{1,0:T(2,128)S(1)}, s32[2,32]{1,0:T(2,128)}, u32[]{:S(2)}) copy-start(s32[2,32]{1,0:T(2,128)} %order_ref.1) | copy-start | bytes 772
  38.4 14.5 %collective-permute-start.5 = (bf16[16,32,1024]{2,1,0:T(8,128)(2,1)S(1)}, bf16[16,32,1024]{2,1,0:T(8,128)(2,1)S(1)}, u32[]{:S(2)}, u32[]{:S(2)}) collective-permute-start(bf16[16,32,1024]{2,1,0:T(8,128)(2,1)S(1)} %shard_map.76.first_ref), channel_id=1, source_target_pairs={{0,1},{1,0},{2,3},{3,2},{4,5},{5,4},{6,7},{7,6},{8,9},{9,8},{10,11... | collective-permute-start | bytes 3145736 | tf_op jit(solution)/shard_map/ppermute | solution.py:276
  49.1 3.8 %copy-start.2 = (bf16[1024,256]{1,0:T(8,128)(2,1)S(1)}, bf16[1024,256]{1,0:T(8,128)(2,1)}, u32[]{:S(2)}) copy-start(bf16[1024,256]{1,0:T(8,128)(2,1)} %constant.34.clone.inverse_ref) | copy-start | bytes 1572868

commit v3 on v2

--- a/solution.py
+++ b/solution.py
@@ -74,11 +74,26 @@
     )(row)
 
 
+def fetch_body(source_ref, out_ref, sem):
+    copy = pltpu.make_async_copy(source_ref, out_ref, sem)
+    copy.start()
+    copy.wait()
+
+
+def fetch(matrix):
+    return pl.pallas_call(
+        fetch_body,
+        out_shape=jax.ShapeDtypeStruct(matrix.shape, matrix.dtype),
+        in_specs=[pl.BlockSpec(memory_space=pltpu.HBM)],
+        out_specs=pl.BlockSpec(memory_space=pltpu.VMEM),
+        scratch_shapes=[pltpu.SemaphoreType.DMA],
+        compiler_params=pltpu.CompilerParams(vmem_limit_bytes=50 * 2**20),
+    )(matrix)
+
+
 def whiten_body(index_ref, *rest, offsets, rows):
-    band_ref, forward_source, out_ref, padded, filtered, forward_ref, sem = rest[-7:]
-    brought = pltpu.make_async_copy(forward_source, forward_ref, sem)
-    brought.start()
-    stacks = rest[:-7]
+    band_ref, forward_ref, out_ref, padded, filtered = rest[-5:]
+    stacks = rest[:-5]
     held = [(o, stacks[k].at[i]) for k, some in enumerate(offsets) for i, o in enumerate(some)]
     stations = padded.shape[1]
     width = stacks[0].shape[-1]
@@ -99,14 +114,10 @@
             window = jnp.concatenate(
                 [jnp.concatenate([padded[g * tiles + tile + i] for g in some], axis=0) for i in range(4)], axis=1
             )
-            filtered[first * stations : first * stations + rows, tile * LANES : (tile + 2) * LANES] = jnp.dot(
+            filtered[:, tile * LANES : (tile + 2) * LANES] = jnp.dot(
                 window, band_ref[...], preferred_element_type=jnp.float32
             ).astype(jnp.bfloat16)
-    brought.wait()
-    for first in range(0, segments, rows // stations):
-        spectra = jnp.dot(
-            filtered[first * stations : first * stations + rows], forward_ref[...], preferred_element_type=jnp.float32
-        )
+        spectra = jnp.dot(filtered[...], forward_ref[...], preferred_element_type=jnp.float32)
         real_part, imag_part = spectra[:, :bins], spectra[:, bins:]
         energy = real_part * real_part + imag_part * imag_part
         water_level = jnp.sum(energy, axis=-1, keepdims=True) * (1.0 / bins)
@@ -123,16 +134,13 @@
     return pl.pallas_call(
         functools.partial(whiten_body, offsets=offsets, rows=rows),
         out_shape=jax.ShapeDtypeStruct((segments, stations, NFFT), jnp.bfloat16),
-        in_specs=[pl.BlockSpec(memory_space=pltpu.SMEM)] + [pl.BlockSpec(memory_space=pltpu.VMEM)] * (len(raw) + 1)
-        + [pl.BlockSpec(memory_space=pl.ANY)],
+        in_specs=[pl.BlockSpec(memory_space=pltpu.SMEM)] + [pl.BlockSpec(memory_space=pltpu.VMEM)] * (len(raw) + 2),
         out_specs=pl.BlockSpec(memory_space=pltpu.VMEM),
         scratch_shapes=[
             pltpu.VMEM((segments * NFFT // LANES + 2, stations, LANES), jnp.bfloat16),
-            pltpu.VMEM((segments * stations, NFFT), jnp.bfloat16),
-            pltpu.VMEM(forward.shape, forward.dtype),
-            pltpu.SemaphoreType.DMA,
+            pltpu.VMEM((rows, NFFT), jnp.bfloat16),
         ],
-        compiler_params=pltpu.CompilerParams(vmem_limit_bytes=50 * 2**20),
+        compiler_params=pltpu.CompilerParams(vmem_limit_bytes=10 * 2**20),
         cost_estimate=pl.CostEstimate(
             flops=2 * segments * stations * NFFT * (NFFT + 512),
             bytes_accessed=2 * segments * stations * NFFT * 2,
@@ -300,7 +308,7 @@
     rows = lax.all_to_all(records.reshape(devices, stations, width), axis, split_axis=0, concat_axis=0)
 
     band = band_matrix(filter_taps)
-    forward = jnp.asarray(forward_matrix(NFFT))
+    forward = fetch(jnp.asarray(forward_matrix(NFFT)))
     inverse = jnp.asarray(inverse_transform_matrix(NFFT, LAGS, devices * width // NFFT))
     first = whiten([kept, taken], [offsets, [o | 1 for o in offsets]], index[None], band, forward)
     second = swap(first, axis, 1)

time: 62.4 us -> 61.8 us (level)
  the two profiles are of different devices: /device:TPU:9 before, /device:TPU:11 now
where the time goes in v3:
time: 61.8 us; the launch traced here: 61.5 us
  waiting for transfers between devices  23.3 us (38%)
  Pallas kernels  19.5 us (32%)
  starting transfers between devices  17.3 us (28%)
  other arithmetic  1.14 us (2%)
    ppermute x6, waiting for transfers between devices, swap(): return lax.ppermute(block, axis, [(i, i ^ distance) for i in range(count)])  12.4 us
    all_to_all x1, waiting for transfers between devices, local(): lax.all_to_all(records.reshape(devices, stations, width), axis, split_axi...  10.9 us
    pallas_call x1, Pallas kernels, correlate(): pl.pallas_call(functools.partial(correlate_body, group=group, unroll=16,...  10 us
    ppermute x6, starting transfers between devices, swap(): return lax.ppermute(block, axis, [(i, i ^ distance) for i in range(count)])  9.98 us
    all_to_all x1, starting transfers between devices, local(): lax.all_to_all(records.reshape(devices, stations, width), axis, split_axi...  7.34 us
    pallas_call x2, Pallas kernels, whiten(): pl.pallas_call(functools.partial(whiten_body, offsets=offsets, rows=rows)...  5.49 us
    pallas_call x1, Pallas kernels, pick(): pl.pallas_call(pick_body, out_shape=jax.ShapeDtypeStruct((steps, stations...  2.21 us
    pallas_call x1, Pallas kernels, fetch(): pl.pallas_call(fetch_body, out_shape=jax.ShapeDtypeStruct(matrix.shape, m...  1.6 us
  transfers between devices with their start and end apart: 7, of which 5 were waited for; matrix products, arithmetic and copies ran while one was open for 0% of the time, Pallas kernels for 12%

profile of v3, /device:TPU:11, one launch (start us, length us, event | category | flops | bytes accessed | tf_op | source)
XLA Modules:
  0.0 61.5 jit_solution(15622677087137015617)
XLA Ops:
  0.0 2.2 %shard_map.76 = bf16[2,32,1024]{2,1,0:T(8,128)(2,1)} custom-call(s32[2]{0:T(128)} %owner_ref.1, bf16[512,1024]{1,0:T(8,128)(2,1)} %records_ref.1), custom_call_target="tpu_custom_call" | custom-call | tf_op jit(solution)/shard_map/pallas_call | solution.py:48
  2.2 1.4 %collective-permute-start.2 = (bf16[1,2,32,1024]{3,2,1,0:T(8,128)(2,1)}, bf16[1,2,32,1024]{3,2,1,0:T(8,128)(2,1)S(1)}, u32[]{:S(2)}, u32[]{:S(2)}) collective-permute-start(bf16[1,2,32,1024]{3,2,1,0:T(8,128)(2,1)} %bitcast.14), channel_id=1, source_target_pairs={{0,12},{1,13},{2,14},{3,15},{4,8},{5,9},{6,10},{7,11},{8,4},{9,5},... | collective-permute-start | bytes 393224 | tf_op jit(solution)/shard_map/ppermute | solution.py:284
  3.6 1.1 %collective-permute-start.1 = (bf16[1,2,32,1024]{3,2,1,0:T(8,128)(2,1)}, bf16[1,2,32,1024]{3,2,1,0:T(8,128)(2,1)S(1)}, u32[]{:S(2)}, u32[]{:S(2)}) collective-permute-start(bf16[1,2,32,1024]{3,2,1,0:T(8,128)(2,1)} %bitcast.15), channel_id=1, source_target_pairs={{0,8},{1,9},{2,10},{3,11},{4,12},{5,13},{6,14},{7,15},{8,0},{9,1},... | collective-permute-start | bytes 393224 | tf_op jit(solution)/shard_map/ppermute | solution.py:284
  4.7 1.1 %collective-permute-start = (bf16[1,2,32,1024]{3,2,1,0:T(8,128)(2,1)}, bf16[1,2,32,1024]{3,2,1,0:T(8,128)(2,1)S(1)}, u32[]{:S(2)}, u32[]{:S(2)}) collective-permute-start(bf16[1,2,32,1024]{3,2,1,0:T(8,128)(2,1)} %bitcast.16), channel_id=1, source_target_pairs={{0,4},{1,5},{2,6},{3,7},{4,0},{5,1},{6,2},{7,3},{8,12},{9,13},{10,... | collective-permute-start | bytes 393224 | tf_op jit(solution)/shard_map/ppermute | solution.py:284
  5.8 6.8 %collective-permute-done.2 = bf16[1,2,32,1024]{3,2,1,0:T(8,128)(2,1)S(1)} collective-permute-done((bf16[1,2,32,1024]{3,2,1,0:T(8,128)(2,1)}, bf16[1,2,32,1024]{3,2,1,0:T(8,128)(2,1)S(1)}, u32[]{:S(2)}, u32[]{:S(2)}) %collective-permute-start.2) | collective-permute-done | bytes 131104 | tf_op jit(solution)/shard_map/ppermute | solution.py:284
  12.6 1.9 %collective-permute-done.1 = bf16[1,2,32,1024]{3,2,1,0:T(8,128)(2,1)S(1)} collective-permute-done((bf16[1,2,32,1024]{3,2,1,0:T(8,128)(2,1)}, bf16[1,2,32,1024]{3,2,1,0:T(8,128)(2,1)S(1)}, u32[]{:S(2)}, u32[]{:S(2)}) %collective-permute-start.1) | collective-permute-done | bytes 131104 | tf_op jit(solution)/shard_map/ppermute | solution.py:284
  14.5 0.1 collective-permute-done
  14.6 1.0 %pad_maximum_fusion = bf16[4,2,32,1024]{3,2,1,0:T(8,128)(2,1)S(1)} fusion(bf16[1,2,32,1024]{3,2,1,0:T(8,128)(2,1)S(1)} %collective-permute-done.2, bf16[1,2,32,1024]{3,2,1,0:T(8,128)(2,1)S(1)} %collective-permute-done.1, bf16[1,2,32,1024]{3,2,1,0:T(8,128)(2,1)S(1)} %collective-permute-done, bf16[1,2,32,1024]{3,2,1,0:T(8,128)(2,1)} %bitcast.17), kind=kLoop, calls=%fused_computation | loop fusion | flops 786432 | bytes 1048576 | tf_op jit(solution)/shard_map/concatenate | solution.py:300
  15.6 1.3 %collective-permute-start.3 = (bf16[4,2,32,1024]{3,2,1,0:T(8,128)(2,1)S(1)}, bf16[4,2,32,1024]{3,2,1,0:T(8,128)(2,1)S(1)}, u32[]{:S(2)}, u32[]{:S(2)}) collective-permute-start(bf16[4,2,32,1024]{3,2,1,0:T(8,128)(2,1)S(1)} %pad_maximum_fusion), channel_id=1, source_target_pairs={{0,2},{1,3},{2,0},{3,1},{4,6},{5,7},{6,4},{7,5},{8,10},{9,11},{10,... | collective-permute-start | bytes 1572872 | tf_op jit(solution)/shard_map/ppermute | solution.py:284
  16.9 7.3 %all-to-all-start = ((bf16[16,32,1024]{2,1,0:T(8,128)(2,1)}), bf16[16,32,1024]{2,1,0:T(8,128)(2,1)S(1)}, u32[]{:S(2)}, u32[]{:S(2)}) async-start(bf16[16,32,1024]{2,1,0:T(8,128)(2,1)} %bitcast.1), calls=%async_computation | async-start | bytes 2097152 | tf_op jit(solution)/shard_map/all_to_all | solution.py:308
  24.2 0.0 copy-start.3
  24.3 3.6 %collective-permute-done.3 = bf16[4,2,32,1024]{3,2,1,0:T(8,128)(2,1)S(1)} collective-permute-done((bf16[4,2,32,1024]{3,2,1,0:T(8,128)(2,1)S(1)}, bf16[4,2,32,1024]{3,2,1,0:T(8,128)(2,1)S(1)}, u32[]{:S(2)}, u32[]{:S(2)}) %collective-permute-start.3) | collective-permute-done | bytes 524320 | tf_op jit(solution)/shard_map/ppermute | solution.py:284
  28.0 5.1 %collective-permute-start.4 = (bf16[8,32,1024]{2,1,0:T(8,128)(2,1)S(1)}, bf16[8,32,1024]{2,1,0:T(8,128)(2,1)S(1)}, u32[]{:S(2)}, u32[]{:S(2)}) collective-permute-start(bf16[8,32,1024]{2,1,0:T(8,128)(2,1)S(1)} %pad_maximum_fusion.2), channel_id=1, source_target_pairs={{0,1},{1,0},{2,3},{3,2},{4,5},{5,4},{6,7},{7,6},{8,9},{9,8},{10,11... | collective-permute-start | bytes 1572872 | tf_op jit(solution)/shard_map/ppermute | solution.py:284
  33.1 0.0 copy-done.3
  33.1 0.1 pad_convert_fusion
  33.1 0.2 shard_map.73.rest_1_.rest_2_
  33.3 1.6 %shard_map.74.rest_2_.rest_3_ = bf16[1024,1024]{1,0:T(8,128)(2,1)S(1)} custom-call(bf16[1024,1024]{1,0:T(8,128)(2,1)} %constant.33.clone.source_ref), custom_call_target="tpu_custom_call" | custom-call | tf_op jit(solution)/shard_map/pallas_call | solution.py:84
  35.0 0.0 collective-permute-done.4.rest_1_
  35.0 3.2 %shard_map.77.first_ref = bf16[16,32,1024]{2,1,0:T(8,128)(2,1)} custom-call(s32[1]{0:T(128)} %bitcast.3.index_ref, bf16[8,32,1024]{2,1,0:T(8,128)(2,1)S(1)} %pad_maximum_fusion.1.rest_0_, bf16[8,32,1024]{2,1,0:T(8,128)(2,1)S(1)} %collective-permute-done.4.rest_1_, bf16[512,256]{1,0:T(8,128)(2,1)S(1)} %shard_map.73.rest_1_.rest_2_, ...), custom_call_target="tpu_custom_call" | custom-call | flops 1610612736 | bytes 2097152 | tf_op jit(solution)/shard_map/pallas_call | solution.py:134
  38.2 0.0 copy-start
  38.2 0.0 copy-start.1
  38.3 0.0 collective-permute-start.5
  38.3 10.9 %all-to-all-done.rest_0_ = bf16[16,32,1024]{2,1,0:T(8,128)(2,1)S(1)} async-done(((bf16[16,32,1024]{2,1,0:T(8,128)(2,1)}), bf16[16,32,1024]{2,1,0:T(8,128)(2,1)S(1)}, u32[]{:S(2)}, u32[]{:S(2)}) %all-to-all-start) | async-done | bytes 1048608 | tf_op jit(solution)/shard_map/all_to_all | solution.py:308
  49.1 0.0 copy-start.2
  49.2 2.3 %shard_map.75.own_ref = bf16[16,32,1024]{2,1,0:T(8,128)(2,1)S(1)} custom-call(s32[1]{0:T(128)} %constant.29.clone.1.index_ref, bf16[16,32,1024]{2,1,0:T(8,128)(2,1)S(1)} %all-to-all-done.rest_0_, bf16[512,256]{1,0:T(8,128)(2,1)S(1)} %shard_map.73.rest_1_.rest_2_, bf16[1024,1024]{1,0:T(8,128)(2,1)S(1)} %shard_map.74.rest_2_.rest_3_), custom_call_target="tpu_custom_call" | custom-call | flops 1610612736 | bytes 2097152 | tf_op jit(solution)/shard_map/pallas_call | solution.py:134
  51.4 0.0 collective-permute-done.5.second_ref
  51.4 0.0 copy-done
  51.4 0.0 copy-done.1
  51.4 0.0 copy-done.2
  51.5 10.0 %shard_map.78 = f32[2,32,32,256]{3,2,1,0:T(8,128)} custom-call(s32[1]{0:T(128)} %bitcast.mine_ref, s32[2,32]{1,0:T(2,128)S(1)} %copy-done.1, s32[2,32,32]{2,1,0:T(8,128)S(1)} %copy-done, bf16[16,32,1024]{2,1,0:T(8,128)(2,1)S(1)} %shard_map.75.own_ref, bf16[16,32,1024]{2,1,0:T(8,128)(2,1)} %shard_map.77.first_ref, ...), custom_call_target="tpu_custom_call" | custom-call | flops 10000000000 | bytes 5242880 | tf_op jit(solution)/shard_map/pallas_call | solution.py:261
  (4 shorter events, 0.2 us)
Async XLA Ops:
  2.2 10.4 %collective-permute-start.2 = (bf16[1,2,32,1024]{3,2,1,0:T(8,128)(2,1)}, bf16[1,2,32,1024]{3,2,1,0:T(8,128)(2,1)S(1)}, u32[]{:S(2)}, u32[]{:S(2)}) collective-permute-start(bf16[1,2,32,1024]{3,2,1,0:T(8,128)(2,1)} %bitcast.14), channel_id=1, source_target_pairs={{0,12},{1,13},{2,14},{3,15},{4,8},{5,9},{6,10},{7,11},{8,4},{9,5},... | collective-permute-start | bytes 393224 | tf_op jit(solution)/shard_map/ppermute | solution.py:284
  3.6 10.9 %collective-permute-start.1 = (bf16[1,2,32,1024]{3,2,1,0:T(8,128)(2,1)}, bf16[1,2,32,1024]{3,2,1,0:T(8,128)(2,1)S(1)}, u32[]{:S(2)}, u32[]{:S(2)}) collective-permute-start(bf16[1,2,32,1024]{3,2,1,0:T(8,128)(2,1)} %bitcast.15), channel_id=1, source_target_pairs={{0,8},{1,9},{2,10},{3,11},{4,12},{5,13},{6,14},{7,15},{8,0},{9,1},... | collective-permute-start | bytes 393224 | tf_op jit(solution)/shard_map/ppermute | solution.py:284
  4.7 9.9 %collective-permute-start = (bf16[1,2,32,1024]{3,2,1,0:T(8,128)(2,1)}, bf16[1,2,32,1024]{3,2,1,0:T(8,128)(2,1)S(1)}, u32[]{:S(2)}, u32[]{:S(2)}) collective-permute-start(bf16[1,2,32,1024]{3,2,1,0:T(8,128)(2,1)} %bitcast.16), channel_id=1, source_target_pairs={{0,4},{1,5},{2,6},{3,7},{4,0},{5,1},{6,2},{7,3},{8,12},{9,13},{10,... | collective-permute-start | bytes 393224 | tf_op jit(solution)/shard_map/ppermute | solution.py:284
  15.6 12.3 %collective-permute-start.3 = (bf16[4,2,32,1024]{3,2,1,0:T(8,128)(2,1)S(1)}, bf16[4,2,32,1024]{3,2,1,0:T(8,128)(2,1)S(1)}, u32[]{:S(2)}, u32[]{:S(2)}) collective-permute-start(bf16[4,2,32,1024]{3,2,1,0:T(8,128)(2,1)S(1)} %pad_maximum_fusion), channel_id=1, source_target_pairs={{0,2},{1,3},{2,0},{3,1},{4,6},{5,7},{6,4},{7,5},{8,10},{9,11},{10,... | collective-permute-start | bytes 1572872 | tf_op jit(solution)/shard_map/ppermute | solution.py:284
  16.9 32.3 %all-to-all-start = ((bf16[16,32,1024]{2,1,0:T(8,128)(2,1)}), bf16[16,32,1024]{2,1,0:T(8,128)(2,1)S(1)}, u32[]{:S(2)}, u32[]{:S(2)}) async-start(bf16[16,32,1024]{2,1,0:T(8,128)(2,1)} %bitcast.1), calls=%async_computation | async-start | bytes 2097152 | tf_op jit(solution)/shard_map/all_to_all | solution.py:308
  24.2 8.8 %copy-start.3 = (bf16[129]{0:T(256)(128)(2,1)S(1)}, bf16[129]{0:T(256)(128)(2,1)}, u32[]{:S(2)}) copy-start(bf16[129]{0:T(256)(128)(2,1)} %param.8) | copy-start | bytes 778
  28.0 7.0 %collective-permute-start.4 = (bf16[8,32,1024]{2,1,0:T(8,128)(2,1)S(1)}, bf16[8,32,1024]{2,1,0:T(8,128)(2,1)S(1)}, u32[]{:S(2)}, u32[]{:S(2)}) collective-permute-start(bf16[8,32,1024]{2,1,0:T(8,128)(2,1)S(1)} %pad_maximum_fusion.2), channel_id=1, source_target_pairs={{0,1},{1,0},{2,3},{3,2},{4,5},{5,4},{6,7},{7,6},{8,9},{9,8},{10,11... | collective-permute-start | bytes 1572872 | tf_op jit(solution)/shard_map/ppermute | solution.py:284
  38.2 13.2 %copy-start = (s32[2,32,32]{2,1,0:T(8,128)S(1)}, s32[2,32,32]{2,1,0:T(8,128)}, u32[]{:S(2)}) copy-start(s32[2,32,32]{2,1,0:T(8,128)} %valid_ref.1) | copy-start | bytes 24580
  38.2 13.2 %copy-start.1 = (s32[2,32]{1,0:T(2,128)S(1)}, s32[2,32]{1,0:T(2,128)}, u32[]{:S(2)}) copy-start(s32[2,32]{1,0:T(2,128)} %order_ref.1) | copy-start | bytes 772
  38.3 13.2 %collective-permute-start.5 = (bf16[16,32,1024]{2,1,0:T(8,128)(2,1)}, bf16[16,32,1024]{2,1,0:T(8,128)(2,1)}, u32[]{:S(2)}, u32[]{:S(2)}) collective-permute-start(bf16[16,32,1024]{2,1,0:T(8,128)(2,1)} %shard_map.77.first_ref), channel_id=1, source_target_pairs={{0,1},{1,0},{2,3},{3,2},{4,5},{5,4},{6,7},{7,6},{8,9},{9,8},{10,11... | collective-permute-start | bytes 3145736 | tf_op jit(solution)/shard_map/ppermute | solution.py:284
  49.1 2.3 %copy-start.2 = (bf16[1024,256]{1,0:T(8,128)(2,1)S(1)}, bf16[1024,256]{1,0:T(8,128)(2,1)}, u32[]{:S(2)}) copy-start(bf16[1024,256]{1,0:T(8,128)(2,1)} %constant.34.clone.inverse_ref) | copy-start | bytes 1572868

commit v4 on v3

--- a/solution.py
+++ b/solution.py
@@ -13,7 +13,6 @@
 NFFT = 1024
 LAGS = 256
 LANES = 128
-SUB = 8
 
 
 def forward_matrix(length):
@@ -177,7 +176,7 @@
                 paired[where, :] = stack.T.astype(jnp.float32)
         return 0
 
-    lax.fori_loop(0, segments, arrange, 0)
+    lax.fori_loop(0, segments, arrange, 0, unroll=4)
     low = lax.broadcasted_iota(jnp.int32, (depth, LANES), 1) < half
     column = lax.broadcasted_iota(jnp.int32, (count, tiles * depth), 1)
     even = lax.rem(lax.div(column, depth), 2) == 0
@@ -254,12 +253,12 @@
     tiles = width // 2 // LANES
     depth = 2 * segments
     assert steps == 2 and tiles * depth == LANES and 2 * stations == count and 4 * stations == LANES
-    group = min(block, 2 * SUB)
+    group = block
     near, near_out = tiles + 1, tiles // 2 + 1
     pitch = (near, near * depth + 1), (near_out, near_out * count + 1)
     vmem, smem = pl.BlockSpec(memory_space=pltpu.VMEM), pl.BlockSpec(memory_space=pltpu.SMEM)
     return pl.pallas_call(
-        functools.partial(correlate_body, group=group, unroll=16, pitch=pitch),
+        functools.partial(correlate_body, group=group, unroll=64, pitch=pitch),
         out_shape=jax.ShapeDtypeStruct((steps, block, stations, lags), jnp.float32),
         in_specs=[smem] * 2 + [vmem] * 5,
         out_specs=pl.BlockSpec(memory_space=pl.ANY),
@@ -270,7 +269,7 @@
             pltpu.VMEM((2, group, stations, lags), jnp.float32),
             pltpu.SemaphoreType.DMA((2,)),
         ],
-        compiler_params=pltpu.CompilerParams(vmem_limit_bytes=30 * 2**20),
+        compiler_params=pltpu.CompilerParams(vmem_limit_bytes=33 * 2**20),
         cost_estimate=pl.CostEstimate(
             flops=10**10,
             bytes_accessed=(own.size + first.size + second.size) * 2 + count * stations * lags * 4,

time: 61.8 us -> 59.5 us (0.963)
  Pallas kernels: 19.5 us -> 17.2 us
    pallas_call x1, Pallas kernels: 10 us -> 7.72 us  [correlate(): pl.pallas_call(functools.partial(correlate_body, group=group, unroll=64,...]
where the time goes in v4:
time: 59.5 us; the launch traced here: 59.2 us
  waiting for transfers between devices  23.3 us (39%)
  starting transfers between devices  17.3 us (29%)
  Pallas kernels  17.2 us (29%)
  other arithmetic  1.14 us (2%)
    ppermute x6, waiting for transfers between devices, swap(): return lax.ppermute(block, axis, [(i, i ^ distance) for i in range(count)])  12.4 us
    all_to_all x1, waiting for transfers between devices, local(): lax.all_to_all(records.reshape(devices, stations, width), axis, split_axi...  10.9 us
    ppermute x6, starting transfers between devices, swap(): return lax.ppermute(block, axis, [(i, i ^ distance) for i in range(count)])  9.98 us
    pallas_call x1, Pallas kernels, correlate(): pl.pallas_call(functools.partial(correlate_body, group=group, unroll=64,...  7.72 us
    all_to_all x1, starting transfers between devices, local(): lax.all_to_all(records.reshape(devices, stations, width), axis, split_axi...  7.34 us
    pallas_call x2, Pallas kernels, whiten(): pl.pallas_call(functools.partial(whiten_body, offsets=offsets, rows=rows)...  5.49 us
    pallas_call x1, Pallas kernels, pick(): pl.pallas_call(pick_body, out_shape=jax.ShapeDtypeStruct((steps, stations...  2.21 us
    pallas_call x1, Pallas kernels, fetch(): pl.pallas_call(fetch_body, out_shape=jax.ShapeDtypeStruct(matrix.shape, m...  1.6 us
  transfers between devices with their start and end apart: 7, of which 5 were waited for; matrix products, arithmetic and copies ran while one was open for 0% of the time, Pallas kernels for 12%

profile of v4, /device:TPU:11, one launch (start us, length us, event | category | flops | bytes accessed | tf_op | source)
XLA Modules:
  0.0 59.2 jit_solution(9503458758310352111)
XLA Ops:
  0.0 2.2 %shard_map.76 = bf16[2,32,1024]{2,1,0:T(8,128)(2,1)} custom-call(s32[2]{0:T(128)} %owner_ref.1, bf16[512,1024]{1,0:T(8,128)(2,1)} %records_ref.1), custom_call_target="tpu_custom_call" | custom-call | tf_op jit(solution)/shard_map/pallas_call | solution.py:47
  2.2 1.4 %collective-permute-start.2 = (bf16[1,2,32,1024]{3,2,1,0:T(8,128)(2,1)}, bf16[1,2,32,1024]{3,2,1,0:T(8,128)(2,1)S(1)}, u32[]{:S(2)}, u32[]{:S(2)}) collective-permute-start(bf16[1,2,32,1024]{3,2,1,0:T(8,128)(2,1)} %bitcast.14), channel_id=1, source_target_pairs={{0,12},{1,13},{2,14},{3,15},{4,8},{5,9},{6,10},{7,11},{8,4},{9,5},... | collective-permute-start | bytes 393224 | tf_op jit(solution)/shard_map/ppermute | solution.py:283
  3.6 1.1 %collective-permute-start.1 = (bf16[1,2,32,1024]{3,2,1,0:T(8,128)(2,1)}, bf16[1,2,32,1024]{3,2,1,0:T(8,128)(2,1)S(1)}, u32[]{:S(2)}, u32[]{:S(2)}) collective-permute-start(bf16[1,2,32,1024]{3,2,1,0:T(8,128)(2,1)} %bitcast.15), channel_id=1, source_target_pairs={{0,8},{1,9},{2,10},{3,11},{4,12},{5,13},{6,14},{7,15},{8,0},{9,1},... | collective-permute-start | bytes 393224 | tf_op jit(solution)/shard_map/ppermute | solution.py:283
  4.7 1.1 %collective-permute-start = (bf16[1,2,32,1024]{3,2,1,0:T(8,128)(2,1)}, bf16[1,2,32,1024]{3,2,1,0:T(8,128)(2,1)S(1)}, u32[]{:S(2)}, u32[]{:S(2)}) collective-permute-start(bf16[1,2,32,1024]{3,2,1,0:T(8,128)(2,1)} %bitcast.16), channel_id=1, source_target_pairs={{0,4},{1,5},{2,6},{3,7},{4,0},{5,1},{6,2},{7,3},{8,12},{9,13},{10,... | collective-permute-start | bytes 393224 | tf_op jit(solution)/shard_map/ppermute | solution.py:283
  5.8 6.8 %collective-permute-done.2 = bf16[1,2,32,1024]{3,2,1,0:T(8,128)(2,1)S(1)} collective-permute-done((bf16[1,2,32,1024]{3,2,1,0:T(8,128)(2,1)}, bf16[1,2,32,1024]{3,2,1,0:T(8,128)(2,1)S(1)}, u32[]{:S(2)}, u32[]{:S(2)}) %collective-permute-start.2) | collective-permute-done | bytes 131104 | tf_op jit(solution)/shard_map/ppermute | solution.py:283
  12.6 1.9 %collective-permute-done.1 = bf16[1,2,32,1024]{3,2,1,0:T(8,128)(2,1)S(1)} collective-permute-done((bf16[1,2,32,1024]{3,2,1,0:T(8,128)(2,1)}, bf16[1,2,32,1024]{3,2,1,0:T(8,128)(2,1)S(1)}, u32[]{:S(2)}, u32[]{:S(2)}) %collective-permute-start.1) | collective-permute-done | bytes 131104 | tf_op jit(solution)/shard_map/ppermute | solution.py:283
  14.5 0.1 collective-permute-done
  14.6 1.0 %pad_maximum_fusion = bf16[4,2,32,1024]{3,2,1,0:T(8,128)(2,1)S(1)} fusion(bf16[1,2,32,1024]{3,2,1,0:T(8,128)(2,1)S(1)} %collective-permute-done.2, bf16[1,2,32,1024]{3,2,1,0:T(8,128)(2,1)S(1)} %collective-permute-done.1, bf16[1,2,32,1024]{3,2,1,0:T(8,128)(2,1)S(1)} %collective-permute-done, bf16[1,2,32,1024]{3,2,1,0:T(8,128)(2,1)} %bitcast.17), kind=kLoop, calls=%fused_computation | loop fusion | flops 786432 | bytes 1048576 | tf_op jit(solution)/shard_map/concatenate | solution.py:299
  15.6 1.3 %collective-permute-start.3 = (bf16[4,2,32,1024]{3,2,1,0:T(8,128)(2,1)S(1)}, bf16[4,2,32,1024]{3,2,1,0:T(8,128)(2,1)S(1)}, u32[]{:S(2)}, u32[]{:S(2)}) collective-permute-start(bf16[4,2,32,1024]{3,2,1,0:T(8,128)(2,1)S(1)} %pad_maximum_fusion), channel_id=1, source_target_pairs={{0,2},{1,3},{2,0},{3,1},{4,6},{5,7},{6,4},{7,5},{8,10},{9,11},{10,... | collective-permute-start | bytes 1572872 | tf_op jit(solution)/shard_map/ppermute | solution.py:283
  16.9 7.3 %all-to-all-start = ((bf16[16,32,1024]{2,1,0:T(8,128)(2,1)}), bf16[16,32,1024]{2,1,0:T(8,128)(2,1)S(1)}, u32[]{:S(2)}, u32[]{:S(2)}) async-start(bf16[16,32,1024]{2,1,0:T(8,128)(2,1)} %bitcast.1), calls=%async_computation | async-start | bytes 2097152 | tf_op jit(solution)/shard_map/all_to_all | solution.py:307
  24.2 0.0 copy-start.3
  24.3 3.6 %collective-permute-done.3 = bf16[4,2,32,1024]{3,2,1,0:T(8,128)(2,1)S(1)} collective-permute-done((bf16[4,2,32,1024]{3,2,1,0:T(8,128)(2,1)S(1)}, bf16[4,2,32,1024]{3,2,1,0:T(8,128)(2,1)S(1)}, u32[]{:S(2)}, u32[]{:S(2)}) %collective-permute-start.3) | collective-permute-done | bytes 524320 | tf_op jit(solution)/shard_map/ppermute | solution.py:283
  28.0 5.1 %collective-permute-start.4 = (bf16[8,32,1024]{2,1,0:T(8,128)(2,1)S(1)}, bf16[8,32,1024]{2,1,0:T(8,128)(2,1)S(1)}, u32[]{:S(2)}, u32[]{:S(2)}) collective-permute-start(bf16[8,32,1024]{2,1,0:T(8,128)(2,1)S(1)} %pad_maximum_fusion.2), channel_id=1, source_target_pairs={{0,1},{1,0},{2,3},{3,2},{4,5},{5,4},{6,7},{7,6},{8,9},{9,8},{10,11... | collective-permute-start | bytes 1572872 | tf_op jit(solution)/shard_map/ppermute | solution.py:283
  33.1 0.0 copy-done.3
  33.1 0.1 pad_convert_fusion
  33.1 0.2 shard_map.73.rest_1_.rest_2_
  33.3 1.6 %shard_map.74.rest_2_.rest_3_ = bf16[1024,1024]{1,0:T(8,128)(2,1)S(1)} custom-call(bf16[1024,1024]{1,0:T(8,128)(2,1)} %constant.33.clone.source_ref), custom_call_target="tpu_custom_call" | custom-call | tf_op jit(solution)/shard_map/pallas_call | solution.py:83
  35.0 0.0 collective-permute-done.4.rest_1_
  35.0 3.2 %shard_map.77.first_ref = bf16[16,32,1024]{2,1,0:T(8,128)(2,1)} custom-call(s32[1]{0:T(128)} %bitcast.3.index_ref, bf16[8,32,1024]{2,1,0:T(8,128)(2,1)S(1)} %pad_maximum_fusion.1.rest_0_, bf16[8,32,1024]{2,1,0:T(8,128)(2,1)S(1)} %collective-permute-done.4.rest_1_, bf16[512,256]{1,0:T(8,128)(2,1)S(1)} %shard_map.73.rest_1_.rest_2_, ...), custom_call_target="tpu_custom_call" | custom-call | flops 1610612736 | bytes 2097152 | tf_op jit(solution)/shard_map/pallas_call | solution.py:133
  38.2 0.0 copy-start
  38.2 0.0 copy-start.1
  38.3 0.0 collective-permute-start.5
  38.3 10.9 %all-to-all-done.rest_0_ = bf16[16,32,1024]{2,1,0:T(8,128)(2,1)S(1)} async-done(((bf16[16,32,1024]{2,1,0:T(8,128)(2,1)}), bf16[16,32,1024]{2,1,0:T(8,128)(2,1)S(1)}, u32[]{:S(2)}, u32[]{:S(2)}) %all-to-all-start) | async-done | bytes 1048608 | tf_op jit(solution)/shard_map/all_to_all | solution.py:307
  49.1 0.0 copy-start.2
  49.2 2.3 %shard_map.75.own_ref = bf16[16,32,1024]{2,1,0:T(8,128)(2,1)S(1)} custom-call(s32[1]{0:T(128)} %constant.29.clone.1.index_ref, bf16[16,32,1024]{2,1,0:T(8,128)(2,1)S(1)} %all-to-all-done.rest_0_, bf16[512,256]{1,0:T(8,128)(2,1)S(1)} %shard_map.73.rest_1_.rest_2_, bf16[1024,1024]{1,0:T(8,128)(2,1)S(1)} %shard_map.74.rest_2_.rest_3_), custom_call_target="tpu_custom_call" | custom-call | flops 1610612736 | bytes 2097152 | tf_op jit(solution)/shard_map/pallas_call | solution.py:133
  51.4 0.0 collective-permute-done.5.second_ref
  51.4 0.0 copy-done
  51.4 0.0 copy-done.1
  51.4 0.0 copy-done.2
  51.5 7.7 %shard_map.78 = f32[2,32,32,256]{3,2,1,0:T(8,128)} custom-call(s32[1]{0:T(128)} %bitcast.mine_ref, s32[2,32]{1,0:T(2,128)S(1)} %copy-done.1, s32[2,32,32]{2,1,0:T(8,128)S(1)} %copy-done, bf16[16,32,1024]{2,1,0:T(8,128)(2,1)S(1)} %shard_map.75.own_ref, bf16[16,32,1024]{2,1,0:T(8,128)(2,1)} %shard_map.77.first_ref, ...), custom_call_target="tpu_custom_call" | custom-call | flops 10000000000 | bytes 5242880 | tf_op jit(solution)/shard_map/pallas_call | solution.py:260
  (4 shorter events, 0.2 us)
Async XLA Ops:
  2.2 10.4 %collective-permute-start.2 = (bf16[1,2,32,1024]{3,2,1,0:T(8,128)(2,1)}, bf16[1,2,32,1024]{3,2,1,0:T(8,128)(2,1)S(1)}, u32[]{:S(2)}, u32[]{:S(2)}) collective-permute-start(bf16[1,2,32,1024]{3,2,1,0:T(8,128)(2,1)} %bitcast.14), channel_id=1, source_target_pairs={{0,12},{1,13},{2,14},{3,15},{4,8},{5,9},{6,10},{7,11},{8,4},{9,5},... | collective-permute-start | bytes 393224 | tf_op jit(solution)/shard_map/ppermute | solution.py:283
  3.6 10.9 %collective-permute-start.1 = (bf16[1,2,32,1024]{3,2,1,0:T(8,128)(2,1)}, bf16[1,2,32,1024]{3,2,1,0:T(8,128)(2,1)S(1)}, u32[]{:S(2)}, u32[]{:S(2)}) collective-permute-start(bf16[1,2,32,1024]{3,2,1,0:T(8,128)(2,1)} %bitcast.15), channel_id=1, source_target_pairs={{0,8},{1,9},{2,10},{3,11},{4,12},{5,13},{6,14},{7,15},{8,0},{9,1},... | collective-permute-start | bytes 393224 | tf_op jit(solution)/shard_map/ppermute | solution.py:283
  4.7 9.9 %collective-permute-start = (bf16[1,2,32,1024]{3,2,1,0:T(8,128)(2,1)}, bf16[1,2,32,1024]{3,2,1,0:T(8,128)(2,1)S(1)}, u32[]{:S(2)}, u32[]{:S(2)}) collective-permute-start(bf16[1,2,32,1024]{3,2,1,0:T(8,128)(2,1)} %bitcast.16), channel_id=1, source_target_pairs={{0,4},{1,5},{2,6},{3,7},{4,0},{5,1},{6,2},{7,3},{8,12},{9,13},{10,... | collective-permute-start | bytes 393224 | tf_op jit(solution)/shard_map/ppermute | solution.py:283
  15.6 12.3 %collective-permute-start.3 = (bf16[4,2,32,1024]{3,2,1,0:T(8,128)(2,1)S(1)}, bf16[4,2,32,1024]{3,2,1,0:T(8,128)(2,1)S(1)}, u32[]{:S(2)}, u32[]{:S(2)}) collective-permute-start(bf16[4,2,32,1024]{3,2,1,0:T(8,128)(2,1)S(1)} %pad_maximum_fusion), channel_id=1, source_target_pairs={{0,2},{1,3},{2,0},{3,1},{4,6},{5,7},{6,4},{7,5},{8,10},{9,11},{10,... | collective-permute-start | bytes 1572872 | tf_op jit(solution)/shard_map/ppermute | solution.py:283
  16.9 32.3 %all-to-all-start = ((bf16[16,32,1024]{2,1,0:T(8,128)(2,1)}), bf16[16,32,1024]{2,1,0:T(8,128)(2,1)S(1)}, u32[]{:S(2)}, u32[]{:S(2)}) async-start(bf16[16,32,1024]{2,1,0:T(8,128)(2,1)} %bitcast.1), calls=%async_computation | async-start | bytes 2097152 | tf_op jit(solution)/shard_map/all_to_all | solution.py:307
  24.2 8.8 %copy-start.3 = (bf16[129]{0:T(256)(128)(2,1)S(1)}, bf16[129]{0:T(256)(128)(2,1)}, u32[]{:S(2)}) copy-start(bf16[129]{0:T(256)(128)(2,1)} %param.8) | copy-start | bytes 778
  28.0 7.0 %collective-permute-start.4 = (bf16[8,32,1024]{2,1,0:T(8,128)(2,1)S(1)}, bf16[8,32,1024]{2,1,0:T(8,128)(2,1)S(1)}, u32[]{:S(2)}, u32[]{:S(2)}) collective-permute-start(bf16[8,32,1024]{2,1,0:T(8,128)(2,1)S(1)} %pad_maximum_fusion.2), channel_id=1, source_target_pairs={{0,1},{1,0},{2,3},{3,2},{4,5},{5,4},{6,7},{7,6},{8,9},{9,8},{10,11... | collective-permute-start | bytes 1572872 | tf_op jit(solution)/shard_map/ppermute | solution.py:283
  38.2 13.2 %copy-start = (s32[2,32,32]{2,1,0:T(8,128)S(1)}, s32[2,32,32]{2,1,0:T(8,128)}, u32[]{:S(2)}) copy-start(s32[2,32,32]{2,1,0:T(8,128)} %valid_ref.1) | copy-start | bytes 24580
  38.2 13.2 %copy-start.1 = (s32[2,32]{1,0:T(2,128)S(1)}, s32[2,32]{1,0:T(2,128)}, u32[]{:S(2)}) copy-start(s32[2,32]{1,0:T(2,128)} %order_ref.1) | copy-start | bytes 772
  38.3 13.2 %collective-permute-start.5 = (bf16[16,32,1024]{2,1,0:T(8,128)(2,1)}, bf16[16,32,1024]{2,1,0:T(8,128)(2,1)}, u32[]{:S(2)}, u32[]{:S(2)}) collective-permute-start(bf16[16,32,1024]{2,1,0:T(8,128)(2,1)} %shard_map.77.first_ref), channel_id=1, source_target_pairs={{0,1},{1,0},{2,3},{3,2},{4,5},{5,4},{6,7},{7,6},{8,9},{9,8},{10,11... | collective-permute-start | bytes 3145736 | tf_op jit(solution)/shard_map/ppermute | solution.py:283
  49.1 2.3 %copy-start.2 = (bf16[1024,256]{1,0:T(8,128)(2,1)S(1)}, bf16[1024,256]{1,0:T(8,128)(2,1)}, u32[]{:S(2)}) copy-start(bf16[1024,256]{1,0:T(8,128)(2,1)} %constant.34.clone.inverse_ref) | copy-start | bytes 1572868

commit v5 on v4

--- a/solution.py
+++ b/solution.py
@@ -291,25 +291,29 @@
     width = records.shape[1]
 
     wanted = pick(ref_owner, records, stations)
-    held, offsets = [wanted[None]], [0]
-    distance = devices
-    while distance > 2:
-        radix = 4 if distance >= 16 else 2
-        distance //= radix
-        block = jnp.concatenate(held, axis=0)
-        held = [block] + [swap(block, axis, j * distance) for j in range(1, radix)]
-        offsets = [j * distance | o for j in range(radix) for o in offsets]
+    own_piece = wanted[None]
+    far_piece = swap(own_piece, axis, devices // 2)
+    chains = {"near": (own_piece, [0]), "far": (far_piece, [devices // 2])}
+    distance, stage = devices // 4, 0
+    while distance > 1:
+        for name, (block, offsets) in chains.items():
+            block = jnp.concatenate([block, swap(block, axis, distance)], axis=0)
+            chains[name] = block, offsets + [distance | o for o in offsets]
+        distance //= 2
+        stage += 1
     mine = lax.rem(index, 2)
-    of_step = lambda k: jnp.concatenate([lax.dynamic_index_in_dim(part, k, 1, keepdims=False) for part in held], axis=0)
-    kept = of_step(mine)
-    taken = swap(of_step(1 - mine), axis, 1)
+    pieces, offsets = [], []
+    for (block, some) in chains.values():
+        pieces.append(lax.dynamic_index_in_dim(block, mine, 1, keepdims=False))
+        pieces.append(swap(lax.dynamic_index_in_dim(block, 1 - mine, 1, keepdims=False), axis, 1))
+        offsets += [some, [o | 1 for o in some]]
 
     rows = lax.all_to_all(records.reshape(devices, stations, width), axis, split_axis=0, concat_axis=0)
 
     band = band_matrix(filter_taps)
     forward = fetch(jnp.asarray(forward_matrix(NFFT)))
     inverse = jnp.asarray(inverse_transform_matrix(NFFT, LAGS, devices * width // NFFT))
-    first = whiten([kept, taken], [offsets, [o | 1 for o in offsets]], index[None], band, forward)
+    first = whiten(pieces, offsets, index[None], band, forward)
     second = swap(first, axis, 1)
     own = whiten([rows], [list(range(devices))], jnp.zeros((1,), jnp.int32), band, forward)
     return correlate(mine[None], reference_station_order, pair_valid, own, first, second, inverse)

time: 59.5 us -> 58.1 us (0.976)
  the two profiles are of different devices: /device:TPU:11 before, /device:TPU:17 now
where the time goes in v5:
time: 58.1 us; the launch traced here: 57.7 us
  waiting for transfers between devices  24.2 us (42%)
  Pallas kernels  17.2 us (30%)
  starting transfers between devices  15.9 us (27%)
    ppermute x8, waiting for transfers between devices, swap(): return lax.ppermute(block, axis, [(i, i ^ distance) for i in range(count)])  24.2 us
    ppermute x8, starting transfers between devices, swap(): return lax.ppermute(block, axis, [(i, i ^ distance) for i in range(count)])  8.98 us
    pallas_call x1, Pallas kernels, correlate(): pl.pallas_call(functools.partial(correlate_body, group=group, unroll=64,...  7.71 us
    all_to_all x1, starting transfers between devices, local(): lax.all_to_all(records.reshape(devices, stations, width), axis, split_axi...  6.91 us
    pallas_call x2, Pallas kernels, whiten(): pl.pallas_call(functools.partial(whiten_body, offsets=offsets, rows=rows)...  5.47 us
    pallas_call x1, Pallas kernels, pick(): pl.pallas_call(pick_body, out_shape=jax.ShapeDtypeStruct((steps, stations...  2.21 us
    pallas_call x1, Pallas kernels, fetch(): pl.pallas_call(fetch_body, out_shape=jax.ShapeDtypeStruct(matrix.shape, m...  1.6 us
  transfers between devices with their start and end apart: 9, of which 3 were waited for; matrix products, arithmetic and copies ran while one was open for 1% of the time, Pallas kernels for 13%

profile of v5, /device:TPU:17, one launch (start us, length us, event | category | flops | bytes accessed | tf_op | source)
XLA Modules:
  0.0 57.7 jit_solution(13750417174256663933)
XLA Ops:
  0.0 2.2 %shard_map.76 = bf16[2,32,1024]{2,1,0:T(8,128)(2,1)} custom-call(s32[2]{0:T(128)} %owner_ref.1, bf16[512,1024]{1,0:T(8,128)(2,1)} %records_ref.1), custom_call_target="tpu_custom_call" | custom-call | tf_op jit(solution)/shard_map/pallas_call | solution.py:47
  2.2 0.0 copy-start.3
  2.2 0.1 collective-permute-start.3
  2.3 1.4 %collective-permute-start = (bf16[1,2,32,1024]{3,2,1,0:T(8,128)(2,1)}, bf16[1,2,32,1024]{3,2,1,0:T(8,128)(2,1)S(1)}, u32[]{:S(2)}, u32[]{:S(2)}) collective-permute-start(bf16[1,2,32,1024]{3,2,1,0:T(8,128)(2,1)} %bitcast.16), channel_id=1, source_target_pairs={{0,4},{1,5},{2,6},{3,7},{4,0},{5,1},{6,2},{7,3},{8,12},{9,13},{10,... | collective-permute-start | bytes 393224 | tf_op jit(solution)/shard_map/ppermute | solution.py:283
  3.7 6.9 %all-to-all-start = ((bf16[16,32,1024]{2,1,0:T(8,128)(2,1)}), bf16[16,32,1024]{2,1,0:T(8,128)(2,1)S(1)}, u32[]{:S(2)}, u32[]{:S(2)}) async-start(bf16[16,32,1024]{2,1,0:T(8,128)(2,1)} %bitcast.14), calls=%async_computation | async-start | bytes 2097152 | tf_op jit(solution)/shard_map/all_to_all | solution.py:311
  10.6 0.0 collective-permute-done.3
  10.6 2.2 %collective-permute-start.4 = (bf16[1,2,32,1024]{3,2,1,0:T(8,128)(2,1)S(1)}, bf16[1,2,32,1024]{3,2,1,0:T(8,128)(2,1)S(1)}, u32[]{:S(2)}, u32[]{:S(2)}) collective-permute-start(bf16[1,2,32,1024]{3,2,1,0:T(8,128)(2,1)S(1)} %collective-permute-done.3), channel_id=1, source_target_pairs={{0,4},{1,5},{2,6},{3,7},{4,0},{5,1},{6,2},{7,3},{8,12},{9,13},{10,... | collective-permute-start | bytes 393224 | tf_op jit(solution)/shard_map/ppermute | solution.py:283
  12.8 0.0 collective-permute-done
  12.8 0.0 copy-done.3
  12.9 1.3 %collective-permute-start.1 = (bf16[2,2,32,1024]{3,2,1,0:T(8,128)(2,1)S(1)}, bf16[2,2,32,1024]{3,2,1,0:T(8,128)(2,1)S(1)}, u32[]{:S(2)}, u32[]{:S(2)}) collective-permute-start(bf16[2,2,32,1024]{3,2,1,0:T(8,128)(2,1)S(1)} %pad_maximum_fusion.1), channel_id=1, source_target_pairs={{0,2},{1,3},{2,0},{3,1},{4,6},{5,7},{6,4},{7,5},{8,10},{9,11},{10,... | collective-permute-start | bytes 786440 | tf_op jit(solution)/shard_map/ppermute | solution.py:283
  14.2 18.3 %collective-permute-done.4 = bf16[1,2,32,1024]{3,2,1,0:T(8,128)(2,1)S(1)} collective-permute-done((bf16[1,2,32,1024]{3,2,1,0:T(8,128)(2,1)S(1)}, bf16[1,2,32,1024]{3,2,1,0:T(8,128)(2,1)S(1)}, u32[]{:S(2)}, u32[]{:S(2)}) %collective-permute-start.4) | collective-permute-done | bytes 131104 | tf_op jit(solution)/shard_map/ppermute | solution.py:283
  32.5 0.0 copy-start.4
  32.5 1.3 %collective-permute-start.5 = (bf16[2,2,32,1024]{3,2,1,0:T(8,128)(2,1)S(1)}, bf16[2,2,32,1024]{3,2,1,0:T(8,128)(2,1)S(1)}, u32[]{:S(2)}, u32[]{:S(2)}) collective-permute-start(bf16[2,2,32,1024]{3,2,1,0:T(8,128)(2,1)S(1)} %pad_maximum_fusion.2), channel_id=1, source_target_pairs={{0,2},{1,3},{2,0},{3,1},{4,6},{5,7},{6,4},{7,5},{8,10},{9,11},{10,... | collective-permute-start | bytes 786440 | tf_op jit(solution)/shard_map/ppermute | solution.py:283
  33.8 0.0 collective-permute-done.1
  33.8 0.1 pad_maximum_fusion
  33.9 1.3 %collective-permute-start.2 = (bf16[4,32,1024]{2,1,0:T(8,128)(2,1)S(1)}, bf16[4,32,1024]{2,1,0:T(8,128)(2,1)S(1)}, u32[]{:S(2)}, u32[]{:S(2)}) collective-permute-start(bf16[4,32,1024]{2,1,0:T(8,128)(2,1)S(1)} %get-tuple-element.7), channel_id=1, source_target_pairs={{0,1},{1,0},{2,3},{3,2},{4,5},{5,4},{6,7},{7,6},{8,9},{9,8},{10,11... | collective-permute-start | bytes 786440 | tf_op jit(solution)/shard_map/ppermute | solution.py:283
  35.2 5.2 %collective-permute-done.5 = bf16[2,2,32,1024]{3,2,1,0:T(8,128)(2,1)S(1)} collective-permute-done((bf16[2,2,32,1024]{3,2,1,0:T(8,128)(2,1)S(1)}, bf16[2,2,32,1024]{3,2,1,0:T(8,128)(2,1)S(1)}, u32[]{:S(2)}, u32[]{:S(2)}) %collective-permute-start.5) | collective-permute-done | bytes 262176 | tf_op jit(solution)/shard_map/ppermute | solution.py:283
  40.5 1.4 %collective-permute-start.6 = (bf16[4,32,1024]{2,1,0:T(8,128)(2,1)S(1)}, bf16[4,32,1024]{2,1,0:T(8,128)(2,1)S(1)}, u32[]{:S(2)}, u32[]{:S(2)}) collective-permute-start(bf16[4,32,1024]{2,1,0:T(8,128)(2,1)S(1)} %get-tuple-element.5), channel_id=1, source_target_pairs={{0,1},{1,0},{2,3},{3,2},{4,5},{5,4},{6,7},{7,6},{8,9},{9,8},{10,11... | collective-permute-start | bytes 786440 | tf_op jit(solution)/shard_map/ppermute | solution.py:283
  41.9 0.0 copy-done.4
  41.9 0.1 pad_convert_fusion
  42.0 0.2 shard_map.73.rest_1_.rest_4_
  42.2 1.6 %shard_map.74.rest_2_.rest_5_ = bf16[1024,1024]{1,0:T(8,128)(2,1)S(1)} custom-call(bf16[1024,1024]{1,0:T(8,128)(2,1)} %constant.33.clone.source_ref), custom_call_target="tpu_custom_call" | custom-call | tf_op jit(solution)/shard_map/pallas_call | solution.py:83
  43.8 0.0 collective-permute-done.2.rest_1_
  43.8 0.0 collective-permute-done.6.rest_3_
  43.8 3.2 %shard_map.77.first_ref = bf16[16,32,1024]{2,1,0:T(8,128)(2,1)} custom-call(s32[1]{0:T(128)} %bitcast.3.index_ref, bf16[4,32,1024]{2,1,0:T(8,128)(2,1)S(1)} %get-tuple-element.8.rest_0_, bf16[4,32,1024]{2,1,0:T(8,128)(2,1)S(1)} %collective-permute-done.2.rest_1_, bf16[4,32,1024]{2,1,0:T(8,128)(2,1)S(1)} %get-tuple-element.6.rest_2_, ...), custom_call_target="tpu_custom_call" | custom-call | flops 1610612736 | bytes 2097152 | tf_op jit(solution)/shard_map/pallas_call | solution.py:133
  47.0 0.0 collective-permute-start.7
  47.0 0.0 all-to-all-done.rest_0_
  47.0 2.2 %shard_map.75.own_ref = bf16[16,32,1024]{2,1,0:T(8,128)(2,1)S(1)} custom-call(s32[1]{0:T(128)} %constant.29.clone.1.index_ref, bf16[16,32,1024]{2,1,0:T(8,128)(2,1)S(1)} %all-to-all-done.rest_0_, bf16[512,256]{1,0:T(8,128)(2,1)S(1)} %shard_map.73.rest_1_.rest_4_, bf16[1024,1024]{1,0:T(8,128)(2,1)S(1)} %shard_map.74.rest_2_.rest_5_), custom_call_target="tpu_custom_call" | custom-call | flops 1610612736 | bytes 2097152 | tf_op jit(solution)/shard_map/pallas_call | solution.py:133
  49.3 0.7 %collective-permute-done.7.second_ref = bf16[16,32,1024]{2,1,0:T(8,128)(2,1)} collective-permute-done((bf16[16,32,1024]{2,1,0:T(8,128)(2,1)}, bf16[16,32,1024]{2,1,0:T(8,128)(2,1)}, u32[]{:S(2)}, u32[]{:S(2)}) %collective-permute-start.7) | collective-permute-done | bytes 1048608 | tf_op jit(solution)/shard_map/ppermute | solution.py:283
  50.0 0.0 copy-done
  50.0 0.0 copy-done.1
  50.0 7.7 %shard_map.78 = f32[2,32,32,256]{3,2,1,0:T(8,128)} custom-call(s32[1]{0:T(128)} %bitcast.mine_ref, s32[2,32]{1,0:T(2,128)S(1)} %copy-done.1, s32[2,32,32]{2,1,0:T(8,128)S(1)} %copy-done, bf16[16,32,1024]{2,1,0:T(8,128)(2,1)S(1)} %shard_map.75.own_ref, bf16[16,32,1024]{2,1,0:T(8,128)(2,1)} %shard_map.77.first_ref, ...), custom_call_target="tpu_custom_call" | custom-call | flops 10000000000 | bytes 5242880 | tf_op jit(solution)/shard_map/pallas_call | solution.py:260
  (11 shorter events, 0.2 us)
Async XLA Ops:
  2.2 10.6 %copy-start.3 = (bf16[2,32,1024]{2,1,0:T(8,128)(2,1)S(1)}, bf16[2,32,1024]{2,1,0:T(8,128)(2,1)}, u32[]{:S(2)}) copy-start(bf16[2,32,1024]{2,1,0:T(8,128)(2,1)} %shard_map.76) | copy-start | bytes 393220
  2.2 8.3 %collective-permute-start.3 = (bf16[1,2,32,1024]{3,2,1,0:T(8,128)(2,1)}, bf16[1,2,32,1024]{3,2,1,0:T(8,128)(2,1)S(1)}, u32[]{:S(2)}, u32[]{:S(2)}) collective-permute-start(bf16[1,2,32,1024]{3,2,1,0:T(8,128)(2,1)} %bitcast.15), channel_id=1, source_target_pairs={{0,8},{1,9},{2,10},{3,11},{4,12},{5,13},{6,14},{7,15},{8,0},{9,1},... | collective-permute-start | bytes 393224 | tf_op jit(solution)/shard_map/ppermute | solution.py:283
  2.3 10.5 %collective-permute-start = (bf16[1,2,32,1024]{3,2,1,0:T(8,128)(2,1)}, bf16[1,2,32,1024]{3,2,1,0:T(8,128)(2,1)S(1)}, u32[]{:S(2)}, u32[]{:S(2)}) collective-permute-start(bf16[1,2,32,1024]{3,2,1,0:T(8,128)(2,1)} %bitcast.16), channel_id=1, source_target_pairs={{0,4},{1,5},{2,6},{3,7},{4,0},{5,1},{6,2},{7,3},{8,12},{9,13},{10,... | collective-permute-start | bytes 393224 | tf_op jit(solution)/shard_map/ppermute | solution.py:283
  3.7 43.4 %all-to-all-start = ((bf16[16,32,1024]{2,1,0:T(8,128)(2,1)}), bf16[16,32,1024]{2,1,0:T(8,128)(2,1)S(1)}, u32[]{:S(2)}, u32[]{:S(2)}) async-start(bf16[16,32,1024]{2,1,0:T(8,128)(2,1)} %bitcast.14), calls=%async_computation | async-start | bytes 2097152 | tf_op jit(solution)/shard_map/all_to_all | solution.py:311
  10.6 21.9 %collective-permute-start.4 = (bf16[1,2,32,1024]{3,2,1,0:T(8,128)(2,1)S(1)}, bf16[1,2,32,1024]{3,2,1,0:T(8,128)(2,1)S(1)}, u32[]{:S(2)}, u32[]{:S(2)}) collective-permute-start(bf16[1,2,32,1024]{3,2,1,0:T(8,128)(2,1)S(1)} %collective-permute-done.3), channel_id=1, source_target_pairs={{0,4},{1,5},{2,6},{3,7},{4,0},{5,1},{6,2},{7,3},{8,12},{9,13},{10,... | collective-permute-start | bytes 393224 | tf_op jit(solution)/shard_map/ppermute | solution.py:283
  12.9 20.9 %collective-permute-start.1 = (bf16[2,2,32,1024]{3,2,1,0:T(8,128)(2,1)S(1)}, bf16[2,2,32,1024]{3,2,1,0:T(8,128)(2,1)S(1)}, u32[]{:S(2)}, u32[]{:S(2)}) collective-permute-start(bf16[2,2,32,1024]{3,2,1,0:T(8,128)(2,1)S(1)} %pad_maximum_fusion.1), channel_id=1, source_target_pairs={{0,2},{1,3},{2,0},{3,1},{4,6},{5,7},{6,4},{7,5},{8,10},{9,11},{10,... | collective-permute-start | bytes 786440 | tf_op jit(solution)/shard_map/ppermute | solution.py:283
  32.5 9.4 %copy-start.4 = (bf16[129]{0:T(256)(128)(2,1)S(1)}, bf16[129]{0:T(256)(128)(2,1)}, u32[]{:S(2)}) copy-start(bf16[129]{0:T(256)(128)(2,1)} %param.8) | copy-start | bytes 778
  32.5 7.9 %collective-permute-start.5 = (bf16[2,2,32,1024]{3,2,1,0:T(8,128)(2,1)S(1)}, bf16[2,2,32,1024]{3,2,1,0:T(8,128)(2,1)S(1)}, u32[]{:S(2)}, u32[]{:S(2)}) collective-permute-start(bf16[2,2,32,1024]{3,2,1,0:T(8,128)(2,1)S(1)} %pad_maximum_fusion.2), channel_id=1, source_target_pairs={{0,2},{1,3},{2,0},{3,1},{4,6},{5,7},{6,4},{7,5},{8,10},{9,11},{10,... | collective-permute-start | bytes 786440 | tf_op jit(solution)/shard_map/ppermute | solution.py:283
  33.9 9.9 %collective-permute-start.2 = (bf16[4,32,1024]{2,1,0:T(8,128)(2,1)S(1)}, bf16[4,32,1024]{2,1,0:T(8,128)(2,1)S(1)}, u32[]{:S(2)}, u32[]{:S(2)}) collective-permute-start(bf16[4,32,1024]{2,1,0:T(8,128)(2,1)S(1)} %get-tuple-element.7), channel_id=1, source_target_pairs={{0,1},{1,0},{2,3},{3,2},{4,5},{5,4},{6,7},{7,6},{8,9},{9,8},{10,11... | collective-permute-start | bytes 786440 | tf_op jit(solution)/shard_map/ppermute | solution.py:283
  40.5 3.3 %collective-permute-start.6 = (bf16[4,32,1024]{2,1,0:T(8,128)(2,1)S(1)}, bf16[4,32,1024]{2,1,0:T(8,128)(2,1)S(1)}, u32[]{:S(2)}, u32[]{:S(2)}) collective-permute-start(bf16[4,32,1024]{2,1,0:T(8,128)(2,1)S(1)} %get-tuple-element.5), channel_id=1, source_target_pairs={{0,1},{1,0},{2,3},{3,2},{4,5},{5,4},{6,7},{7,6},{8,9},{9,8},{10,11... | collective-permute-start | bytes 786440 | tf_op jit(solution)/shard_map/ppermute | solution.py:283
  47.0 3.0 %copy-start = (s32[2,32,32]{2,1,0:T(8,128)S(1)}, s32[2,32,32]{2,1,0:T(8,128)}, u32[]{:S(2)}) copy-start(s32[2,32,32]{2,1,0:T(8,128)} %valid_ref.1) | copy-start | bytes 24580
  47.0 3.0 %copy-start.1 = (s32[2,32]{1,0:T(2,128)S(1)}, s32[2,32]{1,0:T(2,128)}, u32[]{:S(2)}) copy-start(s32[2,32]{1,0:T(2,128)} %order_ref.1) | copy-start | bytes 772
  47.0 3.0 %collective-permute-start.7 = (bf16[16,32,1024]{2,1,0:T(8,128)(2,1)}, bf16[16,32,1024]{2,1,0:T(8,128)(2,1)}, u32[]{:S(2)}, u32[]{:S(2)}) collective-permute-start(bf16[16,32,1024]{2,1,0:T(8,128)(2,1)} %shard_map.77.first_ref), channel_id=1, source_target_pairs={{0,1},{1,0},{2,3},{3,2},{4,5},{5,4},{6,7},{7,6},{8,9},{9,8},{10,11... | collective-permute-start | bytes 3145736 | tf_op jit(solution)/shard_map/ppermute | solution.py:283
  47.0 3.0 %copy-start.2 = (bf16[1024,256]{1,0:T(8,128)(2,1)S(1)}, bf16[1024,256]{1,0:T(8,128)(2,1)}, u32[]{:S(2)}) copy-start(bf16[1024,256]{1,0:T(8,128)(2,1)} %constant.34.clone.inverse_ref) | copy-start | bytes 1572868

commit v6 on v5

--- a/solution.py
+++ b/solution.py
@@ -292,9 +292,13 @@
 
     wanted = pick(ref_owner, records, stations)
     own_piece = wanted[None]
-    far_piece = swap(own_piece, axis, devices // 2)
-    chains = {"near": (own_piece, [0]), "far": (far_piece, [devices // 2])}
-    distance, stage = devices // 4, 0
+    quarter = devices // 4
+    crossed = [swap(own_piece, axis, j * quarter) for j in range(1, 4)]
+    chains = {
+        "near": (jnp.concatenate([own_piece, crossed[0]], axis=0), [0, quarter]),
+        "far": (jnp.concatenate(crossed[1:], axis=0), [2 * quarter, 3 * quarter]),
+    }
+    distance, stage = devices // 8, 0
     while distance > 1:
         for name, (block, offsets) in chains.items():
             block = jnp.concatenate([block, swap(block, axis, distance)], axis=0)

time: 58.1 us -> 54.4 us (0.936)
  the two profiles are of different devices: /device:TPU:17 before, /device:TPU:0 now
where the time goes in v6:
time: 54.4 us; the launch traced here: 54.1 us
  waiting for transfers between devices  22.6 us (42%)
  Pallas kernels  17.2 us (32%)
  starting transfers between devices  13.8 us (25%)
    ppermute x8, waiting for transfers between devices, swap(): return lax.ppermute(block, axis, [(i, i ^ distance) for i in range(count)])  22.6 us
    ppermute x8, starting transfers between devices, swap(): return lax.ppermute(block, axis, [(i, i ^ distance) for i in range(count)])  8.54 us
    pallas_call x1, Pallas kernels, correlate(): pl.pallas_call(functools.partial(correlate_body, group=group, unroll=64,...  7.71 us
    pallas_call x2, Pallas kernels, whiten(): pl.pallas_call(functools.partial(whiten_body, offsets=offsets, rows=rows)...  5.49 us
    all_to_all x1, starting transfers between devices, local(): lax.all_to_all(records.reshape(devices, stations, width), axis, split_axi...  5.26 us
    pallas_call x1, Pallas kernels, pick(): pl.pallas_call(pick_body, out_shape=jax.ShapeDtypeStruct((steps, stations...  2.21 us
    pallas_call x1, Pallas kernels, fetch(): pl.pallas_call(fetch_body, out_shape=jax.ShapeDtypeStruct(matrix.shape, m...  1.6 us
  transfers between devices with their start and end apart: 9, of which 4 were waited for; matrix products, arithmetic and copies ran while one was open for 1% of the time, Pallas kernels for 13%

profile of v6, /device:TPU:0, one launch (start us, length us, event | category | flops | bytes accessed | tf_op | source)
XLA Modules:
  0.0 54.1 jit_solution(3628159574512947154)
XLA Ops:
  0.0 2.2 %shard_map.76 = bf16[2,32,1024]{2,1,0:T(8,128)(2,1)} custom-call(s32[2]{0:T(128)} %owner_ref.1, bf16[512,1024]{1,0:T(8,128)(2,1)} %records_ref.1), custom_call_target="tpu_custom_call" | custom-call | tf_op jit(solution)/shard_map/pallas_call | solution.py:47
  2.2 0.0 copy-start.3
  2.2 3.1 %collective-permute-start = (bf16[1,2,32,1024]{3,2,1,0:T(8,128)(2,1)}, bf16[1,2,32,1024]{3,2,1,0:T(8,128)(2,1)S(1)}, u32[]{:S(2)}, u32[]{:S(2)}) collective-permute-start(bf16[1,2,32,1024]{3,2,1,0:T(8,128)(2,1)} %bitcast.15), channel_id=1, source_target_pairs={{0,4},{1,5},{2,6},{3,7},{4,0},{5,1},{6,2},{7,3},{8,12},{9,13},{10,... | collective-permute-start | bytes 393224 | tf_op jit(solution)/shard_map/ppermute | solution.py:283
  5.3 2.5 %collective-permute-start.4 = (bf16[1,2,32,1024]{3,2,1,0:T(8,128)(2,1)}, bf16[1,2,32,1024]{3,2,1,0:T(8,128)(2,1)S(1)}, u32[]{:S(2)}, u32[]{:S(2)}) collective-permute-start(bf16[1,2,32,1024]{3,2,1,0:T(8,128)(2,1)} %bitcast.16), channel_id=1, source_target_pairs={{0,12},{1,13},{2,14},{3,15},{4,8},{5,9},{6,10},{7,11},{8,4},{9,5},... | collective-permute-start | bytes 393224 | tf_op jit(solution)/shard_map/ppermute | solution.py:283
  7.8 0.1 collective-permute-start.3
  7.9 5.3 %all-to-all-start = ((bf16[16,32,1024]{2,1,0:T(8,128)(2,1)}), bf16[16,32,1024]{2,1,0:T(8,128)(2,1)S(1)}, u32[]{:S(2)}, u32[]{:S(2)}) async-start(bf16[16,32,1024]{2,1,0:T(8,128)(2,1)} %bitcast.14), calls=%async_computation | async-start | bytes 2097152 | tf_op jit(solution)/shard_map/all_to_all | solution.py:315
  13.2 0.0 collective-permute-done
  13.2 0.0 copy-done.3
  13.3 2.0 %collective-permute-start.1 = (bf16[2,2,32,1024]{3,2,1,0:T(8,128)(2,1)S(1)}, bf16[2,2,32,1024]{3,2,1,0:T(8,128)(2,1)S(1)}, u32[]{:S(2)}, u32[]{:S(2)}) collective-permute-start(bf16[2,2,32,1024]{3,2,1,0:T(8,128)(2,1)S(1)} %pad_maximum_fusion.1), channel_id=1, source_target_pairs={{0,2},{1,3},{2,0},{3,1},{4,6},{5,7},{6,4},{7,5},{8,10},{9,11},{10,... | collective-permute-start | bytes 786440 | tf_op jit(solution)/shard_map/ppermute | solution.py:283
  15.2 0.0 collective-permute-done.4
  15.3 11.7 %collective-permute-done.3 = bf16[1,2,32,1024]{3,2,1,0:T(8,128)(2,1)S(1)} collective-permute-done((bf16[1,2,32,1024]{3,2,1,0:T(8,128)(2,1)}, bf16[1,2,32,1024]{3,2,1,0:T(8,128)(2,1)S(1)}, u32[]{:S(2)}, u32[]{:S(2)}) %collective-permute-start.3) | collective-permute-done | bytes 131104 | tf_op jit(solution)/shard_map/ppermute | solution.py:283
  27.0 0.0 copy-start.4
  27.0 0.2 collective-permute-start.5
  27.2 3.1 %collective-permute-done.1 = bf16[2,2,32,1024]{3,2,1,0:T(8,128)(2,1)S(1)} collective-permute-done((bf16[2,2,32,1024]{3,2,1,0:T(8,128)(2,1)S(1)}, bf16[2,2,32,1024]{3,2,1,0:T(8,128)(2,1)S(1)}, u32[]{:S(2)}, u32[]{:S(2)}) %collective-permute-start.1) | collective-permute-done | bytes 262176 | tf_op jit(solution)/shard_map/ppermute | solution.py:283
  30.3 0.1 pad_maximum_fusion
  30.4 0.1 collective-permute-start.2
  30.5 7.5 %collective-permute-done.5 = bf16[2,2,32,1024]{3,2,1,0:T(8,128)(2,1)S(1)} collective-permute-done((bf16[2,2,32,1024]{3,2,1,0:T(8,128)(2,1)S(1)}, bf16[2,2,32,1024]{3,2,1,0:T(8,128)(2,1)S(1)}, u32[]{:S(2)}, u32[]{:S(2)}) %collective-permute-start.5) | collective-permute-done | bytes 262176 | tf_op jit(solution)/shard_map/ppermute | solution.py:283
  38.0 0.1 collective-permute-start.6
  38.1 0.0 copy-done.4
  38.1 0.1 pad_convert_fusion
  38.2 0.2 shard_map.73.rest_1_.rest_4_
  38.4 1.6 %shard_map.74.rest_2_.rest_5_ = bf16[1024,1024]{1,0:T(8,128)(2,1)S(1)} custom-call(bf16[1024,1024]{1,0:T(8,128)(2,1)} %constant.33.clone.source_ref), custom_call_target="tpu_custom_call" | custom-call | tf_op jit(solution)/shard_map/pallas_call | solution.py:83
  40.0 0.0 collective-permute-done.2.rest_1_
  40.0 0.0 collective-permute-done.6.rest_3_
  40.0 3.2 %shard_map.77.first_ref = bf16[16,32,1024]{2,1,0:T(8,128)(2,1)} custom-call(s32[1]{0:T(128)} %bitcast.3.index_ref, bf16[4,32,1024]{2,1,0:T(8,128)(2,1)S(1)} %get-tuple-element.8.rest_0_, bf16[4,32,1024]{2,1,0:T(8,128)(2,1)S(1)} %collective-permute-done.2.rest_1_, bf16[4,32,1024]{2,1,0:T(8,128)(2,1)S(1)} %get-tuple-element.6.rest_2_, ...), custom_call_target="tpu_custom_call" | custom-call | flops 1610612736 | bytes 2097152 | tf_op jit(solution)/shard_map/pallas_call | solution.py:133
  43.3 0.5 collective-permute-start.7
  43.7 0.0 all-to-all-done.rest_0_
  43.7 2.2 %shard_map.75.own_ref = bf16[16,32,1024]{2,1,0:T(8,128)(2,1)S(1)} custom-call(s32[1]{0:T(128)} %constant.29.clone.1.index_ref, bf16[16,32,1024]{2,1,0:T(8,128)(2,1)S(1)} %all-to-all-done.rest_0_, bf16[512,256]{1,0:T(8,128)(2,1)S(1)} %shard_map.73.rest_1_.rest_4_, bf16[1024,1024]{1,0:T(8,128)(2,1)S(1)} %shard_map.74.rest_2_.rest_5_), custom_call_target="tpu_custom_call" | custom-call | flops 1610612736 | bytes 2097152 | tf_op jit(solution)/shard_map/pallas_call | solution.py:133
  46.0 0.4 collective-permute-done.7.second_ref
  46.4 0.0 copy-done
  46.4 0.0 copy-done.2
  46.4 7.7 %shard_map.78 = f32[2,32,32,256]{3,2,1,0:T(8,128)} custom-call(s32[1]{0:T(128)} %bitcast.mine_ref, s32[2,32]{1,0:T(2,128)S(1)} %copy-done.1, s32[2,32,32]{2,1,0:T(8,128)S(1)} %copy-done, bf16[16,32,1024]{2,1,0:T(8,128)(2,1)S(1)} %shard_map.75.own_ref, bf16[16,32,1024]{2,1,0:T(8,128)(2,1)} %shard_map.77.first_ref, ...), custom_call_target="tpu_custom_call" | custom-call | flops 10000000000 | bytes 5242880 | tf_op jit(solution)/shard_map/pallas_call | solution.py:260
  (11 shorter events, 0.2 us)
Async XLA Ops:
  2.2 11.0 %copy-start.3 = (bf16[2,32,1024]{2,1,0:T(8,128)(2,1)S(1)}, bf16[2,32,1024]{2,1,0:T(8,128)(2,1)}, u32[]{:S(2)}) copy-start(bf16[2,32,1024]{2,1,0:T(8,128)(2,1)} %shard_map.76) | copy-start | bytes 393220
  2.2 11.0 %collective-permute-start = (bf16[1,2,32,1024]{3,2,1,0:T(8,128)(2,1)}, bf16[1,2,32,1024]{3,2,1,0:T(8,128)(2,1)S(1)}, u32[]{:S(2)}, u32[]{:S(2)}) collective-permute-start(bf16[1,2,32,1024]{3,2,1,0:T(8,128)(2,1)} %bitcast.15), channel_id=1, source_target_pairs={{0,4},{1,5},{2,6},{3,7},{4,0},{5,1},{6,2},{7,3},{8,12},{9,13},{10,... | collective-permute-start | bytes 393224 | tf_op jit(solution)/shard_map/ppermute | solution.py:283
  5.3 9.9 %collective-permute-start.4 = (bf16[1,2,32,1024]{3,2,1,0:T(8,128)(2,1)}, bf16[1,2,32,1024]{3,2,1,0:T(8,128)(2,1)S(1)}, u32[]{:S(2)}, u32[]{:S(2)}) collective-permute-start(bf16[1,2,32,1024]{3,2,1,0:T(8,128)(2,1)} %bitcast.16), channel_id=1, source_target_pairs={{0,12},{1,13},{2,14},{3,15},{4,8},{5,9},{6,10},{7,11},{8,4},{9,5},... | collective-permute-start | bytes 393224 | tf_op jit(solution)/shard_map/ppermute | solution.py:283
  7.8 19.1 %collective-permute-start.3 = (bf16[1,2,32,1024]{3,2,1,0:T(8,128)(2,1)}, bf16[1,2,32,1024]{3,2,1,0:T(8,128)(2,1)S(1)}, u32[]{:S(2)}, u32[]{:S(2)}) collective-permute-start(bf16[1,2,32,1024]{3,2,1,0:T(8,128)(2,1)} %bitcast.17), channel_id=1, source_target_pairs={{0,8},{1,9},{2,10},{3,11},{4,12},{5,13},{6,14},{7,15},{8,0},{9,1},... | collective-permute-start | bytes 393224 | tf_op jit(solution)/shard_map/ppermute | solution.py:283
  7.9 35.8 %all-to-all-start = ((bf16[16,32,1024]{2,1,0:T(8,128)(2,1)}), bf16[16,32,1024]{2,1,0:T(8,128)(2,1)S(1)}, u32[]{:S(2)}, u32[]{:S(2)}) async-start(bf16[16,32,1024]{2,1,0:T(8,128)(2,1)} %bitcast.14), calls=%async_computation | async-start | bytes 2097152 | tf_op jit(solution)/shard_map/all_to_all | solution.py:315
  13.3 17.0 %collective-permute-start.1 = (bf16[2,2,32,1024]{3,2,1,0:T(8,128)(2,1)S(1)}, bf16[2,2,32,1024]{3,2,1,0:T(8,128)(2,1)S(1)}, u32[]{:S(2)}, u32[]{:S(2)}) collective-permute-start(bf16[2,2,32,1024]{3,2,1,0:T(8,128)(2,1)S(1)} %pad_maximum_fusion.1), channel_id=1, source_target_pairs={{0,2},{1,3},{2,0},{3,1},{4,6},{5,7},{6,4},{7,5},{8,10},{9,11},{10,... | collective-permute-start | bytes 786440 | tf_op jit(solution)/shard_map/ppermute | solution.py:283
  27.0 11.1 %copy-start.4 = (bf16[129]{0:T(256)(128)(2,1)S(1)}, bf16[129]{0:T(256)(128)(2,1)}, u32[]{:S(2)}) copy-start(bf16[129]{0:T(256)(128)(2,1)} %param.8) | copy-start | bytes 778
  27.0 11.0 %collective-permute-start.5 = (bf16[2,2,32,1024]{3,2,1,0:T(8,128)(2,1)S(1)}, bf16[2,2,32,1024]{3,2,1,0:T(8,128)(2,1)S(1)}, u32[]{:S(2)}, u32[]{:S(2)}) collective-permute-start(bf16[2,2,32,1024]{3,2,1,0:T(8,128)(2,1)S(1)} %pad_maximum_fusion.2), channel_id=1, source_target_pairs={{0,2},{1,3},{2,0},{3,1},{4,6},{5,7},{6,4},{7,5},{8,10},{9,11},{10,... | collective-permute-start | bytes 786440 | tf_op jit(solution)/shard_map/ppermute | solution.py:283
  30.4 9.6 %collective-permute-start.2 = (bf16[4,32,1024]{2,1,0:T(8,128)(2,1)S(1)}, bf16[4,32,1024]{2,1,0:T(8,128)(2,1)S(1)}, u32[]{:S(2)}, u32[]{:S(2)}) collective-permute-start(bf16[4,32,1024]{2,1,0:T(8,128)(2,1)S(1)} %get-tuple-element.7), channel_id=1, source_target_pairs={{0,1},{1,0},{2,3},{3,2},{4,5},{5,4},{6,7},{7,6},{8,9},{9,8},{10,11... | collective-permute-start | bytes 786440 | tf_op jit(solution)/shard_map/ppermute | solution.py:283
  38.0 2.0 %collective-permute-start.6 = (bf16[4,32,1024]{2,1,0:T(8,128)(2,1)S(1)}, bf16[4,32,1024]{2,1,0:T(8,128)(2,1)S(1)}, u32[]{:S(2)}, u32[]{:S(2)}) collective-permute-start(bf16[4,32,1024]{2,1,0:T(8,128)(2,1)S(1)} %get-tuple-element.5), channel_id=1, source_target_pairs={{0,1},{1,0},{2,3},{3,2},{4,5},{5,4},{6,7},{7,6},{8,9},{9,8},{10,11... | collective-permute-start | bytes 786440 | tf_op jit(solution)/shard_map/ppermute | solution.py:283
  43.3 3.1 %copy-start = (s32[2,32,32]{2,1,0:T(8,128)S(1)}, s32[2,32,32]{2,1,0:T(8,128)}, u32[]{:S(2)}) copy-start(s32[2,32,32]{2,1,0:T(8,128)} %valid_ref.1) | copy-start | bytes 24580
  43.3 3.1 %copy-start.1 = (s32[2,32]{1,0:T(2,128)S(1)}, s32[2,32]{1,0:T(2,128)}, u32[]{:S(2)}) copy-start(s32[2,32]{1,0:T(2,128)} %order_ref.1) | copy-start | bytes 772
  43.3 3.1 %collective-permute-start.7 = (bf16[16,32,1024]{2,1,0:T(8,128)(2,1)}, bf16[16,32,1024]{2,1,0:T(8,128)(2,1)}, u32[]{:S(2)}, u32[]{:S(2)}) collective-permute-start(bf16[16,32,1024]{2,1,0:T(8,128)(2,1)} %shard_map.77.first_ref), channel_id=1, source_target_pairs={{0,1},{1,0},{2,3},{3,2},{4,5},{5,4},{6,7},{7,6},{8,9},{9,8},{10,11... | collective-permute-start | bytes 3145736 | tf_op jit(solution)/shard_map/ppermute | solution.py:283
  43.7 2.6 %copy-start.2 = (bf16[1024,256]{1,0:T(8,128)(2,1)S(1)}, bf16[1024,256]{1,0:T(8,128)(2,1)}, u32[]{:S(2)}) copy-start(bf16[1024,256]{1,0:T(8,128)(2,1)} %constant.34.clone.inverse_ref) | copy-start | bytes 1572868

commit v7 on v6

--- a/solution.py
+++ b/solution.py
@@ -293,10 +293,17 @@
     wanted = pick(ref_owner, records, stations)
     own_piece = wanted[None]
     quarter = devices // 4
-    crossed = [swap(own_piece, axis, j * quarter) for j in range(1, 4)]
+    quarter_of = lambda source, target: [(source * quarter + i, target * quarter + i) for i in range(quarter)]
+    beside = swap(own_piece, axis, quarter)
+    inner = lax.ppermute(own_piece, axis, quarter_of(1, 2) + quarter_of(2, 1))
+    outer = lax.ppermute(own_piece, axis, quarter_of(0, 2) + quarter_of(3, 1))
+    both = jnp.concatenate([inner, outer], axis=0)
+    relayed = lax.ppermute(both, axis, quarter_of(1, 0) + quarter_of(2, 3))
+    place = index // quarter
+    far_block = jnp.where((place == 1) | (place == 2), both, relayed[::-1])
     chains = {
-        "near": (jnp.concatenate([own_piece, crossed[0]], axis=0), [0, quarter]),
-        "far": (jnp.concatenate(crossed[1:], axis=0), [2 * quarter, 3 * quarter]),
+        "near": (jnp.concatenate([own_piece, beside], axis=0), [0, quarter]),
+        "far": (far_block, [3 * quarter, 2 * quarter]),
     }
     distance, stage = devices // 8, 0
     while distance > 1:

time: 54.4 us -> 64.3 us (1.18)
  starting transfers between devices: 13.8 us -> 19.7 us
  waiting for transfers between devices: 22.6 us -> 26.5 us
    ppermute x0 -> x3, starting transfers between devices: none -> 9.76 us  [the longest x1 7.66 us: local(): outer = lax.ppermute(own_piece, axis, quarter_of(0, 2) + quarter_of(3, 1))]
    ppermute x8 -> x6, starting transfers between devices: 8.54 us -> 3.92 us  [swap(): return lax.ppermute(block, axis, [(i, i ^ distance) for i in range(count)])]
    ppermute x0 -> x3, waiting for transfers between devices: none -> 4.07 us  [the longest x1 4.06 us: local(): outer = lax.ppermute(own_piece, axis, quarter_of(0, 2) + quarter_of(3, 1))]
    all_to_all x1, starting transfers between devices: 5.26 us -> 6.02 us  [local(): lax.all_to_all(records.reshape(devices, stations, width), axis, split_axi...]
    ppermute x8 -> x6, waiting for transfers between devices: 22.6 us -> 22.4 us  [swap(): return lax.ppermute(block, axis, [(i, i ^ distance) for i in range(count)])]
  transfers between devices with their start and end apart: 9 -> 10, of which waited for: 4 -> 4; matrix products, arithmetic and copies ran while one was open for 1% -> 1% of each run, Pallas kernels for 13% -> 11%
where the time goes in v7:
time: 64.3 us; the launch traced here: 63.9 us
  waiting for transfers between devices  26.5 us (41%)
  starting transfers between devices  19.7 us (31%)
  Pallas kernels  17.2 us (27%)
    ppermute x6, waiting for transfers between devices, swap(): return lax.ppermute(block, axis, [(i, i ^ distance) for i in range(count)])  22.4 us
    pallas_call x1, Pallas kernels, correlate(): pl.pallas_call(functools.partial(correlate_body, group=group, unroll=64,...  7.71 us
    ppermute x1, starting transfers between devices, local(): outer = lax.ppermute(own_piece, axis, quarter_of(0, 2) + quarter_of(3, 1))  7.66 us
    all_to_all x1, starting transfers between devices, local(): lax.all_to_all(records.reshape(devices, stations, width), axis, split_axi...  6.02 us
    pallas_call x2, Pallas kernels, whiten(): pl.pallas_call(functools.partial(whiten_body, offsets=offsets, rows=rows)...  5.48 us
    ppermute x1, waiting for transfers between devices, local(): outer = lax.ppermute(own_piece, axis, quarter_of(0, 2) + quarter_of(3, 1))  4.06 us
    ppermute x6, starting transfers between devices, swap(): return lax.ppermute(block, axis, [(i, i ^ distance) for i in range(count)])  3.92 us
    pallas_call x1, Pallas kernels, pick(): pl.pallas_call(pick_body, out_shape=jax.ShapeDtypeStruct((steps, stations...  2.21 us
  transfers between devices with their start and end apart: 10, of which 4 were waited for; matrix products, arithmetic and copies ran while one was open for 1% of the time, Pallas kernels for 11%

profile of v7, /device:TPU:0, one launch (start us, length us, event | category | flops | bytes accessed | tf_op | source)
XLA Modules:
  0.0 63.9 jit_solution(9334410389432001454)
XLA Ops:
  0.0 2.2 %shard_map.76 = bf16[2,32,1024]{2,1,0:T(8,128)(2,1)} custom-call(s32[2]{0:T(128)} %owner_ref.1, bf16[512,1024]{1,0:T(8,128)(2,1)} %records_ref.1), custom_call_target="tpu_custom_call" | custom-call | tf_op jit(solution)/shard_map/pallas_call | solution.py:47
  2.2 0.0 copy-start.3
  2.2 0.8 %collective-permute-start.3 = (bf16[1,2,32,1024]{3,2,1,0:T(8,128)(2,1)}, bf16[1,2,32,1024]{3,2,1,0:T(8,128)(2,1)S(1)}, u32[]{:S(2)}, u32[]{:S(2)}) collective-permute-start(bf16[1,2,32,1024]{3,2,1,0:T(8,128)(2,1)} %bitcast.15), channel_id=1, source_target_pairs={{4,8},{5,9},{6,10},{7,11},{8,4},{9,5},{10,6},{11,7},{20,24},{21,25... | collective-permute-start | bytes 393224 | tf_op jit(solution)/shard_map/ppermute | solution.py:298
  3.0 7.7 %collective-permute-start.4 = (bf16[1,2,32,1024]{3,2,1,0:T(8,128)(2,1)}, bf16[1,2,32,1024]{3,2,1,0:T(8,128)(2,1)S(1)}, u32[]{:S(2)}, u32[]{:S(2)}) collective-permute-start(bf16[1,2,32,1024]{3,2,1,0:T(8,128)(2,1)} %bitcast.16), channel_id=1, source_target_pairs={{0,8},{1,9},{2,10},{3,11},{12,4},{13,5},{14,6},{15,7},{16,24},{17,... | collective-permute-start | bytes 393224 | tf_op jit(solution)/shard_map/ppermute | solution.py:299
  10.7 0.1 collective-permute-start
  10.8 0.0 collective-permute-done.3
  10.8 4.1 %collective-permute-done.4 = bf16[1,2,32,1024]{3,2,1,0:T(8,128)(2,1)S(1)} collective-permute-done((bf16[1,2,32,1024]{3,2,1,0:T(8,128)(2,1)}, bf16[1,2,32,1024]{3,2,1,0:T(8,128)(2,1)S(1)}, u32[]{:S(2)}, u32[]{:S(2)}) %collective-permute-start.4) | collective-permute-done | bytes 131104 | tf_op jit(solution)/shard_map/ppermute | solution.py:299
  14.9 1.3 %collective-permute-start.5 = (bf16[2,2,32,1024]{3,2,1,0:T(8,128)(2,1)S(1)}, bf16[2,2,32,1024]{3,2,1,0:T(8,128)(2,1)S(1)}, u32[]{:S(2)}, u32[]{:S(2)}) collective-permute-start(bf16[2,2,32,1024]{3,2,1,0:T(8,128)(2,1)S(1)} %constant_dynamic-update-slice_fusion), channel_id=1, source_target_pairs={{4,0},{5,1},{6,2},{7,3},{8,12},{9,13},{10,14},{11,15},{20,16},{21,... | collective-permute-start | bytes 786440 | tf_op jit(solution)/shard_map/ppermute | solution.py:301
  16.2 6.0 %all-to-all-start = ((bf16[16,32,1024]{2,1,0:T(8,128)(2,1)}), bf16[16,32,1024]{2,1,0:T(8,128)(2,1)S(1)}, u32[]{:S(2)}, u32[]{:S(2)}) async-start(bf16[16,32,1024]{2,1,0:T(8,128)(2,1)} %bitcast.14), calls=%async_computation | async-start | bytes 2097152 | tf_op jit(solution)/shard_map/all_to_all | solution.py:322
  22.2 0.0 collective-permute-done
  22.3 0.0 copy-start.4
  22.3 2.0 %collective-permute-start.1 = (bf16[2,2,32,1024]{3,2,1,0:T(8,128)(2,1)S(1)}, bf16[2,2,32,1024]{3,2,1,0:T(8,128)(2,1)S(1)}, u32[]{:S(2)}, u32[]{:S(2)}) collective-permute-start(bf16[2,2,32,1024]{3,2,1,0:T(8,128)(2,1)S(1)} %pad_maximum_fusion.1), channel_id=1, source_target_pairs={{0,2},{1,3},{2,0},{3,1},{4,6},{5,7},{6,4},{7,5},{8,10},{9,11},{10,... | collective-permute-start | bytes 786440 | tf_op jit(solution)/shard_map/ppermute | solution.py:283
  24.3 0.0 collective-permute-done.5
  24.3 0.1 reverse_select_fusion
  24.3 1.2 %collective-permute-start.6 = (bf16[2,2,32,1024]{3,2,1,0:T(8,128)(2,1)S(1)}, bf16[2,2,32,1024]{3,2,1,0:T(8,128)(2,1)S(1)}, u32[]{:S(2)}, u32[]{:S(2)}) collective-permute-start(bf16[2,2,32,1024]{3,2,1,0:T(8,128)(2,1)S(1)} %reverse_select_fusion), channel_id=1, source_target_pairs={{0,2},{1,3},{2,0},{3,1},{4,6},{5,7},{6,4},{7,5},{8,10},{9,11},{10,... | collective-permute-start | bytes 786440 | tf_op jit(solution)/shard_map/ppermute | solution.py:283
  25.6 14.4 %collective-permute-done.1 = bf16[2,2,32,1024]{3,2,1,0:T(8,128)(2,1)S(1)} collective-permute-done((bf16[2,2,32,1024]{3,2,1,0:T(8,128)(2,1)S(1)}, bf16[2,2,32,1024]{3,2,1,0:T(8,128)(2,1)S(1)}, u32[]{:S(2)}, u32[]{:S(2)}) %collective-permute-start.1) | collective-permute-done | bytes 262176 | tf_op jit(solution)/shard_map/ppermute | solution.py:283
  39.9 0.1 pad_maximum_fusion
  40.0 0.1 collective-permute-start.2
  40.1 7.7 %collective-permute-done.6 = bf16[2,2,32,1024]{3,2,1,0:T(8,128)(2,1)S(1)} collective-permute-done((bf16[2,2,32,1024]{3,2,1,0:T(8,128)(2,1)S(1)}, bf16[2,2,32,1024]{3,2,1,0:T(8,128)(2,1)S(1)}, u32[]{:S(2)}, u32[]{:S(2)}) %collective-permute-start.6) | collective-permute-done | bytes 262176 | tf_op jit(solution)/shard_map/ppermute | solution.py:283
  47.8 0.1 collective-permute-start.7
  47.9 0.1 pad_convert_fusion
  48.0 0.2 shard_map.73.rest_1_.rest_4_
  48.2 1.6 %shard_map.74.rest_2_.rest_5_ = bf16[1024,1024]{1,0:T(8,128)(2,1)S(1)} custom-call(bf16[1024,1024]{1,0:T(8,128)(2,1)} %constant.45.clone.source_ref), custom_call_target="tpu_custom_call" | custom-call | tf_op jit(solution)/shard_map/pallas_call | solution.py:83
  49.8 0.0 collective-permute-done.2.rest_1_
  49.8 0.0 collective-permute-done.7.rest_3_
  49.8 3.2 %shard_map.77.first_ref = bf16[16,32,1024]{2,1,0:T(8,128)(2,1)} custom-call(s32[1]{0:T(128)} %bitcast.3.index_ref, bf16[4,32,1024]{2,1,0:T(8,128)(2,1)S(1)} %get-tuple-element.8.rest_0_, bf16[4,32,1024]{2,1,0:T(8,128)(2,1)S(1)} %collective-permute-done.2.rest_1_, bf16[4,32,1024]{2,1,0:T(8,128)(2,1)S(1)} %get-tuple-element.6.rest_2_, ...), custom_call_target="tpu_custom_call" | custom-call | flops 1610612736 | bytes 2097152 | tf_op jit(solution)/shard_map/pallas_call | solution.py:133
  53.1 0.5 collective-permute-start.8
  53.6 0.0 all-to-all-done.rest_0_
  53.6 2.2 %shard_map.75.own_ref = bf16[16,32,1024]{2,1,0:T(8,128)(2,1)S(1)} custom-call(s32[1]{0:T(128)} %constant.40.clone.1.index_ref, bf16[16,32,1024]{2,1,0:T(8,128)(2,1)S(1)} %all-to-all-done.rest_0_, bf16[512,256]{1,0:T(8,128)(2,1)S(1)} %shard_map.73.rest_1_.rest_4_, bf16[1024,1024]{1,0:T(8,128)(2,1)S(1)} %shard_map.74.rest_2_.rest_5_), custom_call_target="tpu_custom_call" | custom-call | flops 1610612736 | bytes 2097152 | tf_op jit(solution)/shard_map/pallas_call | solution.py:133
  55.8 0.4 collective-permute-done.8.second_ref
  56.2 0.0 copy-done
  56.2 7.7 %shard_map.78 = f32[2,32,32,256]{3,2,1,0:T(8,128)} custom-call(s32[1]{0:T(128)} %bitcast.mine_ref, s32[2,32]{1,0:T(2,128)S(1)} %copy-done.1, s32[2,32,32]{2,1,0:T(8,128)S(1)} %copy-done, bf16[16,32,1024]{2,1,0:T(8,128)(2,1)S(1)} %shard_map.75.own_ref, bf16[16,32,1024]{2,1,0:T(8,128)(2,1)} %shard_map.77.first_ref, ...), custom_call_target="tpu_custom_call" | custom-call | flops 10000000000 | bytes 5242880 | tf_op jit(solution)/shard_map/pallas_call | solution.py:260
  (12 shorter events, 0.2 us)
Async XLA Ops:
  2.2 20.0 %copy-start.3 = (bf16[2,32,1024]{2,1,0:T(8,128)(2,1)S(1)}, bf16[2,32,1024]{2,1,0:T(8,128)(2,1)}, u32[]{:S(2)}) copy-start(bf16[2,32,1024]{2,1,0:T(8,128)(2,1)} %shard_map.76) | copy-start | bytes 393220
  2.2 8.6 %collective-permute-start.3 = (bf16[1,2,32,1024]{3,2,1,0:T(8,128)(2,1)}, bf16[1,2,32,1024]{3,2,1,0:T(8,128)(2,1)S(1)}, u32[]{:S(2)}, u32[]{:S(2)}) collective-permute-start(bf16[1,2,32,1024]{3,2,1,0:T(8,128)(2,1)} %bitcast.15), channel_id=1, source_target_pairs={{4,8},{5,9},{6,10},{7,11},{8,4},{9,5},{10,6},{11,7},{20,24},{21,25... | collective-permute-start | bytes 393224 | tf_op jit(solution)/shard_map/ppermute | solution.py:298
  3.0 11.8 %collective-permute-start.4 = (bf16[1,2,32,1024]{3,2,1,0:T(8,128)(2,1)}, bf16[1,2,32,1024]{3,2,1,0:T(8,128)(2,1)S(1)}, u32[]{:S(2)}, u32[]{:S(2)}) collective-permute-start(bf16[1,2,32,1024]{3,2,1,0:T(8,128)(2,1)} %bitcast.16), channel_id=1, source_target_pairs={{0,8},{1,9},{2,10},{3,11},{12,4},{13,5},{14,6},{15,7},{16,24},{17,... | collective-permute-start | bytes 393224 | tf_op jit(solution)/shard_map/ppermute | solution.py:299
  10.7 11.5 %collective-permute-start = (bf16[1,2,32,1024]{3,2,1,0:T(8,128)(2,1)}, bf16[1,2,32,1024]{3,2,1,0:T(8,128)(2,1)S(1)}, u32[]{:S(2)}, u32[]{:S(2)}) collective-permute-start(bf16[1,2,32,1024]{3,2,1,0:T(8,128)(2,1)} %bitcast.17), channel_id=1, source_target_pairs={{0,4},{1,5},{2,6},{3,7},{4,0},{5,1},{6,2},{7,3},{8,12},{9,13},{10,... | collective-permute-start | bytes 393224 | tf_op jit(solution)/shard_map/ppermute | solution.py:283
  14.9 9.4 %collective-permute-start.5 = (bf16[2,2,32,1024]{3,2,1,0:T(8,128)(2,1)S(1)}, bf16[2,2,32,1024]{3,2,1,0:T(8,128)(2,1)S(1)}, u32[]{:S(2)}, u32[]{:S(2)}) collective-permute-start(bf16[2,2,32,1024]{3,2,1,0:T(8,128)(2,1)S(1)} %constant_dynamic-update-slice_fusion), channel_id=1, source_target_pairs={{4,0},{5,1},{6,2},{7,3},{8,12},{9,13},{10,14},{11,15},{20,16},{21,... | collective-permute-start | bytes 786440 | tf_op jit(solution)/shard_map/ppermute | solution.py:301
  16.2 37.4 %all-to-all-start = ((bf16[16,32,1024]{2,1,0:T(8,128)(2,1)}), bf16[16,32,1024]{2,1,0:T(8,128)(2,1)S(1)}, u32[]{:S(2)}, u32[]{:S(2)}) async-start(bf16[16,32,1024]{2,1,0:T(8,128)(2,1)} %bitcast.14), calls=%async_computation | async-start | bytes 2097152 | tf_op jit(solution)/shard_map/all_to_all | solution.py:322
  22.3 25.6 %copy-start.4 = (bf16[129]{0:T(256)(128)(2,1)S(1)}, bf16[129]{0:T(256)(128)(2,1)}, u32[]{:S(2)}) copy-start(bf16[129]{0:T(256)(128)(2,1)} %param.8) | copy-start | bytes 778
  22.3 17.6 %collective-permute-start.1 = (bf16[2,2,32,1024]{3,2,1,0:T(8,128)(2,1)S(1)}, bf16[2,2,32,1024]{3,2,1,0:T(8,128)(2,1)S(1)}, u32[]{:S(2)}, u32[]{:S(2)}) collective-permute-start(bf16[2,2,32,1024]{3,2,1,0:T(8,128)(2,1)S(1)} %pad_maximum_fusion.1), channel_id=1, source_target_pairs={{0,2},{1,3},{2,0},{3,1},{4,6},{5,7},{6,4},{7,5},{8,10},{9,11},{10,... | collective-permute-start | bytes 786440 | tf_op jit(solution)/shard_map/ppermute | solution.py:283
  24.3 23.4 %collective-permute-start.6 = (bf16[2,2,32,1024]{3,2,1,0:T(8,128)(2,1)S(1)}, bf16[2,2,32,1024]{3,2,1,0:T(8,128)(2,1)S(1)}, u32[]{:S(2)}, u32[]{:S(2)}) collective-permute-start(bf16[2,2,32,1024]{3,2,1,0:T(8,128)(2,1)S(1)} %reverse_select_fusion), channel_id=1, source_target_pairs={{0,2},{1,3},{2,0},{3,1},{4,6},{5,7},{6,4},{7,5},{8,10},{9,11},{10,... | collective-permute-start | bytes 786440 | tf_op jit(solution)/shard_map/ppermute | solution.py:283
  40.0 9.8 %collective-permute-start.2 = (bf16[4,32,1024]{2,1,0:T(8,128)(2,1)S(1)}, bf16[4,32,1024]{2,1,0:T(8,128)(2,1)S(1)}, u32[]{:S(2)}, u32[]{:S(2)}) collective-permute-start(bf16[4,32,1024]{2,1,0:T(8,128)(2,1)S(1)} %get-tuple-element.7), channel_id=1, source_target_pairs={{0,1},{1,0},{2,3},{3,2},{4,5},{5,4},{6,7},{7,6},{8,9},{9,8},{10,11... | collective-permute-start | bytes 786440 | tf_op jit(solution)/shard_map/ppermute | solution.py:283
  47.8 2.0 %collective-permute-start.7 = (bf16[4,32,1024]{2,1,0:T(8,128)(2,1)S(1)}, bf16[4,32,1024]{2,1,0:T(8,128)(2,1)S(1)}, u32[]{:S(2)}, u32[]{:S(2)}) collective-permute-start(bf16[4,32,1024]{2,1,0:T(8,128)(2,1)S(1)} %get-tuple-element.5), channel_id=1, source_target_pairs={{0,1},{1,0},{2,3},{3,2},{4,5},{5,4},{6,7},{7,6},{8,9},{9,8},{10,11... | collective-permute-start | bytes 786440 | tf_op jit(solution)/shard_map/ppermute | solution.py:283
  53.1 3.1 %copy-start = (s32[2,32,32]{2,1,0:T(8,128)S(1)}, s32[2,32,32]{2,1,0:T(8,128)}, u32[]{:S(2)}) copy-start(s32[2,32,32]{2,1,0:T(8,128)} %valid_ref.1) | copy-start | bytes 24580
  53.1 3.1 %copy-start.1 = (s32[2,32]{1,0:T(2,128)S(1)}, s32[2,32]{1,0:T(2,128)}, u32[]{:S(2)}) copy-start(s32[2,32]{1,0:T(2,128)} %order_ref.1) | copy-start | bytes 772
  53.1 3.1 %collective-permute-start.8 = (bf16[16,32,1024]{2,1,0:T(8,128)(2,1)}, bf16[16,32,1024]{2,1,0:T(8,128)(2,1)}, u32[]{:S(2)}, u32[]{:S(2)}) collective-permute-start(bf16[16,32,1024]{2,1,0:T(8,128)(2,1)} %shard_map.77.first_ref), channel_id=1, source_target_pairs={{0,1},{1,0},{2,3},{3,2},{4,5},{5,4},{6,7},{7,6},{8,9},{9,8},{10,11... | collective-permute-start | bytes 3145736 | tf_op jit(solution)/shard_map/ppermute | solution.py:283
  53.6 2.6 %copy-start.2 = (bf16[1024,256]{1,0:T(8,128)(2,1)S(1)}, bf16[1024,256]{1,0:T(8,128)(2,1)}, u32[]{:S(2)}) copy-start(bf16[1024,256]{1,0:T(8,128)(2,1)} %constant.46.clone.inverse_ref) | copy-start | bytes 1572868

commit v8 on v6

--- a/solution.py
+++ b/solution.py
@@ -11,6 +11,7 @@
 
 
 NFFT = 1024
+PIECE = 8
 LAGS = 256
 LANES = 128
 
@@ -50,7 +51,7 @@
         in_specs=[pl.BlockSpec(memory_space=pltpu.SMEM), pl.BlockSpec(memory_space=pltpu.HBM)],
         out_specs=pl.BlockSpec(memory_space=pltpu.VMEM),
         scratch_shapes=[pltpu.SemaphoreType.DMA((steps,))],
-        compiler_params=pltpu.CompilerParams(vmem_limit_bytes=60 * 2**20),
+        compiler_params=pltpu.CompilerParams(vmem_limit_bytes=53 * 2**20),
     )(owner, records)
 
 
@@ -149,7 +150,7 @@
 
 
 def correlate_body(
-    mine_ref, order_ref, valid_ref, own_ref, first_ref, second_ref, inverse_ref, out_ref, *rest, group, unroll, pitch
+    mine_ref, order_ref, valid_ref, own_ref, first_ref, second_ref, inverse_ref, out_ref, *rest, group, piece, unroll, pitch
 ):
     paired, products, cross, ready, sems = rest
     segments, stations, width = own_ref.shape
@@ -176,7 +177,7 @@
                 paired[where, :] = stack.T.astype(jnp.float32)
         return 0
 
-    lax.fori_loop(0, segments, arrange, 0, unroll=4)
+    lax.fori_loop(0, segments, arrange, 0, unroll=8)
     low = lax.broadcasted_iota(jnp.int32, (depth, LANES), 1) < half
     column = lax.broadcasted_iota(jnp.int32, (count, tiles * depth), 1)
     even = lax.rem(lax.div(column, depth), 2) == 0
@@ -208,10 +209,11 @@
     def place(n):
         return lax.div(n, block // group), pl.multiple_of(lax.rem(n, block // group) * group, group)
 
-    def send(n):
+    def send(n, part):
         step, start = place(n)
-        slot = lax.rem(n, 2)
-        return pltpu.make_async_copy(ready.at[slot], out_ref.at[step, pl.ds(start, group)], sems.at[slot])
+        rows = pl.ds(part * piece, piece)
+        where = out_ref.at[step, pl.ds(pl.multiple_of(start + part * piece, piece), piece)]
+        return pltpu.make_async_copy(ready.at[n, rows], where, sems.at[n, part])
 
     def finish(n, _):
         step, start = place(n)
@@ -224,25 +226,26 @@
                         at = (2 * tile + part) * stations
                         lane = part * bins + (2 * h + tile) * LANES
                         cross[j * stations : (j + 1) * stations, lane : lane + LANES] = turned[at : at + stations]
-        lagged = jnp.dot(cross[...], inverse_ref[...], preferred_element_type=jnp.float32)
         valid = valid_ref[step, pl.ds(start, group), :].astype(jnp.float32)
-
-        @pl.when(n >= 2)
-        def _():
-            send(n - 2).wait()
-
-        slot = lax.rem(n, 2)
-        for j in range(group):
-            kept = jnp.sum(
-                jnp.where(diagonal, jnp.broadcast_to(valid[j : j + 1], square), 0.0), axis=1, keepdims=True
+        for part in range(group // piece):
+            lagged = jnp.dot(
+                cross[part * piece * stations : (part + 1) * piece * stations],
+                inverse_ref[...],
+                preferred_element_type=jnp.float32,
             )
-            ready[slot, j] = lagged[j * stations : (j + 1) * stations] * kept
-        send(n).start()
+            for i in range(piece):
+                j = part * piece + i
+                kept = jnp.sum(
+                    jnp.where(diagonal, jnp.broadcast_to(valid[j : j + 1], square), 0.0), axis=1, keepdims=True
+                )
+                ready[n, j] = lagged[i * stations : (i + 1) * stations] * kept
+            send(n, part).start()
         return 0
 
     lax.fori_loop(0, turns, finish, 0)
-    for n in range(max(turns - 2, 0), turns):
-        send(n).wait()
+    for n in range(turns):
+        for part in range(group // piece):
+            send(n, part).wait()
 
 
 def correlate(mine, order, valid, own, first, second, inverse):
@@ -258,7 +261,7 @@
     pitch = (near, near * depth + 1), (near_out, near_out * count + 1)
     vmem, smem = pl.BlockSpec(memory_space=pltpu.VMEM), pl.BlockSpec(memory_space=pltpu.SMEM)
     return pl.pallas_call(
-        functools.partial(correlate_body, group=group, unroll=64, pitch=pitch),
+        functools.partial(correlate_body, group=group, piece=PIECE, unroll=64, pitch=pitch),
         out_shape=jax.ShapeDtypeStruct((steps, block, stations, lags), jnp.float32),
         in_specs=[smem] * 2 + [vmem] * 5,
         out_specs=pl.BlockSpec(memory_space=pl.ANY),
@@ -266,8 +269,8 @@
             pltpu.VMEM((LANES * pitch[0][1], LANES), jnp.float32),
             pltpu.VMEM((LANES * pitch[1][1], LANES), jnp.float32),
             pltpu.VMEM((group * stations, width), jnp.bfloat16),
-            pltpu.VMEM((2, group, stations, lags), jnp.float32),
-            pltpu.SemaphoreType.DMA((2,)),
+            pltpu.VMEM((count // group, group, stations, lags), jnp.float32),
+            pltpu.SemaphoreType.DMA((count // group, group // PIECE)),
         ],
         compiler_params=pltpu.CompilerParams(vmem_limit_bytes=33 * 2**20),
         cost_estimate=pl.CostEstimate(

time: 54.4 us -> 53.8 us (0.989)
  Pallas kernels: 17.2 us -> 15.9 us
  local copies, waits for them, and re-layouts: 0.15 us -> 0.8 us
    pallas_call x1, Pallas kernels: 2.21 us -> 1.43 us  [pick(): pl.pallas_call(pick_body, out_shape=jax.ShapeDtypeStruct((steps, stations...]
    unnamed x12, local copies, waits for them, and re-layouts: 0.04 us -> 0.69 us
  transfers between devices with their start and end apart: 9 -> 9, of which waited for: 4 -> 4; matrix products, arithmetic and copies ran while one was open for 1% -> 1% of each run, Pallas kernels for 13% -> 14%
where the time goes in v8:
time: 53.8 us; the launch traced here: 53.5 us
  waiting for transfers between devices  22.7 us (42%)
  Pallas kernels  15.9 us (30%)
  starting transfers between devices  13.8 us (26%)
  local copies, waits for them, and re-layouts  0.8 us (1%)
    ppermute x8, waiting for transfers between devices, swap(): return lax.ppermute(block, axis, [(i, i ^ distance) for i in range(count)])  22.7 us
    ppermute x8, starting transfers between devices, swap(): return lax.ppermute(block, axis, [(i, i ^ distance) for i in range(count)])  8.56 us
    pallas_call x1, Pallas kernels, correlate(): pl.pallas_call(functools.partial(correlate_body, group=group, piece=PIECE...  7.17 us
    pallas_call x2, Pallas kernels, whiten(): pl.pallas_call(functools.partial(whiten_body, offsets=offsets, rows=rows)...  5.48 us
    all_to_all x1, starting transfers between devices, local(): lax.all_to_all(records.reshape(devices, stations, width), axis, split_axi...  5.26 us
    pallas_call x1, Pallas kernels, fetch(): pl.pallas_call(fetch_body, out_shape=jax.ShapeDtypeStruct(matrix.shape, m...  1.6 us
    pallas_call x1, Pallas kernels, pick(): pl.pallas_call(pick_body, out_shape=jax.ShapeDtypeStruct((steps, stations...  1.43 us
  transfers between devices with their start and end apart: 9, of which 4 were waited for; matrix products, arithmetic and copies ran while one was open for 1% of the time, Pallas kernels for 14%

profile of v8, /device:TPU:0, one launch (start us, length us, event | category | flops | bytes accessed | tf_op | source)
XLA Modules:
  0.0 53.5 jit_solution(14649506597137866600)
XLA Ops:
  0.0 0.7 %copy-done = s32[2]{0:T(128)S(1)} copy-done((s32[2]{0:T(128)S(1)}, s32[2]{0:T(128)}, u32[]{:S(2)}) %copy-start) | copy-done | bytes 32
  0.7 1.4 %shard_map.76 = bf16[2,32,1024]{2,1,0:T(8,128)(2,1)S(1)} custom-call(s32[2]{0:T(128)S(1)} %copy-done, bf16[512,1024]{1,0:T(8,128)(2,1)} %records_ref.1), custom_call_target="tpu_custom_call" | custom-call | tf_op jit(solution)/shard_map/pallas_call | solution.py:48
  2.1 3.1 %collective-permute-start = (bf16[1,2,32,1024]{3,2,1,0:T(8,128)(2,1)S(1)}, bf16[1,2,32,1024]{3,2,1,0:T(8,128)(2,1)S(1)}, u32[]{:S(2)}, u32[]{:S(2)}) collective-permute-start(bf16[1,2,32,1024]{3,2,1,0:T(8,128)(2,1)S(1)} %bitcast.13), channel_id=1, source_target_pairs={{0,4},{1,5},{2,6},{3,7},{4,0},{5,1},{6,2},{7,3},{8,12},{9,13},{10,... | collective-permute-start | bytes 393224 | tf_op jit(solution)/shard_map/ppermute | solution.py:286
  5.2 2.5 %collective-permute-start.4 = (bf16[1,2,32,1024]{3,2,1,0:T(8,128)(2,1)S(1)}, bf16[1,2,32,1024]{3,2,1,0:T(8,128)(2,1)S(1)}, u32[]{:S(2)}, u32[]{:S(2)}) collective-permute-start(bf16[1,2,32,1024]{3,2,1,0:T(8,128)(2,1)S(1)} %bitcast.14), channel_id=1, source_target_pairs={{0,12},{1,13},{2,14},{3,15},{4,8},{5,9},{6,10},{7,11},{8,4},{9,5},... | collective-permute-start | bytes 393224 | tf_op jit(solution)/shard_map/ppermute | solution.py:286
  7.7 0.1 collective-permute-start.3
  7.8 5.3 %all-to-all-start = ((bf16[16,32,1024]{2,1,0:T(8,128)(2,1)}), bf16[16,32,1024]{2,1,0:T(8,128)(2,1)S(1)}, u32[]{:S(2)}, u32[]{:S(2)}) async-start(bf16[16,32,1024]{2,1,0:T(8,128)(2,1)} %bitcast.19), calls=%async_computation | async-start | bytes 2097152 | tf_op jit(solution)/shard_map/all_to_all | solution.py:318
  13.1 0.0 collective-permute-done
  13.1 2.0 %collective-permute-start.1 = (bf16[2,2,32,1024]{3,2,1,0:T(8,128)(2,1)S(1)}, bf16[2,2,32,1024]{3,2,1,0:T(8,128)(2,1)S(1)}, u32[]{:S(2)}, u32[]{:S(2)}) collective-permute-start(bf16[2,2,32,1024]{3,2,1,0:T(8,128)(2,1)S(1)} %pad_maximum_fusion.1), channel_id=1, source_target_pairs={{0,2},{1,3},{2,0},{3,1},{4,6},{5,7},{6,4},{7,5},{8,10},{9,11},{10,... | collective-permute-start | bytes 786440 | tf_op jit(solution)/shard_map/ppermute | solution.py:286
  15.1 0.0 collective-permute-done.4
  15.1 11.1 %collective-permute-done.3 = bf16[1,2,32,1024]{3,2,1,0:T(8,128)(2,1)S(1)} collective-permute-done((bf16[1,2,32,1024]{3,2,1,0:T(8,128)(2,1)S(1)}, bf16[1,2,32,1024]{3,2,1,0:T(8,128)(2,1)S(1)}, u32[]{:S(2)}, u32[]{:S(2)}) %collective-permute-start.3) | collective-permute-done | bytes 131104 | tf_op jit(solution)/shard_map/ppermute | solution.py:286
  26.3 0.0 copy-start.4
  26.3 0.2 collective-permute-start.5
  26.6 3.8 %collective-permute-done.1 = bf16[2,2,32,1024]{3,2,1,0:T(8,128)(2,1)S(1)} collective-permute-done((bf16[2,2,32,1024]{3,2,1,0:T(8,128)(2,1)S(1)}, bf16[2,2,32,1024]{3,2,1,0:T(8,128)(2,1)S(1)}, u32[]{:S(2)}, u32[]{:S(2)}) %collective-permute-start.1) | collective-permute-done | bytes 262176 | tf_op jit(solution)/shard_map/ppermute | solution.py:286
  30.3 0.1 pad_maximum_fusion
  30.4 0.1 collective-permute-start.2
  30.5 7.4 %collective-permute-done.5 = bf16[2,2,32,1024]{3,2,1,0:T(8,128)(2,1)S(1)} collective-permute-done((bf16[2,2,32,1024]{3,2,1,0:T(8,128)(2,1)S(1)}, bf16[2,2,32,1024]{3,2,1,0:T(8,128)(2,1)S(1)}, u32[]{:S(2)}, u32[]{:S(2)}) %collective-permute-start.5) | collective-permute-done | bytes 262176 | tf_op jit(solution)/shard_map/ppermute | solution.py:286
  38.0 0.1 collective-permute-start.6
  38.1 0.0 copy-done.4
  38.1 0.1 pad_convert_fusion
  38.2 0.2 shard_map.73.rest_1_.rest_4_
  38.4 1.6 %shard_map.74.rest_2_.rest_5_ = bf16[1024,1024]{1,0:T(8,128)(2,1)S(1)} custom-call(bf16[1024,1024]{1,0:T(8,128)(2,1)} %constant.33.clone.source_ref), custom_call_target="tpu_custom_call" | custom-call | tf_op jit(solution)/shard_map/pallas_call | solution.py:84
  40.0 0.0 collective-permute-done.2.rest_1_
  40.0 0.0 collective-permute-done.6.rest_3_
  40.0 3.2 %shard_map.77.first_ref = bf16[16,32,1024]{2,1,0:T(8,128)(2,1)} custom-call(s32[1]{0:T(128)} %bitcast.3.index_ref, bf16[4,32,1024]{2,1,0:T(8,128)(2,1)S(1)} %get-tuple-element.8.rest_0_, bf16[4,32,1024]{2,1,0:T(8,128)(2,1)S(1)} %collective-permute-done.2.rest_1_, bf16[4,32,1024]{2,1,0:T(8,128)(2,1)S(1)} %get-tuple-element.6.rest_2_, ...), custom_call_target="tpu_custom_call" | custom-call | flops 1610612736 | bytes 2097152 | tf_op jit(solution)/shard_map/pallas_call | solution.py:134
  43.2 0.5 collective-permute-start.7
  43.7 0.0 all-to-all-done.rest_0_
  43.7 2.3 %shard_map.75.own_ref = bf16[16,32,1024]{2,1,0:T(8,128)(2,1)S(1)} custom-call(s32[1]{0:T(128)} %constant.29.clone.1.index_ref, bf16[16,32,1024]{2,1,0:T(8,128)(2,1)S(1)} %all-to-all-done.rest_0_, bf16[512,256]{1,0:T(8,128)(2,1)S(1)} %shard_map.73.rest_1_.rest_4_, bf16[1024,1024]{1,0:T(8,128)(2,1)S(1)} %shard_map.74.rest_2_.rest_5_), custom_call_target="tpu_custom_call" | custom-call | flops 1610612736 | bytes 2097152 | tf_op jit(solution)/shard_map/pallas_call | solution.py:134
  46.0 0.4 collective-permute-done.7.second_ref
  46.3 0.0 copy-done.1
  46.3 0.0 copy-done.2
  46.3 0.0 copy-done.3
  46.4 7.2 %shard_map.78 = f32[2,32,32,256]{3,2,1,0:T(8,128)} custom-call(s32[1]{0:T(128)} %bitcast.mine_ref, s32[2,32]{1,0:T(2,128)S(1)} %copy-done.2, s32[2,32,32]{2,1,0:T(8,128)S(1)} %copy-done.1, bf16[16,32,1024]{2,1,0:T(8,128)(2,1)S(1)} %shard_map.75.own_ref, bf16[16,32,1024]{2,1,0:T(8,128)(2,1)} %shard_map.77.first_ref, ...), custom_call_target="tpu_custom_call" | custom-call | flops 10000000000 | bytes 5242880 | tf_op jit(solution)/shard_map/pallas_call | solution.py:263
  (11 shorter events, 0.2 us)
Async XLA Ops:
  0.0 0.7 %copy-start = (s32[2]{0:T(128)S(1)}, s32[2]{0:T(128)}, u32[]{:S(2)}) copy-start(s32[2]{0:T(128)} %owner_ref.1) | copy-start | bytes 28
  2.1 11.0 %collective-permute-start = (bf16[1,2,32,1024]{3,2,1,0:T(8,128)(2,1)S(1)}, bf16[1,2,32,1024]{3,2,1,0:T(8,128)(2,1)S(1)}, u32[]{:S(2)}, u32[]{:S(2)}) collective-permute-start(bf16[1,2,32,1024]{3,2,1,0:T(8,128)(2,1)S(1)} %bitcast.13), channel_id=1, source_target_pairs={{0,4},{1,5},{2,6},{3,7},{4,0},{5,1},{6,2},{7,3},{8,12},{9,13},{10,... | collective-permute-start | bytes 393224 | tf_op jit(solution)/shard_map/ppermute | solution.py:286
  5.2 9.9 %collective-permute-start.4 = (bf16[1,2,32,1024]{3,2,1,0:T(8,128)(2,1)S(1)}, bf16[1,2,32,1024]{3,2,1,0:T(8,128)(2,1)S(1)}, u32[]{:S(2)}, u32[]{:S(2)}) collective-permute-start(bf16[1,2,32,1024]{3,2,1,0:T(8,128)(2,1)S(1)} %bitcast.14), channel_id=1, source_target_pairs={{0,12},{1,13},{2,14},{3,15},{4,8},{5,9},{6,10},{7,11},{8,4},{9,5},... | collective-permute-start | bytes 393224 | tf_op jit(solution)/shard_map/ppermute | solution.py:286
  7.7 18.6 %collective-permute-start.3 = (bf16[1,2,32,1024]{3,2,1,0:T(8,128)(2,1)S(1)}, bf16[1,2,32,1024]{3,2,1,0:T(8,128)(2,1)S(1)}, u32[]{:S(2)}, u32[]{:S(2)}) collective-permute-start(bf16[1,2,32,1024]{3,2,1,0:T(8,128)(2,1)S(1)} %bitcast.15), channel_id=1, source_target_pairs={{0,8},{1,9},{2,10},{3,11},{4,12},{5,13},{6,14},{7,15},{8,0},{9,1},... | collective-permute-start | bytes 393224 | tf_op jit(solution)/shard_map/ppermute | solution.py:286
  7.8 35.9 %all-to-all-start = ((bf16[16,32,1024]{2,1,0:T(8,128)(2,1)}), bf16[16,32,1024]{2,1,0:T(8,128)(2,1)S(1)}, u32[]{:S(2)}, u32[]{:S(2)}) async-start(bf16[16,32,1024]{2,1,0:T(8,128)(2,1)} %bitcast.19), calls=%async_computation | async-start | bytes 2097152 | tf_op jit(solution)/shard_map/all_to_all | solution.py:318
  13.1 17.2 %collective-permute-start.1 = (bf16[2,2,32,1024]{3,2,1,0:T(8,128)(2,1)S(1)}, bf16[2,2,32,1024]{3,2,1,0:T(8,128)(2,1)S(1)}, u32[]{:S(2)}, u32[]{:S(2)}) collective-permute-start(bf16[2,2,32,1024]{3,2,1,0:T(8,128)(2,1)S(1)} %pad_maximum_fusion.1), channel_id=1, source_target_pairs={{0,2},{1,3},{2,0},{3,1},{4,6},{5,7},{6,4},{7,5},{8,10},{9,11},{10,... | collective-permute-start | bytes 786440 | tf_op jit(solution)/shard_map/ppermute | solution.py:286
  26.3 11.8 %copy-start.4 = (bf16[129]{0:T(256)(128)(2,1)S(1)}, bf16[129]{0:T(256)(128)(2,1)}, u32[]{:S(2)}) copy-start(bf16[129]{0:T(256)(128)(2,1)} %param.8) | copy-start | bytes 778
  26.3 11.6 %collective-permute-start.5 = (bf16[2,2,32,1024]{3,2,1,0:T(8,128)(2,1)S(1)}, bf16[2,2,32,1024]{3,2,1,0:T(8,128)(2,1)S(1)}, u32[]{:S(2)}, u32[]{:S(2)}) collective-permute-start(bf16[2,2,32,1024]{3,2,1,0:T(8,128)(2,1)S(1)} %pad_maximum_fusion.2), channel_id=1, source_target_pairs={{0,2},{1,3},{2,0},{3,1},{4,6},{5,7},{6,4},{7,5},{8,10},{9,11},{10,... | collective-permute-start | bytes 786440 | tf_op jit(solution)/shard_map/ppermute | solution.py:286
  30.4 9.5 %collective-permute-start.2 = (bf16[4,32,1024]{2,1,0:T(8,128)(2,1)S(1)}, bf16[4,32,1024]{2,1,0:T(8,128)(2,1)S(1)}, u32[]{:S(2)}, u32[]{:S(2)}) collective-permute-start(bf16[4,32,1024]{2,1,0:T(8,128)(2,1)S(1)} %get-tuple-element.7), channel_id=1, source_target_pairs={{0,1},{1,0},{2,3},{3,2},{4,5},{5,4},{6,7},{7,6},{8,9},{9,8},{10,11... | collective-permute-start | bytes 786440 | tf_op jit(solution)/shard_map/ppermute | solution.py:286
  38.0 2.0 %collective-permute-start.6 = (bf16[4,32,1024]{2,1,0:T(8,128)(2,1)S(1)}, bf16[4,32,1024]{2,1,0:T(8,128)(2,1)S(1)}, u32[]{:S(2)}, u32[]{:S(2)}) collective-permute-start(bf16[4,32,1024]{2,1,0:T(8,128)(2,1)S(1)} %get-tuple-element.5), channel_id=1, source_target_pairs={{0,1},{1,0},{2,3},{3,2},{4,5},{5,4},{6,7},{7,6},{8,9},{9,8},{10,11... | collective-permute-start | bytes 786440 | tf_op jit(solution)/shard_map/ppermute | solution.py:286
  43.2 3.1 %copy-start.1 = (s32[2,32,32]{2,1,0:T(8,128)S(1)}, s32[2,32,32]{2,1,0:T(8,128)}, u32[]{:S(2)}) copy-start(s32[2,32,32]{2,1,0:T(8,128)} %valid_ref.1) | copy-start | bytes 24580
  43.2 3.1 %copy-start.2 = (s32[2,32]{1,0:T(2,128)S(1)}, s32[2,32]{1,0:T(2,128)}, u32[]{:S(2)}) copy-start(s32[2,32]{1,0:T(2,128)} %order_ref.1) | copy-start | bytes 772
  43.2 3.1 %collective-permute-start.7 = (bf16[16,32,1024]{2,1,0:T(8,128)(2,1)}, bf16[16,32,1024]{2,1,0:T(8,128)(2,1)}, u32[]{:S(2)}, u32[]{:S(2)}) collective-permute-start(bf16[16,32,1024]{2,1,0:T(8,128)(2,1)} %shard_map.77.first_ref), channel_id=1, source_target_pairs={{0,1},{1,0},{2,3},{3,2},{4,5},{5,4},{6,7},{7,6},{8,9},{9,8},{10,11... | collective-permute-start | bytes 3145736 | tf_op jit(solution)/shard_map/ppermute | solution.py:286
  43.7 2.6 %copy-start.3 = (bf16[1024,256]{1,0:T(8,128)(2,1)S(1)}, bf16[1024,256]{1,0:T(8,128)(2,1)}, u32[]{:S(2)}) copy-start(bf16[1024,256]{1,0:T(8,128)(2,1)} %constant.34.clone.inverse_ref) | copy-start | bytes 1572868

commit v9 on v8

--- a/solution.py
+++ b/solution.py
@@ -297,6 +297,7 @@
     own_piece = wanted[None]
     quarter = devices // 4
     crossed = [swap(own_piece, axis, j * quarter) for j in range(1, 4)]
+    own_passed = swap(own_piece, axis, quarter // 2)
     chains = {
         "near": (jnp.concatenate([own_piece, crossed[0]], axis=0), [0, quarter]),
         "far": (jnp.concatenate(crossed[1:], axis=0), [2 * quarter, 3 * quarter]),
@@ -304,7 +305,11 @@
     distance, stage = devices // 8, 0
     while distance > 1:
         for name, (block, offsets) in chains.items():
-            block = jnp.concatenate([block, swap(block, axis, distance)], axis=0)
+            if name == "near" and stage == 0:
+                passed = [own_passed, swap(crossed[0], axis, distance)]
+            else:
+                passed = [swap(block, axis, distance)]
+            block = jnp.concatenate([block, *passed], axis=0)
             chains[name] = block, offsets + [distance | o for o in offsets]
         distance //= 2
         stage += 1

time: 53.8 us -> 51.1 us (0.950)
  waiting for transfers between devices: 22.7 us -> 18.7 us
  starting transfers between devices: 13.8 us -> 15.2 us
    ppermute x8 -> x9, waiting for transfers between devices: 22.7 us -> 18.7 us  [swap(): return lax.ppermute(block, axis, [(i, i ^ distance) for i in range(count)])]
    ppermute x8 -> x9, starting transfers between devices: 8.56 us -> 10.2 us  [swap(): return lax.ppermute(block, axis, [(i, i ^ distance) for i in range(count)])]
  transfers between devices with their start and end apart: 9 -> 10, of which waited for: 4 -> 3; matrix products, arithmetic and copies ran while one was open for 1% -> 1% of each run, Pallas kernels for 14% -> 14%
where the time goes in v9:
time: 51.1 us; the launch traced here: 50.8 us
  waiting for transfers between devices  18.7 us (37%)
  Pallas kernels  15.9 us (31%)
  starting transfers between devices  15.2 us (30%)
  local copies, waits for them, and re-layouts  0.8 us (2%)
    ppermute x9, waiting for transfers between devices, swap(): return lax.ppermute(block, axis, [(i, i ^ distance) for i in range(count)])  18.7 us
    ppermute x9, starting transfers between devices, swap(): return lax.ppermute(block, axis, [(i, i ^ distance) for i in range(count)])  10.2 us
    pallas_call x1, Pallas kernels, correlate(): pl.pallas_call(functools.partial(correlate_body, group=group, piece=PIECE...  7.17 us
    pallas_call x2, Pallas kernels, whiten(): pl.pallas_call(functools.partial(whiten_body, offsets=offsets, rows=rows)...  5.48 us
    all_to_all x1, starting transfers between devices, local(): lax.all_to_all(records.reshape(devices, stations, width), axis, split_axi...  4.98 us
    pallas_call x1, Pallas kernels, fetch(): pl.pallas_call(fetch_body, out_shape=jax.ShapeDtypeStruct(matrix.shape, m...  1.6 us
    pallas_call x1, Pallas kernels, pick(): pl.pallas_call(pick_body, out_shape=jax.ShapeDtypeStruct((steps, stations...  1.43 us
  transfers between devices with their start and end apart: 10, of which 3 were waited for; matrix products, arithmetic and copies ran while one was open for 1% of the time, Pallas kernels for 14%

profile of v9, /device:TPU:0, one launch (start us, length us, event | category | flops | bytes accessed | tf_op | source)
XLA Modules:
  0.0 50.8 jit_solution(16648287421164891613)
XLA Ops:
  0.0 0.7 %copy-done = s32[2]{0:T(128)S(1)} copy-done((s32[2]{0:T(128)S(1)}, s32[2]{0:T(128)}, u32[]{:S(2)}) %copy-start) | copy-done | bytes 32
  0.7 1.4 %shard_map.76 = bf16[2,32,1024]{2,1,0:T(8,128)(2,1)S(1)} custom-call(s32[2]{0:T(128)S(1)} %copy-done, bf16[512,1024]{1,0:T(8,128)(2,1)} %records_ref.1), custom_call_target="tpu_custom_call" | custom-call | tf_op jit(solution)/shard_map/pallas_call | solution.py:48
  2.1 5.1 %collective-permute-start.5 = (bf16[1,2,32,1024]{3,2,1,0:T(8,128)(2,1)S(1)}, bf16[1,2,32,1024]{3,2,1,0:T(8,128)(2,1)S(1)}, u32[]{:S(2)}, u32[]{:S(2)}) collective-permute-start(bf16[1,2,32,1024]{3,2,1,0:T(8,128)(2,1)S(1)} %bitcast.13), channel_id=1, source_target_pairs={{0,12},{1,13},{2,14},{3,15},{4,8},{5,9},{6,10},{7,11},{8,4},{9,5},... | collective-permute-start | bytes 393224 | tf_op jit(solution)/shard_map/ppermute | solution.py:286
  7.2 0.0 collective-permute-start.4
  7.2 0.6 %collective-permute-start = (bf16[1,2,32,1024]{3,2,1,0:T(8,128)(2,1)S(1)}, bf16[1,2,32,1024]{3,2,1,0:T(8,128)(2,1)S(1)}, u32[]{:S(2)}, u32[]{:S(2)}) collective-permute-start(bf16[1,2,32,1024]{3,2,1,0:T(8,128)(2,1)S(1)} %bitcast.15), channel_id=1, source_target_pairs={{0,4},{1,5},{2,6},{3,7},{4,0},{5,1},{6,2},{7,3},{8,12},{9,13},{10,... | collective-permute-start | bytes 393224 | tf_op jit(solution)/shard_map/ppermute | solution.py:286
  7.9 1.7 %collective-permute-start.1 = (bf16[1,2,32,1024]{3,2,1,0:T(8,128)(2,1)S(1)}, bf16[1,2,32,1024]{3,2,1,0:T(8,128)(2,1)S(1)}, u32[]{:S(2)}, u32[]{:S(2)}) collective-permute-start(bf16[1,2,32,1024]{3,2,1,0:T(8,128)(2,1)S(1)} %bitcast.16), channel_id=1, source_target_pairs={{0,2},{1,3},{2,0},{3,1},{4,6},{5,7},{6,4},{7,5},{8,10},{9,11},{10,... | collective-permute-start | bytes 393224 | tf_op jit(solution)/shard_map/ppermute | solution.py:286
  9.5 5.0 %all-to-all-start = ((bf16[16,32,1024]{2,1,0:T(8,128)(2,1)}), bf16[16,32,1024]{2,1,0:T(8,128)(2,1)S(1)}, u32[]{:S(2)}, u32[]{:S(2)}) async-start(bf16[16,32,1024]{2,1,0:T(8,128)(2,1)} %bitcast.19), calls=%async_computation | async-start | bytes 2097152 | tf_op jit(solution)/shard_map/all_to_all | solution.py:323
  14.5 0.0 collective-permute-done.5
  14.6 3.8 %collective-permute-done.4 = bf16[1,2,32,1024]{3,2,1,0:T(8,128)(2,1)S(1)} collective-permute-done((bf16[1,2,32,1024]{3,2,1,0:T(8,128)(2,1)S(1)}, bf16[1,2,32,1024]{3,2,1,0:T(8,128)(2,1)S(1)}, u32[]{:S(2)}, u32[]{:S(2)}) %collective-permute-start.4) | collective-permute-done | bytes 131104 | tf_op jit(solution)/shard_map/ppermute | solution.py:286
  18.4 0.0 copy-start.4
  18.4 1.6 %collective-permute-start.6 = (bf16[2,2,32,1024]{3,2,1,0:T(8,128)(2,1)S(1)}, bf16[2,2,32,1024]{3,2,1,0:T(8,128)(2,1)S(1)}, u32[]{:S(2)}, u32[]{:S(2)}) collective-permute-start(bf16[2,2,32,1024]{3,2,1,0:T(8,128)(2,1)S(1)} %pad_maximum_fusion.1), channel_id=1, source_target_pairs={{0,2},{1,3},{2,0},{3,1},{4,6},{5,7},{6,4},{7,5},{8,10},{9,11},{10,... | collective-permute-start | bytes 786440 | tf_op jit(solution)/shard_map/ppermute | solution.py:286
  20.0 0.0 collective-permute-done
  20.0 0.5 collective-permute-start.2
  20.6 0.0 collective-permute-done.1
  20.6 14.1 %collective-permute-done.2 = bf16[1,2,32,1024]{3,2,1,0:T(8,128)(2,1)S(1)} collective-permute-done((bf16[1,2,32,1024]{3,2,1,0:T(8,128)(2,1)S(1)}, bf16[1,2,32,1024]{3,2,1,0:T(8,128)(2,1)S(1)}, u32[]{:S(2)}, u32[]{:S(2)}) %collective-permute-start.2) | collective-permute-done | bytes 131104 | tf_op jit(solution)/shard_map/ppermute | solution.py:286
  34.7 0.1 pad_maximum_fusion
  34.8 0.1 collective-permute-start.3
  34.9 0.0 collective-permute-done.6
  34.9 0.5 %collective-permute-start.7 = (bf16[4,32,1024]{2,1,0:T(8,128)(2,1)S(1)}, bf16[4,32,1024]{2,1,0:T(8,128)(2,1)S(1)}, u32[]{:S(2)}, u32[]{:S(2)}) collective-permute-start(bf16[4,32,1024]{2,1,0:T(8,128)(2,1)S(1)} %get-tuple-element.5), channel_id=1, source_target_pairs={{0,1},{1,0},{2,3},{3,2},{4,5},{5,4},{6,7},{7,6},{8,9},{9,8},{10,11... | collective-permute-start | bytes 786440 | tf_op jit(solution)/shard_map/ppermute | solution.py:286
  35.5 0.0 copy-done.4
  35.5 0.1 pad_convert_fusion
  35.6 0.2 shard_map.73.rest_1_.rest_4_
  35.8 1.6 %shard_map.74.rest_2_.rest_5_ = bf16[1024,1024]{1,0:T(8,128)(2,1)S(1)} custom-call(bf16[1024,1024]{1,0:T(8,128)(2,1)} %constant.33.clone.source_ref), custom_call_target="tpu_custom_call" | custom-call | tf_op jit(solution)/shard_map/pallas_call | solution.py:84
  37.4 0.0 collective-permute-done.3.rest_1_
  37.4 0.0 collective-permute-done.7.rest_3_
  37.4 3.2 %shard_map.77.first_ref = bf16[16,32,1024]{2,1,0:T(8,128)(2,1)} custom-call(s32[1]{0:T(128)} %bitcast.3.index_ref, bf16[4,32,1024]{2,1,0:T(8,128)(2,1)S(1)} %get-tuple-element.8.rest_0_, bf16[4,32,1024]{2,1,0:T(8,128)(2,1)S(1)} %collective-permute-done.3.rest_1_, bf16[4,32,1024]{2,1,0:T(8,128)(2,1)S(1)} %get-tuple-element.6.rest_2_, ...), custom_call_target="tpu_custom_call" | custom-call | flops 1610612736 | bytes 2097152 | tf_op jit(solution)/shard_map/pallas_call | solution.py:134
  40.6 0.0 collective-permute-start.8
  40.7 0.0 all-to-all-done.rest_0_
  40.7 2.2 %shard_map.75.own_ref = bf16[16,32,1024]{2,1,0:T(8,128)(2,1)S(1)} custom-call(s32[1]{0:T(128)} %constant.29.clone.1.index_ref, bf16[16,32,1024]{2,1,0:T(8,128)(2,1)S(1)} %all-to-all-done.rest_0_, bf16[512,256]{1,0:T(8,128)(2,1)S(1)} %shard_map.73.rest_1_.rest_4_, bf16[1024,1024]{1,0:T(8,128)(2,1)S(1)} %shard_map.74.rest_2_.rest_5_), custom_call_target="tpu_custom_call" | custom-call | flops 1610612736 | bytes 2097152 | tf_op jit(solution)/shard_map/pallas_call | solution.py:134
  42.9 0.7 %collective-permute-done.8.second_ref = bf16[16,32,1024]{2,1,0:T(8,128)(2,1)} collective-permute-done((bf16[16,32,1024]{2,1,0:T(8,128)(2,1)}, bf16[16,32,1024]{2,1,0:T(8,128)(2,1)}, u32[]{:S(2)}, u32[]{:S(2)}) %collective-permute-start.8) | collective-permute-done | bytes 1048608 | tf_op jit(solution)/shard_map/ppermute | solution.py:286
  43.6 0.0 copy-done.1
  43.6 7.2 %shard_map.78 = f32[2,32,32,256]{3,2,1,0:T(8,128)} custom-call(s32[1]{0:T(128)} %bitcast.mine_ref, s32[2,32]{1,0:T(2,128)S(1)} %copy-done.2, s32[2,32,32]{2,1,0:T(8,128)S(1)} %copy-done.1, bf16[16,32,1024]{2,1,0:T(8,128)(2,1)S(1)} %shard_map.75.own_ref, bf16[16,32,1024]{2,1,0:T(8,128)(2,1)} %shard_map.77.first_ref, ...), custom_call_target="tpu_custom_call" | custom-call | flops 10000000000 | bytes 5242880 | tf_op jit(solution)/shard_map/pallas_call | solution.py:263
  (12 shorter events, 0.2 us)
Async XLA Ops:
  0.0 0.7 %copy-start = (s32[2]{0:T(128)S(1)}, s32[2]{0:T(128)}, u32[]{:S(2)}) copy-start(s32[2]{0:T(128)} %owner_ref.1) | copy-start | bytes 28
  2.1 12.5 %collective-permute-start.5 = (bf16[1,2,32,1024]{3,2,1,0:T(8,128)(2,1)S(1)}, bf16[1,2,32,1024]{3,2,1,0:T(8,128)(2,1)S(1)}, u32[]{:S(2)}, u32[]{:S(2)}) collective-permute-start(bf16[1,2,32,1024]{3,2,1,0:T(8,128)(2,1)S(1)} %bitcast.13), channel_id=1, source_target_pairs={{0,12},{1,13},{2,14},{3,15},{4,8},{5,9},{6,10},{7,11},{8,4},{9,5},... | collective-permute-start | bytes 393224 | tf_op jit(solution)/shard_map/ppermute | solution.py:286
  7.2 11.1 %collective-permute-start.4 = (bf16[1,2,32,1024]{3,2,1,0:T(8,128)(2,1)S(1)}, bf16[1,2,32,1024]{3,2,1,0:T(8,128)(2,1)S(1)}, u32[]{:S(2)}, u32[]{:S(2)}) collective-permute-start(bf16[1,2,32,1024]{3,2,1,0:T(8,128)(2,1)S(1)} %bitcast.14), channel_id=1, source_target_pairs={{0,8},{1,9},{2,10},{3,11},{4,12},{5,13},{6,14},{7,15},{8,0},{9,1},... | collective-permute-start | bytes 393224 | tf_op jit(solution)/shard_map/ppermute | solution.py:286
  7.2 12.8 %collective-permute-start = (bf16[1,2,32,1024]{3,2,1,0:T(8,128)(2,1)S(1)}, bf16[1,2,32,1024]{3,2,1,0:T(8,128)(2,1)S(1)}, u32[]{:S(2)}, u32[]{:S(2)}) collective-permute-start(bf16[1,2,32,1024]{3,2,1,0:T(8,128)(2,1)S(1)} %bitcast.15), channel_id=1, source_target_pairs={{0,4},{1,5},{2,6},{3,7},{4,0},{5,1},{6,2},{7,3},{8,12},{9,13},{10,... | collective-permute-start | bytes 393224 | tf_op jit(solution)/shard_map/ppermute | solution.py:286
  7.9 12.7 %collective-permute-start.1 = (bf16[1,2,32,1024]{3,2,1,0:T(8,128)(2,1)S(1)}, bf16[1,2,32,1024]{3,2,1,0:T(8,128)(2,1)S(1)}, u32[]{:S(2)}, u32[]{:S(2)}) collective-permute-start(bf16[1,2,32,1024]{3,2,1,0:T(8,128)(2,1)S(1)} %bitcast.16), channel_id=1, source_target_pairs={{0,2},{1,3},{2,0},{3,1},{4,6},{5,7},{6,4},{7,5},{8,10},{9,11},{10,... | collective-permute-start | bytes 393224 | tf_op jit(solution)/shard_map/ppermute | solution.py:286
  9.5 31.1 %all-to-all-start = ((bf16[16,32,1024]{2,1,0:T(8,128)(2,1)}), bf16[16,32,1024]{2,1,0:T(8,128)(2,1)S(1)}, u32[]{:S(2)}, u32[]{:S(2)}) async-start(bf16[16,32,1024]{2,1,0:T(8,128)(2,1)} %bitcast.19), calls=%async_computation | async-start | bytes 2097152 | tf_op jit(solution)/shard_map/all_to_all | solution.py:323
  18.4 17.1 %copy-start.4 = (bf16[129]{0:T(256)(128)(2,1)S(1)}, bf16[129]{0:T(256)(128)(2,1)}, u32[]{:S(2)}) copy-start(bf16[129]{0:T(256)(128)(2,1)} %param.8) | copy-start | bytes 778
  18.4 16.4 %collective-permute-start.6 = (bf16[2,2,32,1024]{3,2,1,0:T(8,128)(2,1)S(1)}, bf16[2,2,32,1024]{3,2,1,0:T(8,128)(2,1)S(1)}, u32[]{:S(2)}, u32[]{:S(2)}) collective-permute-start(bf16[2,2,32,1024]{3,2,1,0:T(8,128)(2,1)S(1)} %pad_maximum_fusion.1), channel_id=1, source_target_pairs={{0,2},{1,3},{2,0},{3,1},{4,6},{5,7},{6,4},{7,5},{8,10},{9,11},{10,... | collective-permute-start | bytes 786440 | tf_op jit(solution)/shard_map/ppermute | solution.py:286
  20.0 14.6 %collective-permute-start.2 = (bf16[1,2,32,1024]{3,2,1,0:T(8,128)(2,1)S(1)}, bf16[1,2,32,1024]{3,2,1,0:T(8,128)(2,1)S(1)}, u32[]{:S(2)}, u32[]{:S(2)}) collective-permute-start(bf16[1,2,32,1024]{3,2,1,0:T(8,128)(2,1)S(1)} %collective-permute-done), channel_id=1, source_target_pairs={{0,2},{1,3},{2,0},{3,1},{4,6},{5,7},{6,4},{7,5},{8,10},{9,11},{10,... | collective-permute-start | bytes 393224 | tf_op jit(solution)/shard_map/ppermute | solution.py:286
  34.8 2.6 %collective-permute-start.3 = (bf16[4,32,1024]{2,1,0:T(8,128)(2,1)S(1)}, bf16[4,32,1024]{2,1,0:T(8,128)(2,1)S(1)}, u32[]{:S(2)}, u32[]{:S(2)}) collective-permute-start(bf16[4,32,1024]{2,1,0:T(8,128)(2,1)S(1)} %get-tuple-element.7), channel_id=1, source_target_pairs={{0,1},{1,0},{2,3},{3,2},{4,5},{5,4},{6,7},{7,6},{8,9},{9,8},{10,11... | collective-permute-start | bytes 786440 | tf_op jit(solution)/shard_map/ppermute | solution.py:286
  34.9 2.4 %collective-permute-start.7 = (bf16[4,32,1024]{2,1,0:T(8,128)(2,1)S(1)}, bf16[4,32,1024]{2,1,0:T(8,128)(2,1)S(1)}, u32[]{:S(2)}, u32[]{:S(2)}) collective-permute-start(bf16[4,32,1024]{2,1,0:T(8,128)(2,1)S(1)} %get-tuple-element.5), channel_id=1, source_target_pairs={{0,1},{1,0},{2,3},{3,2},{4,5},{5,4},{6,7},{7,6},{8,9},{9,8},{10,11... | collective-permute-start | bytes 786440 | tf_op jit(solution)/shard_map/ppermute | solution.py:286
  40.6 3.0 %copy-start.1 = (s32[2,32,32]{2,1,0:T(8,128)S(1)}, s32[2,32,32]{2,1,0:T(8,128)}, u32[]{:S(2)}) copy-start(s32[2,32,32]{2,1,0:T(8,128)} %valid_ref.1) | copy-start | bytes 24580
  40.6 3.0 %copy-start.2 = (s32[2,32]{1,0:T(2,128)S(1)}, s32[2,32]{1,0:T(2,128)}, u32[]{:S(2)}) copy-start(s32[2,32]{1,0:T(2,128)} %order_ref.1) | copy-start | bytes 772
  40.6 3.0 %collective-permute-start.8 = (bf16[16,32,1024]{2,1,0:T(8,128)(2,1)}, bf16[16,32,1024]{2,1,0:T(8,128)(2,1)}, u32[]{:S(2)}, u32[]{:S(2)}) collective-permute-start(bf16[16,32,1024]{2,1,0:T(8,128)(2,1)} %shard_map.77.first_ref), channel_id=1, source_target_pairs={{0,1},{1,0},{2,3},{3,2},{4,5},{5,4},{6,7},{7,6},{8,9},{9,8},{10,11... | collective-permute-start | bytes 3145736 | tf_op jit(solution)/shard_map/ppermute | solution.py:286
  40.7 3.0 %copy-start.3 = (bf16[1024,256]{1,0:T(8,128)(2,1)S(1)}, bf16[1024,256]{1,0:T(8,128)(2,1)}, u32[]{:S(2)}) copy-start(bf16[1024,256]{1,0:T(8,128)(2,1)} %constant.34.clone.inverse_ref) | copy-start | bytes 1572868
